TPU v7x, 512 devices: a whole 4x8x8 slice. The times are simulated.
512 devices in a mesh: blk: 64 (over y, x, z_lo), rep: 8 (over z_hi, core).
Axes of the slice: x: 4, y: 8, z: 8 (z_hi: 4, z_lo: 2; z = z_hi * 2 + z_lo), core: 2. Of those that a mesh axis runs over, the one named last changes fastest.
Arguments:
- features: bfloat16 [65536, 256], P(('blk', 'rep')), may hold values from -6 to 6
- degrees: int32 [65536], P(('blk', 'rep')), may hold values from 4 to 64
- tile_values: bfloat16 [512, 16, 8, 128, 128], P(('blk', 'rep')), may hold values from 0 to 1
- tile_rows: int32 [512, 16, 8], P(('blk', 'rep')), may hold values from 0 to 7, as said below
- tile_counts: int32 [512, 16], P(('blk', 'rep')), may hold values from 1 to 8, as said below
- weight: bfloat16 [256, 256], replicated, may hold values from -0.375 to 0.375
- cotangent: bfloat16 [65536, 256], P(('blk', 'rep')), may hold values from -6 to 6
Outputs:
- activations: bfloat16 [65536, 256], P(('blk', 'rep'))
- grad_weight: float32 [256, 256], replicated
- grad_features: bfloat16 [65536, 256], P(('blk', 'rep'))
Inputs may be any that keep to these rules, and one draw needn't show every extreme that they name: `tile_rows`: the 8 slots of one owner and distance name the 8 row blocks of its slab, each once. Only the first tile_counts[o, s] slots of owner o and distance s are live. In every draw some slab has all 8 slots live at every distance for every owner in it.
All inputs are finite; a program needn't handle non-finite values.
Results may differ from a plain program's by a relative error of at most 0.0077.
Values may be sent and summed in bfloat16 or wider, within the bound.
No kernel may reach another device: no remote copies, remote signals or barrier semaphores. Data moves between devices by JAX's collectives and lax.ppermute only.
A program may use at most 64 MiB of HBM per device.

v0:
```python
import math

import jax
import jax.numpy as jnp
from jax import lax
from jax.sharding import PartitionSpec as P


def passed_along(block, axis, distance):
    devices = range(lax.axis_size(axis))
    route = [((i - distance) % len(devices), i) for i in devices]
    return lax.ppermute(block, axis, route)


def per_device(features, degrees, tile_values, tile_rows, tile_counts, weight, cotangent):
    own_rows = features.shape[0]
    feature_width = features.shape[1]
    span_count = tile_values.shape[1]
    slot_count = tile_values.shape[2]
    block_size = tile_values.shape[3]
    inv_root = lax.rsqrt(degrees.astype(jnp.float32))[:, None]
    scaled = (features.astype(jnp.float32) * inv_root).astype(jnp.bfloat16)
    tile_stack = tile_values[0]
    row_stack = tile_rows[0]
    count_stack = tile_counts[0]
    slot_ids = jnp.arange(slot_count, dtype=jnp.int32)

    def load_distance(distance):
        tile_block = lax.dynamic_index_in_dim(tile_stack, distance, 0, keepdims=False)
        row_ids = lax.dynamic_index_in_dim(row_stack, distance, 0, keepdims=False)
        live_count = lax.dynamic_index_in_dim(count_stack, distance, 0, keepdims=False)
        return (tile_block, row_ids, live_count)

    def gather_rows(partial_sum, distance, source_rows):
        tile_block, row_ids, live_count = load_distance(distance)
        match_table = row_ids[None, :] == slot_ids[:, None]
        slot_of_row = jnp.sum(jnp.where(match_table, slot_ids[None, :], 0), axis=1)
        arranged = jnp.take(tile_block, slot_of_row, axis=0)
        row_live = slot_of_row < live_count
        product = jnp.einsum(
            "mij,jf->mif", arranged, source_rows, preferred_element_type=jnp.float32
        )
        return partial_sum + jnp.where(row_live[:, None, None], product, 0.0)

    def forward_turn(distance, carry):
        partial_sum, source_rows = carry
        partial_sum = gather_rows(partial_sum, distance, source_rows)
        source_rows = passed_along(source_rows, "blk", 1)
        return (partial_sum, source_rows)

    start_total = jnp.zeros((slot_count, block_size, feature_width), jnp.float32)
    partial_sum, source_rows = lax.fori_loop(0, span_count - 1, forward_turn, (start_total, scaled))
    partial_sum = gather_rows(partial_sum, span_count - 1, source_rows)
    slab_partial = partial_sum.reshape(slot_count * block_size, feature_width)
    own_sum = lax.psum_scatter(slab_partial, "rep", scatter_dimension=0, tiled=True)
    aggregated = (own_sum * inv_root).astype(jnp.bfloat16)
    pre_act = jnp.dot(aggregated, weight, preferred_element_type=jnp.float32)
    sigma = jax.nn.sigmoid(pre_act)
    activations = (pre_act * sigma).astype(jnp.bfloat16)
    act_grad = (cotangent.astype(jnp.float32) * sigma * (1.0 + pre_act * (1.0 - sigma))).astype(
        jnp.bfloat16
    )
    local_weight = lax.dot_general(
        aggregated, act_grad, (((0,), (0,)), ((), ())), preferred_element_type=jnp.float32
    )
    node_total = own_rows * lax.axis_size("blk") * lax.axis_size("rep")
    grad_weight = lax.psum(local_weight, ("blk", "rep")) / math.sqrt(node_total)
    back_grad = lax.dot_general(
        act_grad, weight, (((1,), (1,)), ((), ())), preferred_element_type=jnp.float32
    )
    back_scaled = (back_grad * inv_root).astype(jnp.bfloat16)
    slab_grads = lax.all_gather(back_scaled, "rep", axis=0, tiled=True).reshape(
        slot_count, block_size, feature_width
    )

    def scatter_rows(back_sum, distance):
        tile_block, row_ids, live_count = load_distance(distance)
        picked = jnp.take(slab_grads, row_ids, axis=0)
        picked = jnp.where((slot_ids < live_count)[:, None, None], picked, jnp.zeros_like(picked))
        return back_sum + jnp.einsum(
            "kij,kif->jf", tile_block, picked, preferred_element_type=jnp.float32
        )

    def backward_turn(turn_index, back_sum):
        back_sum = scatter_rows(back_sum, span_count - 1 - turn_index)
        return passed_along(back_sum, "blk", -1)

    zero_back = jnp.zeros((own_rows, feature_width), jnp.float32)
    back_total = lax.fori_loop(0, span_count - 1, backward_turn, zero_back)
    back_total = scatter_rows(back_total, 0)
    grad_features = (back_total * inv_root).astype(jnp.bfloat16)
    return (activations, grad_weight, grad_features)


def solution(mesh):
    placed = (
        P(("blk", "rep"), None),
        P(("blk", "rep")),
        P(("blk", "rep"), None, None, None, None),
        P(("blk", "rep"), None, None),
        P(("blk", "rep"), None),
        P(),
        P(("blk", "rep"), None),
    )
    return jax.shard_map(
        per_device,
        mesh=mesh,
        in_specs=placed,
        out_specs=(P(("blk", "rep"), None), P(), P(("blk", "rep"), None)),
        check_vma=False,
    )
```

profile of v0, /device:TPU:1, one launch (start us, length us, event | category | flops | bytes accessed | tf_op | source)
XLA Modules:
  0.0 516.0 jit_solution(8821793906793815661)
XLA Ops:
  14.3 142.4 %while.34 = (s32[]{:T(128)}, f32[8,128,256]{2,1,0:T(8,128)S(1)}, bf16[128,256]{1,0:T(8,128)(2,1)S(1)}, s32[16,8]{1,0:T(8,128)S(1)}, s32[16]{0:T(128)}, /*index=5...) while((s32[]{:T(128)}, f32[8,128,256]{2,1,0:T(8,128)S(1)}, ...), condition=%wide.region_2.4_spmd.clone.clone, body=%wide.region_0.3_spmd.clone.clone.sunk | while | flops 68027656 | bytes 3871199 | solution.py:52
  14.3 4.8 collective-permute-start.1
  23.4 2.4 collective-permute-done.1
  32.1 3.0 collective-permute-done.1
  41.3 3.0 collective-permute-done.1
  50.5 3.0 collective-permute-done.1
  59.8 3.0 collective-permute-done.1
  69.0 3.7 collective-permute-done.1
  78.9 3.0 collective-permute-done.1
  88.1 3.0 collective-permute-done.1
  97.3 3.0 collective-permute-done.1
  106.5 3.0 collective-permute-done.1
  115.8 3.0 collective-permute-done.1
  125.0 3.0 collective-permute-done.1
  134.2 3.0 collective-permute-done.1
  143.4 3.0 collective-permute-done.1
  152.6 4.0 collective-permute-done.1
  158.7 58.0 %reduce-scatter.2.cloned.1.call-done = f32[128,256]{1,0:T(8,128)} async-done(((f32[1024,256]{1,0:T(8,128)}), f32[128,256]{1,0:T(8,128)}) %reduce-scatter.2.cloned.1.call-update) | async-done | bytes 131088 | tf_op jit(solution)/shard_map/reduce_scatter | solution.py:55
  218.7 16.9 %all_gather.3 = bf16[1024,256]{1,0:T(8,128)(2,1)S(1)} all-gather(bf16[128,256]{1,0:T(8,128)(2,1)S(1)} %fusion.25), channel_id=1, replica_groups=mesh['blk'=64,'rep'=8] {'rep'}, dimensions={0}, use_global_device_ids=true | all-gather | bytes 589824 | tf_op jit(solution)/shard_map/all_gather | solution.py:72
  238.1 200.0 %while.33 = (s32[]{:T(128)}, f32[128,256]{1,0:T(8,128)S(1)}, bf16[16,8,128,128]{3,2,1,0:T(8,128)(2,1)}, s32[16]{0:T(128)S(1)}, s32[16,8]{1,0:T(8,128)S(1)}, /*in...) while((s32[]{:T(128)}, f32[128,256]{1,0:T(8,128)S(1)}, ...), condition=%wide.region_7.10_spmd.clone, body=%wide.region_6.9_spmd.clone.sunk | while | flops 67667008 | bytes 2625907 | solution.py:89
  241.4 6.4 %collective-permute-start = (f32[128,256]{1,0:T(8,128)S(1)}, f32[128,256]{1,0:T(8,128)S(1)}, u32[]{:S(2)}, u32[]{:S(2)}) collective-permute-start(f32[128,256]{1,0:T(8,128)S(1)} %fusion.53), channel_id=1, source_target_pairs={{8,0},{16,8},{24,16},{32,24},{40,32},{48,40},{56,48},{64,56},{72,6... | collective-permute-start | bytes 393224 | tf_op jit(solution)/shard_map/while/body/eval_jaxpr/ppermute | solution.py:12
  247.8 2.7 collective-permute-done
  253.7 8.3 %collective-permute-start = (f32[128,256]{1,0:T(8,128)S(1)}, f32[128,256]{1,0:T(8,128)S(1)}, u32[]{:S(2)}, u32[]{:S(2)}) collective-permute-start(f32[128,256]{1,0:T(8,128)S(1)} %fusion.53), channel_id=1, source_target_pairs={{8,0},{16,8},{24,16},{32,24},{40,32},{48,40},{56,48},{64,56},{72,6... | collective-permute-start | bytes 393224 | tf_op jit(solution)/shard_map/while/body/eval_jaxpr/ppermute | solution.py:12
  262.1 1.9 collective-permute-done
  267.2 8.0 %collective-permute-start = (f32[128,256]{1,0:T(8,128)S(1)}, f32[128,256]{1,0:T(8,128)S(1)}, u32[]{:S(2)}, u32[]{:S(2)}) collective-permute-start(f32[128,256]{1,0:T(8,128)S(1)} %fusion.53), channel_id=1, source_target_pairs={{8,0},{16,8},{24,16},{32,24},{40,32},{48,40},{56,48},{64,56},{72,6... | collective-permute-start | bytes 393224 | tf_op jit(solution)/shard_map/while/body/eval_jaxpr/ppermute | solution.py:12
  275.3 1.9 collective-permute-done
  280.5 8.0 %collective-permute-start = (f32[128,256]{1,0:T(8,128)S(1)}, f32[128,256]{1,0:T(8,128)S(1)}, u32[]{:S(2)}, u32[]{:S(2)}) collective-permute-start(f32[128,256]{1,0:T(8,128)S(1)} %fusion.53), channel_id=1, source_target_pairs={{8,0},{16,8},{24,16},{32,24},{40,32},{48,40},{56,48},{64,56},{72,6... | collective-permute-start | bytes 393224 | tf_op jit(solution)/shard_map/while/body/eval_jaxpr/ppermute | solution.py:12
  288.5 1.9 collective-permute-done
  293.7 8.0 %collective-permute-start = (f32[128,256]{1,0:T(8,128)S(1)}, f32[128,256]{1,0:T(8,128)S(1)}, u32[]{:S(2)}, u32[]{:S(2)}) collective-permute-start(f32[128,256]{1,0:T(8,128)S(1)} %fusion.53), channel_id=1, source_target_pairs={{8,0},{16,8},{24,16},{32,24},{40,32},{48,40},{56,48},{64,56},{72,6... | collective-permute-start | bytes 393224 | tf_op jit(solution)/shard_map/while/body/eval_jaxpr/ppermute | solution.py:12
  301.7 1.9 collective-permute-done
  306.9 8.0 %collective-permute-start = (f32[128,256]{1,0:T(8,128)S(1)}, f32[128,256]{1,0:T(8,128)S(1)}, u32[]{:S(2)}, u32[]{:S(2)}) collective-permute-start(f32[128,256]{1,0:T(8,128)S(1)} %fusion.53), channel_id=1, source_target_pairs={{8,0},{16,8},{24,16},{32,24},{40,32},{48,40},{56,48},{64,56},{72,6... | collective-permute-start | bytes 393224 | tf_op jit(solution)/shard_map/while/body/eval_jaxpr/ppermute | solution.py:12
  314.9 1.9 collective-permute-done
  320.1 8.0 %collective-permute-start = (f32[128,256]{1,0:T(8,128)S(1)}, f32[128,256]{1,0:T(8,128)S(1)}, u32[]{:S(2)}, u32[]{:S(2)}) collective-permute-start(f32[128,256]{1,0:T(8,128)S(1)} %fusion.53), channel_id=1, source_target_pairs={{8,0},{16,8},{24,16},{32,24},{40,32},{48,40},{56,48},{64,56},{72,6... | collective-permute-start | bytes 393224 | tf_op jit(solution)/shard_map/while/body/eval_jaxpr/ppermute | solution.py:12
  328.1 1.9 collective-permute-done
  333.3 8.0 %collective-permute-start = (f32[128,256]{1,0:T(8,128)S(1)}, f32[128,256]{1,0:T(8,128)S(1)}, u32[]{:S(2)}, u32[]{:S(2)}) collective-permute-start(f32[128,256]{1,0:T(8,128)S(1)} %fusion.53), channel_id=1, source_target_pairs={{8,0},{16,8},{24,16},{32,24},{40,32},{48,40},{56,48},{64,56},{72,6... | collective-permute-start | bytes 393224 | tf_op jit(solution)/shard_map/while/body/eval_jaxpr/ppermute | solution.py:12
  341.4 1.9 collective-permute-done
  346.6 8.0 %collective-permute-start = (f32[128,256]{1,0:T(8,128)S(1)}, f32[128,256]{1,0:T(8,128)S(1)}, u32[]{:S(2)}, u32[]{:S(2)}) collective-permute-start(f32[128,256]{1,0:T(8,128)S(1)} %fusion.53), channel_id=1, source_target_pairs={{8,0},{16,8},{24,16},{32,24},{40,32},{48,40},{56,48},{64,56},{72,6... | collective-permute-start | bytes 393224 | tf_op jit(solution)/shard_map/while/body/eval_jaxpr/ppermute | solution.py:12
  359.8 8.0 %collective-permute-start = (f32[128,256]{1,0:T(8,128)S(1)}, f32[128,256]{1,0:T(8,128)S(1)}, u32[]{:S(2)}, u32[]{:S(2)}) collective-permute-start(f32[128,256]{1,0:T(8,128)S(1)} %fusion.53), channel_id=1, source_target_pairs={{8,0},{16,8},{24,16},{32,24},{40,32},{48,40},{56,48},{64,56},{72,6... | collective-permute-start | bytes 393224 | tf_op jit(solution)/shard_map/while/body/eval_jaxpr/ppermute | solution.py:12
  367.8 1.9 collective-permute-done
  373.0 8.1 %collective-permute-start = (f32[128,256]{1,0:T(8,128)S(1)}, f32[128,256]{1,0:T(8,128)S(1)}, u32[]{:S(2)}, u32[]{:S(2)}) collective-permute-start(f32[128,256]{1,0:T(8,128)S(1)} %fusion.53), channel_id=1, source_target_pairs={{8,0},{16,8},{24,16},{32,24},{40,32},{48,40},{56,48},{64,56},{72,6... | collective-permute-start | bytes 393224 | tf_op jit(solution)/shard_map/while/body/eval_jaxpr/ppermute | solution.py:12
  386.2 8.0 %collective-permute-start = (f32[128,256]{1,0:T(8,128)S(1)}, f32[128,256]{1,0:T(8,128)S(1)}, u32[]{:S(2)}, u32[]{:S(2)}) collective-permute-start(f32[128,256]{1,0:T(8,128)S(1)} %fusion.53), channel_id=1, source_target_pairs={{8,0},{16,8},{24,16},{32,24},{40,32},{48,40},{56,48},{64,56},{72,6... | collective-permute-start | bytes 393224 | tf_op jit(solution)/shard_map/while/body/eval_jaxpr/ppermute | solution.py:12
  394.2 2.0 collective-permute-done
  399.5 8.0 %collective-permute-start = (f32[128,256]{1,0:T(8,128)S(1)}, f32[128,256]{1,0:T(8,128)S(1)}, u32[]{:S(2)}, u32[]{:S(2)}) collective-permute-start(f32[128,256]{1,0:T(8,128)S(1)} %fusion.53), channel_id=1, source_target_pairs={{8,0},{16,8},{24,16},{32,24},{40,32},{48,40},{56,48},{64,56},{72,6... | collective-permute-start | bytes 393224 | tf_op jit(solution)/shard_map/while/body/eval_jaxpr/ppermute | solution.py:12
  407.5 3.2 collective-permute-done
  414.0 8.1 %collective-permute-start = (f32[128,256]{1,0:T(8,128)S(1)}, f32[128,256]{1,0:T(8,128)S(1)}, u32[]{:S(2)}, u32[]{:S(2)}) collective-permute-start(f32[128,256]{1,0:T(8,128)S(1)} %fusion.53), channel_id=1, source_target_pairs={{8,0},{16,8},{24,16},{32,24},{40,32},{48,40},{56,48},{64,56},{72,6... | collective-permute-start | bytes 393224 | tf_op jit(solution)/shard_map/while/body/eval_jaxpr/ppermute | solution.py:12
  422.1 2.4 collective-permute-done
  427.8 8.3 %collective-permute-start = (f32[128,256]{1,0:T(8,128)S(1)}, f32[128,256]{1,0:T(8,128)S(1)}, u32[]{:S(2)}, u32[]{:S(2)}) collective-permute-start(f32[128,256]{1,0:T(8,128)S(1)} %fusion.53), channel_id=1, source_target_pairs={{8,0},{16,8},{24,16},{32,24},{40,32},{48,40},{56,48},{64,56},{72,6... | collective-permute-start | bytes 393224 | tf_op jit(solution)/shard_map/while/body/eval_jaxpr/ppermute | solution.py:12
  440.0 67.5 %all-reduce.2.cloned.1.call-done = f32[256,256]{1,0:T(8,128)} async-done(((f32[256,256]{1,0:T(8,128)}), f32[256,256]{1,0:T(8,128)}) %all-reduce.2.cloned.1.call-update) | async-done | bytes 262160 | tf_op jit(solution)/shard_map/psum | solution.py:67
  (275 shorter events, 161.9 us)
Async XLA Ops:
  7.2 209.5 %copy-start = (bf16[256,256]{1,0:T(8,128)(2,1)S(1)}, bf16[256,256]{1,0:T(8,128)(2,1)}, u32[]{:S(2)}) copy-start(bf16[256,256]{1,0:T(8,128)(2,1)} %param.20) | copy-start | bytes 393220
  7.2 209.5 %reduce-scatter.2.cloned.1.call-start = ((), (), s32[]{:S(2)}) async-start(), calls=%async_computation.1 | async-start | bytes 1179648 | tf_op jit(solution)/shard_map/reduce_scatter | solution.py:55
  14.3 202.4 %copy-start.2 = (bf16[128,256]{1,0:T(8,128)(2,1)S(1)}, bf16[128,256]{1,0:T(8,128)(2,1)}, u32[]{:S(2)}) copy-start(bf16[128,256]{1,0:T(8,128)(2,1)} %param.21) | copy-start | bytes 196612
  14.3 11.6 %collective-permute-start.1 = (bf16[128,256]{1,0:T(8,128)(2,1)S(1)}, bf16[128,256]{1,0:T(8,128)(2,1)S(1)}, u32[]{:S(2)}, u32[]{:S(2)}) collective-permute-start(bf16[128,256]{1,0:T(8,128)(2,1)S(1)} %copy.29), channel_id=1, source_target_pairs={{504,0},{0,8},{8,16},{16,24},{24,32},{32,40},{40,48},{48,56},{56,6... | collective-permute-start | bytes 196616 | tf_op jit(solution)/shard_map/while/body/eval_jaxpr/ppermute | solution.py:12
  25.9 9.2 %collective-permute-start.1 = (bf16[128,256]{1,0:T(8,128)(2,1)S(1)}, bf16[128,256]{1,0:T(8,128)(2,1)S(1)}, u32[]{:S(2)}, u32[]{:S(2)}) collective-permute-start(bf16[128,256]{1,0:T(8,128)(2,1)S(1)} %copy.29), channel_id=1, source_target_pairs={{504,0},{0,8},{8,16},{16,24},{24,32},{32,40},{40,48},{48,56},{56,6... | collective-permute-start | bytes 196616 | tf_op jit(solution)/shard_map/while/body/eval_jaxpr/ppermute | solution.py:12
  35.1 9.2 %collective-permute-start.1 = (bf16[128,256]{1,0:T(8,128)(2,1)S(1)}, bf16[128,256]{1,0:T(8,128)(2,1)S(1)}, u32[]{:S(2)}, u32[]{:S(2)}) collective-permute-start(bf16[128,256]{1,0:T(8,128)(2,1)S(1)} %copy.29), channel_id=1, source_target_pairs={{504,0},{0,8},{8,16},{16,24},{24,32},{32,40},{40,48},{48,56},{56,6... | collective-permute-start | bytes 196616 | tf_op jit(solution)/shard_map/while/body/eval_jaxpr/ppermute | solution.py:12
  44.3 9.2 %collective-permute-start.1 = (bf16[128,256]{1,0:T(8,128)(2,1)S(1)}, bf16[128,256]{1,0:T(8,128)(2,1)S(1)}, u32[]{:S(2)}, u32[]{:S(2)}) collective-permute-start(bf16[128,256]{1,0:T(8,128)(2,1)S(1)} %copy.29), channel_id=1, source_target_pairs={{504,0},{0,8},{8,16},{16,24},{24,32},{32,40},{40,48},{48,56},{56,6... | collective-permute-start | bytes 196616 | tf_op jit(solution)/shard_map/while/body/eval_jaxpr/ppermute | solution.py:12
  53.5 9.2 %collective-permute-start.1 = (bf16[128,256]{1,0:T(8,128)(2,1)S(1)}, bf16[128,256]{1,0:T(8,128)(2,1)S(1)}, u32[]{:S(2)}, u32[]{:S(2)}) collective-permute-start(bf16[128,256]{1,0:T(8,128)(2,1)S(1)} %copy.29), channel_id=1, source_target_pairs={{504,0},{0,8},{8,16},{16,24},{24,32},{32,40},{40,48},{48,56},{56,6... | collective-permute-start | bytes 196616 | tf_op jit(solution)/shard_map/while/body/eval_jaxpr/ppermute | solution.py:12
  62.8 9.9 %collective-permute-start.1 = (bf16[128,256]{1,0:T(8,128)(2,1)S(1)}, bf16[128,256]{1,0:T(8,128)(2,1)S(1)}, u32[]{:S(2)}, u32[]{:S(2)}) collective-permute-start(bf16[128,256]{1,0:T(8,128)(2,1)S(1)} %copy.29), channel_id=1, source_target_pairs={{504,0},{0,8},{8,16},{16,24},{24,32},{32,40},{40,48},{48,56},{56,6... | collective-permute-start | bytes 196616 | tf_op jit(solution)/shard_map/while/body/eval_jaxpr/ppermute | solution.py:12
  72.6 9.2 %collective-permute-start.1 = (bf16[128,256]{1,0:T(8,128)(2,1)S(1)}, bf16[128,256]{1,0:T(8,128)(2,1)S(1)}, u32[]{:S(2)}, u32[]{:S(2)}) collective-permute-start(bf16[128,256]{1,0:T(8,128)(2,1)S(1)} %copy.29), channel_id=1, source_target_pairs={{504,0},{0,8},{8,16},{16,24},{24,32},{32,40},{40,48},{48,56},{56,6... | collective-permute-start | bytes 196616 | tf_op jit(solution)/shard_map/while/body/eval_jaxpr/ppermute | solution.py:12
  81.9 9.2 %collective-permute-start.1 = (bf16[128,256]{1,0:T(8,128)(2,1)S(1)}, bf16[128,256]{1,0:T(8,128)(2,1)S(1)}, u32[]{:S(2)}, u32[]{:S(2)}) collective-permute-start(bf16[128,256]{1,0:T(8,128)(2,1)S(1)} %copy.29), channel_id=1, source_target_pairs={{504,0},{0,8},{8,16},{16,24},{24,32},{32,40},{40,48},{48,56},{56,6... | collective-permute-start | bytes 196616 | tf_op jit(solution)/shard_map/while/body/eval_jaxpr/ppermute | solution.py:12
  91.1 9.2 %collective-permute-start.1 = (bf16[128,256]{1,0:T(8,128)(2,1)S(1)}, bf16[128,256]{1,0:T(8,128)(2,1)S(1)}, u32[]{:S(2)}, u32[]{:S(2)}) collective-permute-start(bf16[128,256]{1,0:T(8,128)(2,1)S(1)} %copy.29), channel_id=1, source_target_pairs={{504,0},{0,8},{8,16},{16,24},{24,32},{32,40},{40,48},{48,56},{56,6... | collective-permute-start | bytes 196616 | tf_op jit(solution)/shard_map/while/body/eval_jaxpr/ppermute | solution.py:12
  100.3 9.2 %collective-permute-start.1 = (bf16[128,256]{1,0:T(8,128)(2,1)S(1)}, bf16[128,256]{1,0:T(8,128)(2,1)S(1)}, u32[]{:S(2)}, u32[]{:S(2)}) collective-permute-start(bf16[128,256]{1,0:T(8,128)(2,1)S(1)} %copy.29), channel_id=1, source_target_pairs={{504,0},{0,8},{8,16},{16,24},{24,32},{32,40},{40,48},{48,56},{56,6... | collective-permute-start | bytes 196616 | tf_op jit(solution)/shard_map/while/body/eval_jaxpr/ppermute | solution.py:12
  109.5 9.2 %collective-permute-start.1 = (bf16[128,256]{1,0:T(8,128)(2,1)S(1)}, bf16[128,256]{1,0:T(8,128)(2,1)S(1)}, u32[]{:S(2)}, u32[]{:S(2)}) collective-permute-start(bf16[128,256]{1,0:T(8,128)(2,1)S(1)} %copy.29), channel_id=1, source_target_pairs={{504,0},{0,8},{8,16},{16,24},{24,32},{32,40},{40,48},{48,56},{56,6... | collective-permute-start | bytes 196616 | tf_op jit(solution)/shard_map/while/body/eval_jaxpr/ppermute | solution.py:12
  118.8 9.2 %collective-permute-start.1 = (bf16[128,256]{1,0:T(8,128)(2,1)S(1)}, bf16[128,256]{1,0:T(8,128)(2,1)S(1)}, u32[]{:S(2)}, u32[]{:S(2)}) collective-permute-start(bf16[128,256]{1,0:T(8,128)(2,1)S(1)} %copy.29), channel_id=1, source_target_pairs={{504,0},{0,8},{8,16},{16,24},{24,32},{32,40},{40,48},{48,56},{56,6... | collective-permute-start | bytes 196616 | tf_op jit(solution)/shard_map/while/body/eval_jaxpr/ppermute | solution.py:12
  128.0 9.2 %collective-permute-start.1 = (bf16[128,256]{1,0:T(8,128)(2,1)S(1)}, bf16[128,256]{1,0:T(8,128)(2,1)S(1)}, u32[]{:S(2)}, u32[]{:S(2)}) collective-permute-start(bf16[128,256]{1,0:T(8,128)(2,1)S(1)} %copy.29), channel_id=1, source_target_pairs={{504,0},{0,8},{8,16},{16,24},{24,32},{32,40},{40,48},{48,56},{56,6... | collective-permute-start | bytes 196616 | tf_op jit(solution)/shard_map/while/body/eval_jaxpr/ppermute | solution.py:12
  137.2 9.2 %collective-permute-start.1 = (bf16[128,256]{1,0:T(8,128)(2,1)S(1)}, bf16[128,256]{1,0:T(8,128)(2,1)S(1)}, u32[]{:S(2)}, u32[]{:S(2)}) collective-permute-start(bf16[128,256]{1,0:T(8,128)(2,1)S(1)} %copy.29), channel_id=1, source_target_pairs={{504,0},{0,8},{8,16},{16,24},{24,32},{32,40},{40,48},{48,56},{56,6... | collective-permute-start | bytes 196616 | tf_op jit(solution)/shard_map/while/body/eval_jaxpr/ppermute | solution.py:12
  146.4 10.2 %collective-permute-start.1 = (bf16[128,256]{1,0:T(8,128)(2,1)S(1)}, bf16[128,256]{1,0:T(8,128)(2,1)S(1)}, u32[]{:S(2)}, u32[]{:S(2)}) collective-permute-start(bf16[128,256]{1,0:T(8,128)(2,1)S(1)} %copy.29), channel_id=1, source_target_pairs={{504,0},{0,8},{8,16},{16,24},{24,32},{32,40},{40,48},{48,56},{56,6... | collective-permute-start | bytes 196616 | tf_op jit(solution)/shard_map/while/body/eval_jaxpr/ppermute | solution.py:12
  156.6 81.5 %copy-start.1 = (s32[16]{0:T(128)S(1)}, s32[16]{0:T(128)}, u32[]{:S(2)}) copy-start(s32[16]{0:T(128)} %get-tuple-element.582) | copy-start | bytes 196
  158.0 349.5 %all-reduce.2.cloned.1.call-start = ((), (), s32[]{:S(2)}) async-start(), calls=%async_computation.2 | async-start | bytes 524288 | tf_op jit(solution)/shard_map/psum | solution.py:67
  241.4 9.0 %collective-permute-start = (f32[128,256]{1,0:T(8,128)S(1)}, f32[128,256]{1,0:T(8,128)S(1)}, u32[]{:S(2)}, u32[]{:S(2)}) collective-permute-start(f32[128,256]{1,0:T(8,128)S(1)} %fusion.53), channel_id=1, source_target_pairs={{8,0},{16,8},{24,16},{32,24},{40,32},{48,40},{56,48},{64,56},{72,6... | collective-permute-start | bytes 393224 | tf_op jit(solution)/shard_map/while/body/eval_jaxpr/ppermute | solution.py:12
  253.7 10.3 %collective-permute-start = (f32[128,256]{1,0:T(8,128)S(1)}, f32[128,256]{1,0:T(8,128)S(1)}, u32[]{:S(2)}, u32[]{:S(2)}) collective-permute-start(f32[128,256]{1,0:T(8,128)S(1)} %fusion.53), channel_id=1, source_target_pairs={{8,0},{16,8},{24,16},{32,24},{40,32},{48,40},{56,48},{64,56},{72,6... | collective-permute-start | bytes 393224 | tf_op jit(solution)/shard_map/while/body/eval_jaxpr/ppermute | solution.py:12
  267.2 10.0 %collective-permute-start = (f32[128,256]{1,0:T(8,128)S(1)}, f32[128,256]{1,0:T(8,128)S(1)}, u32[]{:S(2)}, u32[]{:S(2)}) collective-permute-start(f32[128,256]{1,0:T(8,128)S(1)} %fusion.53), channel_id=1, source_target_pairs={{8,0},{16,8},{24,16},{32,24},{40,32},{48,40},{56,48},{64,56},{72,6... | collective-permute-start | bytes 393224 | tf_op jit(solution)/shard_map/while/body/eval_jaxpr/ppermute | solution.py:12
  280.5 10.0 %collective-permute-start = (f32[128,256]{1,0:T(8,128)S(1)}, f32[128,256]{1,0:T(8,128)S(1)}, u32[]{:S(2)}, u32[]{:S(2)}) collective-permute-start(f32[128,256]{1,0:T(8,128)S(1)} %fusion.53), channel_id=1, source_target_pairs={{8,0},{16,8},{24,16},{32,24},{40,32},{48,40},{56,48},{64,56},{72,6... | collective-permute-start | bytes 393224 | tf_op jit(solution)/shard_map/while/body/eval_jaxpr/ppermute | solution.py:12
  293.7 10.0 %collective-permute-start = (f32[128,256]{1,0:T(8,128)S(1)}, f32[128,256]{1,0:T(8,128)S(1)}, u32[]{:S(2)}, u32[]{:S(2)}) collective-permute-start(f32[128,256]{1,0:T(8,128)S(1)} %fusion.53), channel_id=1, source_target_pairs={{8,0},{16,8},{24,16},{32,24},{40,32},{48,40},{56,48},{64,56},{72,6... | collective-permute-start | bytes 393224 | tf_op jit(solution)/shard_map/while/body/eval_jaxpr/ppermute | solution.py:12
  306.9 9.9 %collective-permute-start = (f32[128,256]{1,0:T(8,128)S(1)}, f32[128,256]{1,0:T(8,128)S(1)}, u32[]{:S(2)}, u32[]{:S(2)}) collective-permute-start(f32[128,256]{1,0:T(8,128)S(1)} %fusion.53), channel_id=1, source_target_pairs={{8,0},{16,8},{24,16},{32,24},{40,32},{48,40},{56,48},{64,56},{72,6... | collective-permute-start | bytes 393224 | tf_op jit(solution)/shard_map/while/body/eval_jaxpr/ppermute | solution.py:12
  320.1 10.0 %collective-permute-start = (f32[128,256]{1,0:T(8,128)S(1)}, f32[128,256]{1,0:T(8,128)S(1)}, u32[]{:S(2)}, u32[]{:S(2)}) collective-permute-start(f32[128,256]{1,0:T(8,128)S(1)} %fusion.53), channel_id=1, source_target_pairs={{8,0},{16,8},{24,16},{32,24},{40,32},{48,40},{56,48},{64,56},{72,6... | collective-permute-start | bytes 393224 | tf_op jit(solution)/shard_map/while/body/eval_jaxpr/ppermute | solution.py:12
  333.3 10.0 %collective-permute-start = (f32[128,256]{1,0:T(8,128)S(1)}, f32[128,256]{1,0:T(8,128)S(1)}, u32[]{:S(2)}, u32[]{:S(2)}) collective-permute-start(f32[128,256]{1,0:T(8,128)S(1)} %fusion.53), channel_id=1, source_target_pairs={{8,0},{16,8},{24,16},{32,24},{40,32},{48,40},{56,48},{64,56},{72,6... | collective-permute-start | bytes 393224 | tf_op jit(solution)/shard_map/while/body/eval_jaxpr/ppermute | solution.py:12
  346.6 9.9 %collective-permute-start = (f32[128,256]{1,0:T(8,128)S(1)}, f32[128,256]{1,0:T(8,128)S(1)}, u32[]{:S(2)}, u32[]{:S(2)}) collective-permute-start(f32[128,256]{1,0:T(8,128)S(1)} %fusion.53), channel_id=1, source_target_pairs={{8,0},{16,8},{24,16},{32,24},{40,32},{48,40},{56,48},{64,56},{72,6... | collective-permute-start | bytes 393224 | tf_op jit(solution)/shard_map/while/body/eval_jaxpr/ppermute | solution.py:12
  359.8 10.0 %collective-permute-start = (f32[128,256]{1,0:T(8,128)S(1)}, f32[128,256]{1,0:T(8,128)S(1)}, u32[]{:S(2)}, u32[]{:S(2)}) collective-permute-start(f32[128,256]{1,0:T(8,128)S(1)} %fusion.53), channel_id=1, source_target_pairs={{8,0},{16,8},{24,16},{32,24},{40,32},{48,40},{56,48},{64,56},{72,6... | collective-permute-start | bytes 393224 | tf_op jit(solution)/shard_map/while/body/eval_jaxpr/ppermute | solution.py:12
  373.0 10.0 %collective-permute-start = (f32[128,256]{1,0:T(8,128)S(1)}, f32[128,256]{1,0:T(8,128)S(1)}, u32[]{:S(2)}, u32[]{:S(2)}) collective-permute-start(f32[128,256]{1,0:T(8,128)S(1)} %fusion.53), channel_id=1, source_target_pairs={{8,0},{16,8},{24,16},{32,24},{40,32},{48,40},{56,48},{64,56},{72,6... | collective-permute-start | bytes 393224 | tf_op jit(solution)/shard_map/while/body/eval_jaxpr/ppermute | solution.py:12
  386.2 10.0 %collective-permute-start = (f32[128,256]{1,0:T(8,128)S(1)}, f32[128,256]{1,0:T(8,128)S(1)}, u32[]{:S(2)}, u32[]{:S(2)}) collective-permute-start(f32[128,256]{1,0:T(8,128)S(1)} %fusion.53), channel_id=1, source_target_pairs={{8,0},{16,8},{24,16},{32,24},{40,32},{48,40},{56,48},{64,56},{72,6... | collective-permute-start | bytes 393224 | tf_op jit(solution)/shard_map/while/body/eval_jaxpr/ppermute | solution.py:12
  399.5 11.3 %collective-permute-start = (f32[128,256]{1,0:T(8,128)S(1)}, f32[128,256]{1,0:T(8,128)S(1)}, u32[]{:S(2)}, u32[]{:S(2)}) collective-permute-start(f32[128,256]{1,0:T(8,128)S(1)} %fusion.53), channel_id=1, source_target_pairs={{8,0},{16,8},{24,16},{32,24},{40,32},{48,40},{56,48},{64,56},{72,6... | collective-permute-start | bytes 393224 | tf_op jit(solution)/shard_map/while/body/eval_jaxpr/ppermute | solution.py:12
  414.0 10.6 %collective-permute-start = (f32[128,256]{1,0:T(8,128)S(1)}, f32[128,256]{1,0:T(8,128)S(1)}, u32[]{:S(2)}, u32[]{:S(2)}) collective-permute-start(f32[128,256]{1,0:T(8,128)S(1)} %fusion.53), channel_id=1, source_target_pairs={{8,0},{16,8},{24,16},{32,24},{40,32},{48,40},{56,48},{64,56},{72,6... | collective-permute-start | bytes 393224 | tf_op jit(solution)/shard_map/while/body/eval_jaxpr/ppermute | solution.py:12
  427.8 10.3 %collective-permute-start = (f32[128,256]{1,0:T(8,128)S(1)}, f32[128,256]{1,0:T(8,128)S(1)}, u32[]{:S(2)}, u32[]{:S(2)}) collective-permute-start(f32[128,256]{1,0:T(8,128)S(1)} %fusion.53), channel_id=1, source_target_pairs={{8,0},{16,8},{24,16},{32,24},{40,32},{48,40},{56,48},{64,56},{72,6... | collective-permute-start | bytes 393224 | tf_op jit(solution)/shard_map/while/body/eval_jaxpr/ppermute | solution.py:12
Sparse Core Ops, SparseCore 0:
  158.1 58.5 reduce-scatter.1
  237.6 269.7 all-reduce.1
where the time goes:
time: 519 us; the launch traced here: 516 us
  waiting for transfers between devices  203 us (39%)
  starting transfers between devices  151 us (29%)
  local copies, waits for them, and re-layouts  66.3 us (13%)
  matrix products  36.1 us (7%)
  other arithmetic  26.9 us (5%)
  blocking collectives  16.9 us (3%)
  between operations  14.2 us (3%)
    ppermute x30, starting transfers between devices, passed_along(): return lax.ppermute(block, axis, route)  151 us
    ppermute x30, waiting for transfers between devices, passed_along(): return lax.ppermute(block, axis, route)  77.5 us
    psum x1, waiting for transfers between devices, per_device(): grad_weight = lax.psum(local_weight, ('blk', 'rep')) / math.sqrt(node_total)  67.5 us
    reduce_scatter x1, waiting for transfers between devices, per_device(): lax.psum_scatter(slab_partial, 'rep', scatter_dimension=0, tiled=True)  58 us
    dynamic_slice x31, local copies, waits for them, and re-layouts, load_distance(): lax.dynamic_index_in_dim(count_stack, distance, 0, keepdims=False)  29.8 us
    dot_general x16, matrix products, scatter_rows(): jnp.einsum('kij,kif->jf', tile_block, picked, preferred_element_type=jnp....  21.2 us
    all_gather x1, blocking collectives, per_device(): lax.all_gather(back_scaled, 'rep', axis=0, tiled=True)  16.9 us
    squeeze x16, local copies, waits for them, and re-layouts, load_distance(): lax.dynamic_index_in_dim(tile_stack, distance, 0, keepdims=False)  15.6 us
  transfers between devices with their start and end apart: 32, of which 32 were waited for; matrix products, arithmetic and copies ran while one was open for 22% of the time, Pallas kernels for 0%

commit v1 on v0

v1 whole, which is shorter than its diff:
```python
import math

import jax
import jax.numpy as jnp
from jax import lax
from jax.experimental import pallas as pl
from jax.experimental.pallas import tpu as pltpu
from jax.sharding import Mesh, PartitionSpec as P

BF = jnp.bfloat16
F32 = jnp.float32
ROW, COL, REP = "y", ("x", "zl"), ("zh", "core")
N_ROW, N_COL, N_ZH, N_CORE = 8, 8, 4, 2
N_REP = N_ZH * N_CORE


def arrange_kernel(rows_ref, counts_ref, col_ref, tile_ref, out_ref):
    distance = pl.program_id(0)
    col = col_ref[0]
    block = tile_ref.shape[-1]
    live_count = counts_ref[0, distance]
    wrapped = lax.rem(distance, N_COL)
    same_turn = col >= wrapped
    source = jnp.where(same_turn, col - wrapped, col - wrapped + N_COL)
    near = distance < N_COL
    slot = jnp.where(same_turn == near, 1, 0)
    place = source * 2 + slot
    for k in range(tile_ref.shape[2]):
        owner = rows_ref[0, distance, k]
        row = lax.rem(owner, N_CORE) * N_ZH + lax.div(owner, N_CORE)
        tile = tile_ref[0, 0, k]
        tile = jnp.where(k < live_count, tile, jnp.zeros_like(tile))
        out_ref[
            pl.ds(pl.multiple_of(row * block, block), block),
            pl.ds(pl.multiple_of(place * block, block), block),
        ] = tile


def arrange(tile_values, tile_rows, tile_counts, col):
    _, span, cap, rows, cols = tile_values.shape
    size = span * cap * rows * cols
    return pl.pallas_call(
        arrange_kernel,
        out_shape=jax.ShapeDtypeStruct((cap * rows, span * cols), BF),
        grid_spec=pltpu.PrefetchScalarGridSpec(
            num_scalar_prefetch=3,
            grid=(span,),
            in_specs=[pl.BlockSpec((1, 1, cap, rows, cols), lambda s, *_: (0, s, 0, 0, 0))],
            out_specs=pl.BlockSpec((cap * rows, span * cols), lambda s, *_: (0, 0)),
        ),
        cost_estimate=pl.CostEstimate(flops=size, bytes_accessed=4 * size, transcendentals=0),
        name="arrange_tiles",
    )(tile_rows, tile_counts, col, tile_values)


def shifted(block, distance):
    return lax.ppermute(block, ROW, [((i - distance) % N_ROW, i) for i in range(N_ROW)])


def copies_to(block, axis, count):
    return lax.all_to_all(jnp.broadcast_to(block[None], (count,) + block.shape), axis, 0, 0)


def summed_in_f32(stack):
    return jnp.sum(stack.astype(F32), axis=0)


def per_device(features, degrees, tile_values, tile_rows, tile_counts, weight, cotangent):
    own_rows, width = features.shape
    col = lax.axis_index(COL)
    columns = jnp.arange(N_COL, dtype=jnp.int32)[:, None, None]
    inv_root = lax.rsqrt(degrees.astype(F32))[:, None]
    scaled = (features.astype(F32) * inv_root).astype(BF)

    one_back = shifted(scaled, 1)
    two_back = shifted(scaled, 2)
    adjacency = arrange(tile_values, tile_rows, tile_counts, col[None])
    own_or_two = jnp.where(columns >= col, scaled[None], two_back[None])
    offer = jnp.stack([jnp.broadcast_to(one_back[None], own_or_two.shape), own_or_two], axis=1)
    window = lax.all_to_all(offer, COL, 0, 0).reshape(-1, width)

    partial = jnp.dot(adjacency, window, preferred_element_type=F32).astype(BF)
    halves = lax.all_to_all(partial.reshape(N_CORE, -1, width), "core", 0, 0)
    half = summed_in_f32(halves).astype(BF)
    shares = lax.all_to_all(half.reshape(N_ZH, own_rows, width), "zh", 0, 0)
    own_sum = summed_in_f32(shares)

    aggregated = (own_sum * inv_root).astype(BF)
    pre_act = jnp.dot(aggregated, weight, preferred_element_type=F32)
    sigma = jax.nn.sigmoid(pre_act)
    activations = (pre_act * sigma).astype(BF)
    act_grad = (cotangent.astype(F32) * sigma * (1.0 + pre_act * (1.0 - sigma))).astype(BF)
    back_grad = lax.dot_general(
        act_grad, weight, (((1,), (1,)), ((), ())), preferred_element_type=F32
    )
    back_scaled = (back_grad * inv_root).astype(BF)
    along_zh = copies_to(back_scaled, "zh", N_ZH).reshape(-1, width)
    slab_grads = lax.all_gather(along_zh, "core", axis=0, tiled=True)

    local_weight = lax.dot_general(
        aggregated, act_grad, (((0,), (0,)), ((), ())), preferred_element_type=F32
    )
    weight_rows = lax.all_to_all(local_weight.astype(BF).reshape(N_REP, -1, width), REP, 0, 0)
    weight_rows = summed_in_f32(weight_rows).astype(BF)
    weight_rows = summed_in_f32(copies_to(weight_rows, COL, N_COL)).astype(BF)
    weight_rows = summed_in_f32(copies_to(weight_rows, ROW, N_ROW))
    node_total = own_rows * N_ROW * N_COL * N_REP
    weight_rows = (weight_rows / math.sqrt(node_total)).astype(BF)
    grad_weight = copies_to(weight_rows, REP, N_REP).reshape(-1, width).astype(F32)

    returned = lax.dot_general(
        adjacency, slab_grads, (((0,), (0,)), ((), ())), preferred_element_type=F32
    ).astype(BF)
    arrived = lax.all_to_all(
        returned.reshape(N_COL, 2, own_rows, width), COL, 0, 0
    ).astype(F32)
    for_one = jnp.sum(arrived[:, 0], axis=0).astype(BF)
    for_two = jnp.sum(jnp.where(columns < col, arrived[:, 1], 0.0), axis=0).astype(BF)
    for_own = jnp.sum(jnp.where(columns >= col, arrived[:, 1], 0.0), axis=0)
    from_one = shifted(for_one, -1)
    from_two = shifted(for_two, -2)
    back_total = for_own + from_one.astype(F32) + from_two.astype(F32)
    grad_features = (back_total * inv_root).astype(BF)
    return (activations, grad_weight, grad_features)


def solution(mesh):
    fine = Mesh(
        mesh.devices.reshape(N_ROW, 4, 2, N_ZH, N_CORE), ("y", "x", "zl", "zh", "core")
    )
    nodes = ("y", "x", "zl", "zh", "core")
    placed = (
        P(nodes, None),
        P(nodes),
        P(nodes, None, None, None, None),
        P(nodes, None, None),
        P(nodes, None),
        P(),
        P(nodes, None),
    )
    return jax.shard_map(
        per_device,
        mesh=fine,
        in_specs=placed,
        out_specs=(P(nodes, None), P(), P(nodes, None)),
        check_vma=False,
    )
```

time: 519 us -> 152 us (0.29)
  waiting for transfers between devices: 203 us -> 38.6 us
  starting transfers between devices: 151 us -> 51.4 us
  local copies, waits for them, and re-layouts: 66.3 us -> 3.44 us
  matrix products: 36.1 us -> 9.99 us
  other arithmetic: 26.9 us -> 5.03 us
  between operations: 14.2 us -> 0.82 us
  blocking collectives: 16.9 us -> 30.1 us
  Pallas kernels: 0 us -> 11.5 us
    ppermute x30 -> x4, starting transfers between devices: 151 us -> 13.4 us  [shifted(): lax.ppermute(block, ROW, [((i - distance) % N_ROW, i) for i in range(N_RO...]
    ppermute x30 -> x4, waiting for transfers between devices: 77.5 us -> 3.51 us  [shifted(): lax.ppermute(block, ROW, [((i - distance) % N_ROW, i) for i in range(N_RO...]
    psum x1 -> x0, waiting for transfers between devices: 67.5 us -> none  [per_device(): grad_weight = lax.psum(local_weight, ('blk', 'rep')) / math.sqrt(node_total)]
    reduce_scatter x1 -> x0, waiting for transfers between devices: 58 us -> none  [per_device(): lax.psum_scatter(slab_partial, 'rep', scatter_dimension=0, tiled=True)]
    all_to_all x0 -> x7, starting transfers between devices: none -> 38 us  [the longest x4 21.5 us: copies_to(): lax.all_to_all(jnp.broadcast_to(block[None], (count,) + block.shape), axi...]
    all_to_all x0 -> x7, waiting for transfers between devices: none -> 35.1 us  [the longest x4 14.8 us: copies_to(): lax.all_to_all(jnp.broadcast_to(block[None], (count,) + block.shape), axi...]
    dynamic_slice x32 -> x0, local copies, waits for them, and re-layouts: 30.8 us -> none  [the longest x31 29.8 us: load_distance(): lax.dynamic_index_in_dim(count_stack, distance, 0, keepdims=False)]
    all_to_all x0 -> x2, blocking collectives: none -> 25.4 us  [the longest x1 18.3 us: per_device(): shares = lax.all_to_all(half.reshape(N_ZH, own_rows, width), 'zh', 0, 0)]
  transfers between devices with their start and end apart: 32 -> 11, of which waited for: 32 -> 10; matrix products, arithmetic and copies ran while one was open for 22% -> 4% of each run, Pallas kernels for 0% -> 8%
where the time goes in v1:
time: 152 us; the launch traced here: 151 us
  starting transfers between devices  51.4 us (34%)
  waiting for transfers between devices  38.6 us (25%)
  blocking collectives  30.1 us (20%)
  Pallas kernels  11.5 us (8%)
  matrix products  9.99 us (7%)
  other arithmetic  5.03 us (3%)
  local copies, waits for them, and re-layouts  3.44 us (2%)
    all_to_all x4, starting transfers between devices, copies_to(): lax.all_to_all(jnp.broadcast_to(block[None], (count,) + block.shape), axi...  21.5 us
    all_to_all x1, blocking collectives, per_device(): shares = lax.all_to_all(half.reshape(N_ZH, own_rows, width), 'zh', 0, 0)  18.3 us
    all_to_all x4, waiting for transfers between devices, copies_to(): lax.all_to_all(jnp.broadcast_to(block[None], (count,) + block.shape), axi...  14.8 us
    ppermute x4, starting transfers between devices, shifted(): lax.ppermute(block, ROW, [((i - distance) % N_ROW, i) for i in range(N_RO...  13.4 us
    pallas_call x1, Pallas kernels, arrange(): pl.pallas_call(arrange_kernel, out_shape=jax.ShapeDtypeStruct((cap * rows...  11.5 us
    all_to_all x1, waiting for transfers between devices, per_device(): lax.all_to_all(returned.reshape(N_COL, 2, own_rows, width), COL, 0, 0)  11.1 us
    all_to_all x1, waiting for transfers between devices, per_device(): lax.all_to_all(local_weight.astype(BF).reshape(N_REP, -1, width), REP, 0, 0)  7.93 us
    all_to_all x1, blocking collectives, per_device(): halves = lax.all_to_all(partial.reshape(N_CORE, -1, width), 'core', 0, 0)  7.14 us
  transfers between devices with their start and end apart: 11, of which 10 were waited for; matrix products, arithmetic and copies ran while one was open for 4% of the time, Pallas kernels for 8%

profile of v1, /device:TPU:1, one launch (start us, length us, event | category | flops | bytes accessed | tf_op | source)
XLA Modules:
  0.0 150.9 jit_solution(17981514707336543213)
XLA Ops:
  0.6 0.0 copy-start
  0.6 0.0 copy-start.1
  0.7 0.7 convert_rsqrt_fusion
  1.4 0.9 multiply_convert_fusion.4
  2.3 5.0 %collective-permute-start.1 = (bf16[128,256]{1,0:T(8,128)(2,1)S(1)}, bf16[128,256]{1,0:T(8,128)(2,1)S(1)}, u32[]{:S(2)}, u32[]{:S(2)}) collective-permute-start(bf16[128,256]{1,0:T(8,128)(2,1)S(1)} %multiply_convert_fusion.4), channel_id=1, source_target_pairs={{384,0},{448,64},{0,128},{64,192},{128,256},{192,320},{256,384},{3... | collective-permute-start | bytes 196616 | tf_op jit(solution)/shard_map/ppermute | solution.py:57
  7.3 3.2 %collective-permute-start = (bf16[128,256]{1,0:T(8,128)(2,1)S(1)}, bf16[128,256]{1,0:T(8,128)(2,1)S(1)}, u32[]{:S(2)}, u32[]{:S(2)}) collective-permute-start(bf16[128,256]{1,0:T(8,128)(2,1)S(1)} %multiply_convert_fusion.4), channel_id=1, source_target_pairs={{448,0},{0,64},{64,128},{128,192},{192,256},{256,320},{320,384},{3... | collective-permute-start | bytes 196616 | tf_op jit(solution)/shard_map/ppermute | solution.py:57
  10.6 0.2 collective-permute-done.1
  10.7 0.1 broadcast_select_fusion
  10.9 2.7 %collective-permute-done = bf16[128,256]{1,0:T(8,128)(2,1)S(1)} collective-permute-done((bf16[128,256]{1,0:T(8,128)(2,1)S(1)}, bf16[128,256]{1,0:T(8,128)(2,1)S(1)}, u32[]{:S(2)}, u32[]{:S(2)}) %collective-permute-start) | collective-permute-done | bytes 65568 | tf_op jit(solution)/shard_map/ppermute | solution.py:57
  13.6 1.1 pad_maximum_fusion
  14.7 5.8 %all-to-all-start = ((bf16[8,2,128,256]{3,2,1,0:T(8,128)(2,1)}), bf16[8,2,128,256]{3,2,1,0:T(8,128)(2,1)S(1)}, u32[]{:S(2)}, u32[]{:S(2)}) async-start(bf16[8,2,128,256]{3,2,1,0:T(8,128)(2,1)} %pad_maximum_fusion), calls=%async_computation | async-start | bytes 2097152 | tf_op jit(solution)/shard_map/all_to_all | solution.py:80
  20.5 0.7 copy.11.rows_ref
  21.2 11.5 %arrange_tiles.1 = bf16[1024,2048]{1,0:T(8,128)(2,1)} custom-call(s32[1,16,8]{2,1,0:T(8,128)} %copy.11.rows_ref, s32[1,16]{1,0:T(1,128)} %counts_ref.1, s32[1]{0:T(128)} %bitcast.col_ref, bf16[1,16,8,128,128]{4,3,2,1,0:T(8,128)(2,1)} %tile_ref.1), custom_call_target="tpu_custom_call" | custom-call | flops 2097152 | bytes 8388608 | tf_op jit(solution)/shard_map/arrange_tiles/pallas_call | solution.py:42
  32.7 1.2 all-to-all-done
  33.8 3.5 %convolution_convert_fusion.1 = bf16[1024,256]{1,0:T(8,128)(2,1)S(1)} fusion(bf16[1024,2048]{1,0:T(8,128)(2,1)} %arrange_tiles.1, bf16[2048,256]{1,0:T(8,128)(2,1)S(1)} %bitcast.25), kind=kOutput, calls=%fused_computation.1 | convolution fusion | flops 1074003968 | bytes 5767168 | tf_op jit(solution)/shard_map/dot_general | solution.py:82
  37.3 7.1 %all_to_all.45 = bf16[2,512,256]{2,1,0:T(8,128)(2,1)S(1)} all-to-all(bf16[2,512,256]{2,1,0:T(8,128)(2,1)S(1)} %bitcast.27), channel_id=1, replica_groups=mesh['y'=8,'x'=4,'zl'=2,'zh'=4,'core'=2] {'core'}, dimensions={0} | all-to-all | bytes 1048576 | tf_op jit(solution)/shard_map/all_to_all | solution.py:83
  44.4 0.2 reduce_sum.81
  44.6 18.3 %all_to_all.46 = bf16[4,128,256]{2,1,0:T(8,128)(2,1)S(1)} all-to-all(bf16[4,128,256]{2,1,0:T(8,128)(2,1)S(1)} %bitcast.26), channel_id=1, replica_groups=mesh['y'=8,'x'=4,'zl'=2,'zh'=4,'core'=2] {'zh'}, dimensions={0} | all-to-all | bytes 524288 | tf_op jit(solution)/shard_map/all_to_all | solution.py:85
  63.0 0.9 multiply_convert_fusion.1
  63.9 0.9 convolution_convert_fusion.2
  64.8 5.7 %all-to-all-start.3 = ((bf16[8,32,256]{2,1,0:T(8,128)(2,1)}), bf16[8,32,256]{2,1,0:T(8,128)(2,1)S(1)}, u32[]{:S(2)}, u32[]{:S(2)}) async-start(bf16[8,32,256]{2,1,0:T(8,128)(2,1)} %bitcast.4), calls=%async_computation.3 | async-start | bytes 262144 | tf_op jit(solution)/shard_map/all_to_all | solution.py:103
  70.6 0.2 fusion
  70.8 7.9 %all-to-all-done.3 = bf16[8,32,256]{2,1,0:T(8,128)(2,1)S(1)} async-done(((bf16[8,32,256]{2,1,0:T(8,128)(2,1)}), bf16[8,32,256]{2,1,0:T(8,128)(2,1)S(1)}, u32[]{:S(2)}, u32[]{:S(2)}) %all-to-all-start.3) | async-done | bytes 131104 | tf_op jit(solution)/shard_map/all_to_all | solution.py:103
  78.7 0.7 broadcast_in_dim.82
  79.4 3.4 %all-to-all-start.7 = ((bf16[4,128,256]{2,1,0:T(8,128)(2,1)}), bf16[4,128,256]{2,1,0:T(8,128)(2,1)S(1)}, u32[]{:S(2)}, u32[]{:S(2)}) async-start(bf16[4,128,256]{2,1,0:T(8,128)(2,1)} %broadcast_in_dim.82), calls=%async_computation.7 | async-start | bytes 524288 | tf_op jit(solution)/shard_map/all_to_all | solution.py:61
  82.8 8.1 %all-to-all-done.7 = bf16[4,128,256]{2,1,0:T(8,128)(2,1)S(1)} async-done(((bf16[4,128,256]{2,1,0:T(8,128)(2,1)}), bf16[4,128,256]{2,1,0:T(8,128)(2,1)S(1)}, u32[]{:S(2)}, u32[]{:S(2)}) %all-to-all-start.7) | async-done | bytes 262176 | tf_op jit(solution)/shard_map/all_to_all | solution.py:61
  90.9 0.7 broadcast_in_dim.78
  91.6 4.3 %all-to-all-start.4 = ((bf16[8,32,256]{2,1,0:T(8,128)(2,1)}), bf16[8,32,256]{2,1,0:T(8,128)(2,1)S(1)}, u32[]{:S(2)}, u32[]{:S(2)}) async-start(bf16[8,32,256]{2,1,0:T(8,128)(2,1)} %broadcast_in_dim.78), calls=%async_computation.4 | async-start | bytes 262144 | tf_op jit(solution)/shard_map/all_to_all | solution.py:61
  95.8 4.7 %all_gather.3 = bf16[1024,256]{1,0:T(8,128)(2,1)S(1)} all-gather(bf16[512,256]{1,0:T(8,128)(2,1)S(1)} %bitcast.24), channel_id=1, replica_groups=mesh['y'=8,'x'=4,'zl'=2,'zh'=4,'core'=2] {'core'}, dimensions={0}, use_global_device_ids=true | all-gather | bytes 786432 | tf_op jit(solution)/shard_map/all_gather | solution.py:98
  100.5 0.9 all-to-all-done.4
  101.4 0.7 broadcast_in_dim.79
  102.1 5.0 %all-to-all-start.5 = ((bf16[8,32,256]{2,1,0:T(8,128)(2,1)}), bf16[8,32,256]{2,1,0:T(8,128)(2,1)S(1)}, u32[]{:S(2)}, u32[]{:S(2)}) async-start(bf16[8,32,256]{2,1,0:T(8,128)(2,1)} %broadcast_in_dim.79), calls=%async_computation.5 | async-start | bytes 262144 | tf_op jit(solution)/shard_map/all_to_all | solution.py:61
  107.1 4.5 %convolution_convert_fusion = bf16[2048,256]{1,0:T(8,128)(2,1)} fusion(bf16[1024,2048]{1,0:T(8,128)(2,1)} %arrange_tiles.1, bf16[1024,256]{1,0:T(8,128)(2,1)S(1)} %all_gather.3), kind=kOutput, calls=%fused_computation | convolution fusion | flops 1074266112 | bytes 5767168 | tf_op jit(solution)/shard_map/dot_general | solution.py:111
  111.6 3.4 %all-to-all-done.5 = bf16[8,32,256]{2,1,0:T(8,128)(2,1)S(1)} async-done(((bf16[8,32,256]{2,1,0:T(8,128)(2,1)}), bf16[8,32,256]{2,1,0:T(8,128)(2,1)S(1)}, u32[]{:S(2)}, u32[]{:S(2)}) %all-to-all-start.5) | async-done | bytes 131104 | tf_op jit(solution)/shard_map/all_to_all | solution.py:61
  115.0 4.9 %all-to-all-start.8 = ((bf16[8,2,128,256]{3,2,1,0:T(8,128)(2,1)}), bf16[8,2,128,256]{3,2,1,0:T(8,128)(2,1)S(1)}, u32[]{:S(2)}, u32[]{:S(2)}) async-start(bf16[8,2,128,256]{3,2,1,0:T(8,128)(2,1)} %bitcast.7), calls=%async_computation.8 | async-start | bytes 2097152 | tf_op jit(solution)/shard_map/all_to_all | solution.py:114
  120.0 11.1 %all-to-all-done.8 = bf16[8,2,128,256]{3,2,1,0:T(8,128)(2,1)S(1)} async-done(((bf16[8,2,128,256]{3,2,1,0:T(8,128)(2,1)}), bf16[8,2,128,256]{3,2,1,0:T(8,128)(2,1)S(1)}, u32[]{:S(2)}, u32[]{:S(2)}) %all-to-all-start.8) | async-done | bytes 1048608 | tf_op jit(solution)/shard_map/all_to_all | solution.py:114
  131.2 0.7 broadcast_in_dim.80
  131.8 8.8 %all-to-all-start.6 = ((bf16[8,32,256]{2,1,0:T(8,128)(2,1)}), bf16[8,32,256]{2,1,0:T(8,128)(2,1)S(1)}, u32[]{:S(2)}, u32[]{:S(2)}) async-start(bf16[8,32,256]{2,1,0:T(8,128)(2,1)} %broadcast_in_dim.80), calls=%async_computation.6 | async-start | bytes 262144 | tf_op jit(solution)/shard_map/all_to_all | solution.py:61
  140.6 0.2 convert_element_type.92
  140.9 0.2 select_reduce_fusion.1
  141.1 2.0 %collective-permute-start.3 = (bf16[128,256]{1,0:T(8,128)(2,1)S(1)}, bf16[128,256]{1,0:T(8,128)(2,1)S(1)}, u32[]{:S(2)}, u32[]{:S(2)}) collective-permute-start(bf16[128,256]{1,0:T(8,128)(2,1)S(1)} %get-tuple-element.4), channel_id=1, source_target_pairs={{128,0},{192,64},{256,128},{320,192},{384,256},{448,320},{0,384},{... | collective-permute-start | bytes 196616 | tf_op jit(solution)/shard_map/ppermute | solution.py:57
  143.1 0.1 slice_reduce_fusion
  143.2 3.1 %collective-permute-start.2 = (bf16[128,256]{1,0:T(8,128)(2,1)S(1)}, bf16[128,256]{1,0:T(8,128)(2,1)S(1)}, u32[]{:S(2)}, u32[]{:S(2)}) collective-permute-start(bf16[128,256]{1,0:T(8,128)(2,1)S(1)} %slice_reduce_fusion), channel_id=1, source_target_pairs={{64,0},{128,64},{192,128},{256,192},{320,256},{384,320},{448,384},... | collective-permute-start | bytes 196616 | tf_op jit(solution)/shard_map/ppermute | solution.py:57
  146.3 2.5 %all-to-all-done.6 = bf16[8,32,256]{2,1,0:T(8,128)(2,1)S(1)} async-done(((bf16[8,32,256]{2,1,0:T(8,128)(2,1)}), bf16[8,32,256]{2,1,0:T(8,128)(2,1)S(1)}, u32[]{:S(2)}, u32[]{:S(2)}) %all-to-all-start.6) | async-done | bytes 131104 | tf_op jit(solution)/shard_map/all_to_all | solution.py:61
  148.8 0.7 bitcast_convert_fusion
  149.5 0.0 collective-permute-done.3
  149.5 0.6 collective-permute-done.2
  150.1 0.7 multiply_convert_fusion
  (12 shorter events, 0.2 us)
Async XLA Ops:
  0.6 62.3 %copy-start = (bf16[256,256]{1,0:T(8,128)(2,1)S(1)}, bf16[256,256]{1,0:T(8,128)(2,1)}, u32[]{:S(2)}) copy-start(bf16[256,256]{1,0:T(8,128)(2,1)} %param.12) | copy-start | bytes 393220
  0.6 19.8 %copy-start.1 = (s32[1,16,8]{1,2,0:T(8,128)S(1)}, s32[1,16,8]{1,2,0:T(8,128)}, u32[]{:S(2)}) copy-start(s32[1,16,8]{1,2,0:T(8,128)} %param.10) | copy-start | bytes 1540
  2.3 8.5 %collective-permute-start.1 = (bf16[128,256]{1,0:T(8,128)(2,1)S(1)}, bf16[128,256]{1,0:T(8,128)(2,1)S(1)}, u32[]{:S(2)}, u32[]{:S(2)}) collective-permute-start(bf16[128,256]{1,0:T(8,128)(2,1)S(1)} %multiply_convert_fusion.4), channel_id=1, source_target_pairs={{384,0},{448,64},{0,128},{64,192},{128,256},{192,320},{256,384},{3... | collective-permute-start | bytes 196616 | tf_op jit(solution)/shard_map/ppermute | solution.py:57
  7.3 6.2 %collective-permute-start = (bf16[128,256]{1,0:T(8,128)(2,1)S(1)}, bf16[128,256]{1,0:T(8,128)(2,1)S(1)}, u32[]{:S(2)}, u32[]{:S(2)}) collective-permute-start(bf16[128,256]{1,0:T(8,128)(2,1)S(1)} %multiply_convert_fusion.4), channel_id=1, source_target_pairs={{448,0},{0,64},{64,128},{128,192},{192,256},{256,320},{320,384},{3... | collective-permute-start | bytes 196616 | tf_op jit(solution)/shard_map/ppermute | solution.py:57
  14.7 19.2 %all-to-all-start = ((bf16[8,2,128,256]{3,2,1,0:T(8,128)(2,1)}), bf16[8,2,128,256]{3,2,1,0:T(8,128)(2,1)S(1)}, u32[]{:S(2)}, u32[]{:S(2)}) async-start(bf16[8,2,128,256]{3,2,1,0:T(8,128)(2,1)} %pad_maximum_fusion), calls=%async_computation | async-start | bytes 2097152 | tf_op jit(solution)/shard_map/all_to_all | solution.py:80
  33.8 29.1 %copy-start.2 = (bf16[128,256]{1,0:T(8,128)(2,1)S(1)}, bf16[128,256]{1,0:T(8,128)(2,1)}, u32[]{:S(2)}) copy-start(bf16[128,256]{1,0:T(8,128)(2,1)} %param.13) | copy-start | bytes 196612
  64.8 13.9 %all-to-all-start.3 = ((bf16[8,32,256]{2,1,0:T(8,128)(2,1)}), bf16[8,32,256]{2,1,0:T(8,128)(2,1)S(1)}, u32[]{:S(2)}, u32[]{:S(2)}) async-start(bf16[8,32,256]{2,1,0:T(8,128)(2,1)} %bitcast.4), calls=%async_computation.3 | async-start | bytes 262144 | tf_op jit(solution)/shard_map/all_to_all | solution.py:103
  79.4 11.5 %all-to-all-start.7 = ((bf16[4,128,256]{2,1,0:T(8,128)(2,1)}), bf16[4,128,256]{2,1,0:T(8,128)(2,1)S(1)}, u32[]{:S(2)}, u32[]{:S(2)}) async-start(bf16[4,128,256]{2,1,0:T(8,128)(2,1)} %broadcast_in_dim.82), calls=%async_computation.7 | async-start | bytes 524288 | tf_op jit(solution)/shard_map/all_to_all | solution.py:61
  91.6 9.8 %all-to-all-start.4 = ((bf16[8,32,256]{2,1,0:T(8,128)(2,1)}), bf16[8,32,256]{2,1,0:T(8,128)(2,1)S(1)}, u32[]{:S(2)}, u32[]{:S(2)}) async-start(bf16[8,32,256]{2,1,0:T(8,128)(2,1)} %broadcast_in_dim.78), calls=%async_computation.4 | async-start | bytes 262144 | tf_op jit(solution)/shard_map/all_to_all | solution.py:61
  102.1 13.0 %all-to-all-start.5 = ((bf16[8,32,256]{2,1,0:T(8,128)(2,1)}), bf16[8,32,256]{2,1,0:T(8,128)(2,1)S(1)}, u32[]{:S(2)}, u32[]{:S(2)}) async-start(bf16[8,32,256]{2,1,0:T(8,128)(2,1)} %broadcast_in_dim.79), calls=%async_computation.5 | async-start | bytes 262144 | tf_op jit(solution)/shard_map/all_to_all | solution.py:61
  115.0 16.1 %all-to-all-start.8 = ((bf16[8,2,128,256]{3,2,1,0:T(8,128)(2,1)}), bf16[8,2,128,256]{3,2,1,0:T(8,128)(2,1)S(1)}, u32[]{:S(2)}, u32[]{:S(2)}) async-start(bf16[8,2,128,256]{3,2,1,0:T(8,128)(2,1)} %bitcast.7), calls=%async_computation.8 | async-start | bytes 2097152 | tf_op jit(solution)/shard_map/all_to_all | solution.py:114
  131.8 17.0 %all-to-all-start.6 = ((bf16[8,32,256]{2,1,0:T(8,128)(2,1)}), bf16[8,32,256]{2,1,0:T(8,128)(2,1)S(1)}, u32[]{:S(2)}, u32[]{:S(2)}) async-start(bf16[8,32,256]{2,1,0:T(8,128)(2,1)} %broadcast_in_dim.80), calls=%async_computation.6 | async-start | bytes 262144 | tf_op jit(solution)/shard_map/all_to_all | solution.py:61
  141.1 8.4 %collective-permute-start.3 = (bf16[128,256]{1,0:T(8,128)(2,1)S(1)}, bf16[128,256]{1,0:T(8,128)(2,1)S(1)}, u32[]{:S(2)}, u32[]{:S(2)}) collective-permute-start(bf16[128,256]{1,0:T(8,128)(2,1)S(1)} %get-tuple-element.4), channel_id=1, source_target_pairs={{128,0},{192,64},{256,128},{320,192},{384,256},{448,320},{0,384},{... | collective-permute-start | bytes 196616 | tf_op jit(solution)/shard_map/ppermute | solution.py:57
  143.2 6.9 %collective-permute-start.2 = (bf16[128,256]{1,0:T(8,128)(2,1)S(1)}, bf16[128,256]{1,0:T(8,128)(2,1)S(1)}, u32[]{:S(2)}, u32[]{:S(2)}) collective-permute-start(bf16[128,256]{1,0:T(8,128)(2,1)S(1)} %slice_reduce_fusion), channel_id=1, source_target_pairs={{64,0},{128,64},{192,128},{256,192},{320,256},{384,320},{448,384},... | collective-permute-start | bytes 196616 | tf_op jit(solution)/shard_map/ppermute | solution.py:57

commit v2 on v1

v2 whole, which is shorter than its diff:
```python
import math

import jax
import jax.numpy as jnp
from jax import lax
from jax.experimental import pallas as pl
from jax.experimental.pallas import tpu as pltpu
from jax.sharding import Mesh, PartitionSpec as P


BF = jnp.bfloat16
F32 = jnp.float32
ROW, COL, REP = "y", ("x", "zl"), ("zh", "core")
N_ROW, N_COL, N_ZH, N_CORE = 8, 8, 4, 2
N_REP = N_ZH * N_CORE


def arrange_kernel(rows_ref, counts_ref, col_ref, tile_hbm, out_ref, flip_ref, tiles, arrived):
    _, span, cap, block, _ = tile_hbm.shape

    def fetch(distance):
        return pltpu.make_async_copy(
            tile_hbm.at[0, distance], tiles.at[distance], arrived.at[distance]
        )

    for distance in range(span):
        fetch(distance).start()
    col = col_ref[0]

    def place_distance(distance, carry):
        fetch(distance).wait()
        live_count = counts_ref[0, distance]
        wrapped = lax.rem(distance, N_COL)
        same_turn = col >= wrapped
        source = jnp.where(same_turn, col - wrapped, col - wrapped + N_COL)
        near = distance < N_COL
        slot = jnp.where(same_turn == near, 1, 0)
        at_col = pl.ds(pl.multiple_of((source * 2 + slot) * block, block), block)
        for k in range(cap):
            owner = rows_ref[0, distance, k]
            row = lax.rem(owner, N_CORE) * N_ZH + lax.div(owner, N_CORE)
            at_row = pl.ds(pl.multiple_of(row * block, block), block)
            tile = tiles[distance, k]
            tile = jnp.where(k < live_count, tile, jnp.zeros_like(tile))
            out_ref[at_row, at_col] = tile
            flip_ref[at_col, at_row] = tile.T
        return carry

    lax.fori_loop(0, span, place_distance, 0)


def arrange(tile_values, tile_rows, tile_counts, col):
    _, span, cap, rows, cols = tile_values.shape
    size = span * cap * rows * cols
    whole = pl.BlockSpec(memory_space=pltpu.VMEM)
    scalars = pl.BlockSpec(memory_space=pltpu.SMEM)
    return pl.pallas_call(
        arrange_kernel,
        out_shape=(
            jax.ShapeDtypeStruct((cap * rows, span * cols), BF),
            jax.ShapeDtypeStruct((span * cols, cap * rows), BF),
        ),
        in_specs=[scalars, scalars, scalars, pl.BlockSpec(memory_space=pltpu.HBM)],
        out_specs=(whole, whole),
        scratch_shapes=[
            pltpu.VMEM((span, cap, rows, cols), BF),
            pltpu.SemaphoreType.DMA((span,)),
        ],
        cost_estimate=pl.CostEstimate(flops=size, bytes_accessed=4 * size, transcendentals=0),
        name="arrange_tiles",
    )(tile_rows, tile_counts, col, tile_values)


def shifted(block, distance):
    return lax.ppermute(block, ROW, [((i - distance) % N_ROW, i) for i in range(N_ROW)])


def copies_to(block, axis, count):
    return lax.all_to_all(jnp.broadcast_to(block[None], (count,) + block.shape), axis, 0, 0)


def summed_in_f32(blocks):
    total = blocks[0].astype(F32)
    for block in blocks[1:]:
        total = total + block.astype(F32)
    return total


def per_device(features, degrees, tile_values, tile_rows, tile_counts, weight, cotangent):
    own_rows, width = features.shape
    col = lax.axis_index(COL)
    columns = jnp.arange(N_COL, dtype=jnp.int32)[:, None, None]
    inv_root = lax.rsqrt(degrees.astype(F32))[:, None]
    scaled = (features.astype(F32) * inv_root).astype(BF)

    one_back = shifted(scaled, 1)
    two_back = shifted(scaled, 2)
    adjacency, flipped = arrange(tile_values, tile_rows, tile_counts, col[None])
    own_or_two = jnp.where(columns >= col, scaled[None], two_back[None])
    offer = jnp.stack([jnp.broadcast_to(one_back[None], own_or_two.shape), own_or_two], axis=1)
    window = lax.all_to_all(offer, COL, 0, 0).reshape(-1, width)

    partial = jnp.dot(adjacency, window, preferred_element_type=F32).astype(BF)
    core = lax.axis_index("core")
    halves = lax.all_to_all(partial.reshape(N_CORE, -1, width), "core", 0, 0)
    half = summed_in_f32(halves).astype(BF)
    shares = lax.all_to_all(half.reshape(N_ZH, own_rows, width), "zh", 0, 0)
    own_sum = summed_in_f32(shares)

    aggregated = (own_sum * inv_root).astype(BF)
    pre_act = jnp.dot(aggregated, weight, preferred_element_type=F32)
    sigma = jax.nn.sigmoid(pre_act)
    activations = (pre_act * sigma).astype(BF)
    act_grad = (cotangent.astype(F32) * sigma * (1.0 + pre_act * (1.0 - sigma))).astype(BF)
    back_grad = lax.dot_general(
        act_grad, weight, (((1,), (1,)), ((), ())), preferred_element_type=F32
    )
    back_scaled = (back_grad * inv_root).astype(BF)
    local_weight = lax.dot_general(
        aggregated, act_grad, (((0,), (0,)), ((), ())), preferred_element_type=F32
    ).astype(BF)
    copies = jnp.broadcast_to(back_scaled[None], (N_ZH,) + back_scaled.shape)
    offer = jnp.concatenate([copies, local_weight.reshape(N_ZH, -1, width)], axis=1)
    given = lax.all_to_all(offer, "zh", 0, 0)
    along_zh = given[:, :own_rows].reshape(-1, width)
    weight_part = summed_in_f32(given[:, own_rows:]).astype(BF)
    pair = lax.all_gather(
        jnp.concatenate([along_zh, weight_part], axis=0), "core", axis=0, tiled=False
    )
    gathered = along_zh.shape[0]
    slab_grads = pair[:, :gathered].reshape(-1, width)
    weight_pair = pair[:, gathered:].reshape(N_CORE, N_CORE, -1, width)
    weight_rows = summed_in_f32(lax.dynamic_index_in_dim(weight_pair, core, 1, keepdims=False))

    along_y = copies_to(weight_rows.astype(BF), ROW, N_ROW)
    weight_rows = summed_in_f32(along_y).astype(BF)
    returned = jnp.dot(flipped, slab_grads, preferred_element_type=F32).astype(BF)
    returned = returned.reshape(N_COL, 2 * own_rows, width)
    copies = jnp.broadcast_to(weight_rows[None], (N_COL,) + weight_rows.shape)
    home = lax.all_to_all(jnp.concatenate([returned, copies], axis=1), COL, 0, 0)
    node_total = own_rows * N_ROW * N_COL * N_REP
    weight_rows = (summed_in_f32(home[:, 2 * own_rows :]) / math.sqrt(node_total)).astype(BF)
    along_rep = copies_to(weight_rows, REP, N_REP)
    grad_weight = along_rep.reshape(-1, width).astype(F32)

    arrived = home[:, : 2 * own_rows].reshape(N_COL, 2, own_rows, width)
    for_one = summed_in_f32(arrived[:, 0]).astype(BF)
    nothing = jnp.zeros((), BF)
    for_two = summed_in_f32(jnp.where(columns < col, arrived[:, 1], nothing)).astype(BF)
    for_own = summed_in_f32(jnp.where(columns >= col, arrived[:, 1], nothing))
    from_two = shifted(for_two, -2)
    from_one = shifted(for_one, -1)
    back_total = for_own + from_one.astype(F32) + from_two.astype(F32)
    grad_features = (back_total * inv_root).astype(BF)
    return (activations, grad_weight, grad_features)


def solution(mesh):
    fine = Mesh(
        mesh.devices.reshape(N_ROW, 4, 2, N_ZH, N_CORE), ("y", "x", "zl", "zh", "core")
    )
    nodes = ("y", "x", "zl", "zh", "core")
    placed = (
        P(nodes, None),
        P(nodes),
        P(nodes, None, None, None, None),
        P(nodes, None, None),
        P(nodes, None),
        P(),
        P(nodes, None),
    )

    return jax.shard_map(
        per_device,
        mesh=fine,
        in_specs=placed,
        out_specs=(P(nodes, None), P(), P(nodes, None)),
        check_vma=False,
    )
```

time: 152 us -> 141 us (0.928)
  starting transfers between devices: 51.4 us -> 39 us
  waiting for transfers between devices: 38.6 us -> 44.6 us
  Pallas kernels: 11.5 us -> 8.3 us
  matrix products: 9.99 us -> 8.15 us
  other arithmetic: 5.03 us -> 6.8 us
    all_to_all x4 -> x2, starting transfers between devices: 21.5 us -> 11.7 us  [copies_to(): lax.all_to_all(jnp.broadcast_to(block[None], (count,) + block.shape), axi...]
    all_to_all x2, waiting for transfers between devices: 19.1 us -> 25.5 us  [the longest x1 14.8 us: per_device(): lax.all_to_all(jnp.concatenate([returned, copies], axis=1), COL, 0, 0)]
    pallas_call x1, Pallas kernels: 11.5 us -> 8.3 us  [arrange(): pl.pallas_call(arrange_kernel, out_shape=(jax.ShapeDtypeStruct((cap * row...]
    all_to_all x1, waiting for transfers between devices: 1.16 us -> 4.36 us  [per_device(): window = lax.all_to_all(offer, COL, 0, 0).reshape(-1, width)]
    all_to_all x2, starting transfers between devices: 10.7 us -> 7.59 us  [the longest x1 4.03 us: per_device(): given = lax.all_to_all(offer, 'zh', 0, 0)]
    all_to_all x4 -> x2, waiting for transfers between devices: 14.8 us -> 11.8 us  [copies_to(): lax.all_to_all(jnp.broadcast_to(block[None], (count,) + block.shape), axi...]
    concatenate x0 -> x3, other arithmetic: none -> 1.93 us  [the longest x1 1.13 us: per_device(): jnp.concatenate([returned, copies], axis=1)]
  transfers between devices with their start and end apart: 11 -> 9, of which waited for: 10 -> 7; matrix products, arithmetic and copies ran while one was open for 4% -> 4% of each run, Pallas kernels for 8% -> 6%
where the time goes in v2:
time: 141 us; the launch traced here: 140 us
  waiting for transfers between devices  44.6 us (32%)
  starting transfers between devices  39 us (28%)
  blocking collectives  30.2 us (21%)
  Pallas kernels  8.3 us (6%)
  matrix products  8.15 us (6%)
  other arithmetic  6.8 us (5%)
  local copies, waits for them, and re-layouts  2.22 us (2%)
    all_to_all x1, blocking collectives, per_device(): shares = lax.all_to_all(half.reshape(N_ZH, own_rows, width), 'zh', 0, 0)  18.3 us
    all_to_all x1, waiting for transfers between devices, per_device(): lax.all_to_all(jnp.concatenate([returned, copies], axis=1), COL, 0, 0)  14.8 us
    ppermute x4, starting transfers between devices, shifted(): lax.ppermute(block, ROW, [((i - distance) % N_ROW, i) for i in range(N_RO...  13.9 us
    all_to_all x2, waiting for transfers between devices, copies_to(): lax.all_to_all(jnp.broadcast_to(block[None], (count,) + block.shape), axi...  11.8 us
    all_to_all x2, starting transfers between devices, copies_to(): lax.all_to_all(jnp.broadcast_to(block[None], (count,) + block.shape), axi...  11.7 us
    all_to_all x1, waiting for transfers between devices, per_device(): given = lax.all_to_all(offer, 'zh', 0, 0)  10.6 us
    pallas_call x1, Pallas kernels, arrange(): pl.pallas_call(arrange_kernel, out_shape=(jax.ShapeDtypeStruct((cap * row...  8.3 us
    all_to_all x1, blocking collectives, per_device(): halves = lax.all_to_all(partial.reshape(N_CORE, -1, width), 'core', 0, 0)  7.26 us
  transfers between devices with their start and end apart: 9, of which 7 were waited for; matrix products, arithmetic and copies ran while one was open for 4% of the time, Pallas kernels for 6%

profile of v2, /device:TPU:1, one launch (start us, length us, event | category | flops | bytes accessed | tf_op | source)
XLA Modules:
  0.0 140.1 jit_solution(16884422020471706341)
XLA Ops:
  0.6 0.0 copy-start
  0.6 0.7 convert_rsqrt_fusion
  1.3 0.9 multiply_convert_fusion.2
  2.3 5.0 %collective-permute-start.1 = (bf16[128,256]{1,0:T(8,128)(2,1)S(1)}, bf16[128,256]{1,0:T(8,128)(2,1)S(1)}, u32[]{:S(2)}, u32[]{:S(2)}) collective-permute-start(bf16[128,256]{1,0:T(8,128)(2,1)S(1)} %multiply_convert_fusion.2), channel_id=1, source_target_pairs={{384,0},{448,64},{0,128},{64,192},{128,256},{192,320},{256,384},{3... | collective-permute-start | bytes 196616 | tf_op jit(solution)/shard_map/ppermute | solution.py:75
  7.3 3.2 %collective-permute-start = (bf16[128,256]{1,0:T(8,128)(2,1)S(1)}, bf16[128,256]{1,0:T(8,128)(2,1)S(1)}, u32[]{:S(2)}, u32[]{:S(2)}) collective-permute-start(bf16[128,256]{1,0:T(8,128)(2,1)S(1)} %multiply_convert_fusion.2), channel_id=1, source_target_pairs={{448,0},{0,64},{64,128},{128,192},{192,256},{256,320},{320,384},{3... | collective-permute-start | bytes 196616 | tf_op jit(solution)/shard_map/ppermute | solution.py:75
  10.5 0.2 collective-permute-done.1
  10.7 0.1 broadcast_select_fusion.2
  10.8 0.0 copy-start.1
  10.8 2.7 %collective-permute-done = bf16[128,256]{1,0:T(8,128)(2,1)S(1)} collective-permute-done((bf16[128,256]{1,0:T(8,128)(2,1)S(1)}, bf16[128,256]{1,0:T(8,128)(2,1)S(1)}, u32[]{:S(2)}, u32[]{:S(2)}) %collective-permute-start) | collective-permute-done | bytes 65568 | tf_op jit(solution)/shard_map/ppermute | solution.py:75
  13.6 1.2 pad_maximum_fusion.1
  14.7 5.8 %all-to-all-start = ((bf16[8,2,128,256]{3,2,1,0:T(8,128)(2,1)}), bf16[8,2,128,256]{3,2,1,0:T(8,128)(2,1)S(1)}, u32[]{:S(2)}, u32[]{:S(2)}) async-start(bf16[8,2,128,256]{3,2,1,0:T(8,128)(2,1)} %pad_maximum_fusion.1), calls=%async_computation | async-start | bytes 2097152 | tf_op jit(solution)/shard_map/all_to_all | solution.py:101
  20.6 0.0 copy-done.1
  20.6 0.7 copy.10.rows_ref
  21.2 8.3 %arrange_tiles.1 = (bf16[1024,2048]{1,0:T(8,128)(2,1)}, bf16[2048,1024]{1,0:T(8,128)(2,1)}) custom-call(s32[1,16,8]{2,1,0:T(8,128)} %copy.10.rows_ref, s32[1,16]{1,0:T(1,128)} %counts_ref.1, s32[1]{0:T(128)} %bitcast.col_ref, bf16[1,16,8,128,128]{4,3,2,1,0:T(8,128)(2,1)} %tile_hbm.1), custom_call_target="tpu_custom_call" | custom-call | flops 2097152 | bytes 8388608 | tf_op jit(solution)/shard_map/arrange_tiles/pallas_call | solution.py:57
  29.5 4.4 %all-to-all-done = bf16[8,2,128,256]{3,2,1,0:T(8,128)(2,1)S(1)} async-done(((bf16[8,2,128,256]{3,2,1,0:T(8,128)(2,1)}), bf16[8,2,128,256]{3,2,1,0:T(8,128)(2,1)S(1)}, u32[]{:S(2)}, u32[]{:S(2)}) %all-to-all-start) | async-done | bytes 1048608 | tf_op jit(solution)/shard_map/all_to_all | solution.py:101
  33.9 3.5 %convolution_convert_fusion.1 = bf16[1024,256]{1,0:T(8,128)(2,1)S(1)} fusion(bf16[1024,2048]{1,0:T(8,128)(2,1)} %get-tuple-element.5, bf16[2048,256]{1,0:T(8,128)(2,1)S(1)} %bitcast.59), kind=kOutput, calls=%fused_computation.1 | convolution fusion | flops 1074003968 | bytes 5767168 | tf_op jit(solution)/shard_map/dot_general | solution.py:103
  37.4 0.0 copy-start.2
  37.4 7.3 %all_to_all.35 = bf16[2,512,256]{2,1,0:T(8,128)(2,1)S(1)} all-to-all(bf16[2,512,256]{2,1,0:T(8,128)(2,1)S(1)} %bitcast.63), channel_id=1, replica_groups=mesh['y'=8,'x'=4,'zl'=2,'zh'=4,'core'=2] {'core'}, dimensions={0} | all-to-all | bytes 1048576 | tf_op jit(solution)/shard_map/all_to_all | solution.py:105
  44.6 0.1 add_convert_fusion
  44.7 18.3 %all_to_all.36 = bf16[4,128,256]{2,1,0:T(8,128)(2,1)S(1)} all-to-all(bf16[4,128,256]{2,1,0:T(8,128)(2,1)S(1)} %bitcast.58), channel_id=1, replica_groups=mesh['y'=8,'x'=4,'zl'=2,'zh'=4,'core'=2] {'zh'}, dimensions={0} | all-to-all | bytes 524288 | tf_op jit(solution)/shard_map/all_to_all | solution.py:107
  63.0 0.1 fusion.4
  63.1 0.9 multiply_convert_fusion
  64.0 0.2 convolution_convert_fusion.2
  64.2 0.2 fusion
  64.4 0.8 pad_maximum_fusion.2
  65.2 4.0 %all-to-all-start.3 = ((bf16[4,192,256]{2,1,0:T(8,128)(2,1)}), bf16[4,192,256]{2,1,0:T(8,128)(2,1)S(1)}, u32[]{:S(2)}, u32[]{:S(2)}) async-start(bf16[4,192,256]{2,1,0:T(8,128)(2,1)} %pad_maximum_fusion.2), calls=%async_computation.3 | async-start | bytes 786432 | tf_op jit(solution)/shard_map/all_to_all | solution.py:124
  69.2 10.6 %all-to-all-done.3 = bf16[4,192,256]{2,1,0:T(8,128)(2,1)S(1)} async-done(((bf16[4,192,256]{2,1,0:T(8,128)(2,1)}), bf16[4,192,256]{2,1,0:T(8,128)(2,1)S(1)}, u32[]{:S(2)}, u32[]{:S(2)}) %all-to-all-start.3) | async-done | bytes 393248 | tf_op jit(solution)/shard_map/all_to_all | solution.py:124
  80.0 4.6 %all-gather = bf16[1152,256]{1,0:T(8,128)(2,1)S(1)} all-gather(bf16[576,256]{1,0:T(8,128)(2,1)S(1)} %pad_maximum_fusion.3), channel_id=2, replica_groups=mesh['y'=8,'x'=4,'zl'=2,'zh'=4,'core'=2] {'core'}, dimensions={0}, use_global_device_ids=true | all-gather | bytes 884736 | tf_op jit(solution)/shard_map/all_gather | solution.py:127
  84.6 0.7 broadcast_in_dim.83
  85.3 5.7 %all-to-all-start.4 = ((bf16[8,32,256]{2,1,0:T(8,128)(2,1)}), bf16[8,32,256]{2,1,0:T(8,128)(2,1)S(1)}, u32[]{:S(2)}, u32[]{:S(2)}) async-start(bf16[8,32,256]{2,1,0:T(8,128)(2,1)} %broadcast_in_dim.83), calls=%async_computation.4 | async-start | bytes 262144 | tf_op jit(solution)/shard_map/all_to_all | solution.py:79
  91.0 3.4 %convolution_convert_fusion = bf16[2048,256]{1,0:T(8,128)(2,1)S(1)} fusion(bf16[2048,1024]{1,0:T(8,128)(2,1)} %get-tuple-element.6, bf16[1024,256]{1,0:T(8,128)(2,1)S(1)} %bitcast.62), kind=kOutput, calls=%fused_computation | convolution fusion | flops 1074266112 | bytes 5767168 | tf_op jit(solution)/shard_map/dot_general | solution.py:137
  94.4 4.5 %all-to-all-done.4 = bf16[8,32,256]{2,1,0:T(8,128)(2,1)S(1)} async-done(((bf16[8,32,256]{2,1,0:T(8,128)(2,1)}), bf16[8,32,256]{2,1,0:T(8,128)(2,1)S(1)}, u32[]{:S(2)}, u32[]{:S(2)}) %all-to-all-start.4) | async-done | bytes 131104 | tf_op jit(solution)/shard_map/all_to_all | solution.py:79
  98.9 1.1 pad_maximum_fusion
  100.1 3.6 %all-to-all-start.5 = ((bf16[8,288,256]{2,1,0:T(8,128)(2,1)}), bf16[8,288,256]{2,1,0:T(8,128)(2,1)S(1)}, u32[]{:S(2)}, u32[]{:S(2)}) async-start(bf16[8,288,256]{2,1,0:T(8,128)(2,1)} %pad_maximum_fusion), calls=%async_computation.5 | async-start | bytes 2359296 | tf_op jit(solution)/shard_map/all_to_all | solution.py:140
  103.6 14.8 %all-to-all-done.5 = bf16[8,288,256]{2,1,0:T(8,128)(2,1)S(1)} async-done(((bf16[8,288,256]{2,1,0:T(8,128)(2,1)}), bf16[8,288,256]{2,1,0:T(8,128)(2,1)S(1)}, u32[]{:S(2)}, u32[]{:S(2)}) %all-to-all-start.5) | async-done | bytes 1179680 | tf_op jit(solution)/shard_map/all_to_all | solution.py:140
  118.5 0.1 slice.142
  118.6 0.1 fusion.5
  118.6 0.1 broadcast_select_fusion.1
  118.8 0.1 fusion.6
  118.9 3.7 %collective-permute-start.3 = (bf16[128,256]{1,0:T(8,128)(2,1)S(1)}, bf16[128,256]{1,0:T(8,128)(2,1)S(1)}, u32[]{:S(2)}, u32[]{:S(2)}) collective-permute-start(bf16[128,256]{1,0:T(8,128)(2,1)S(1)} %fusion.6), channel_id=1, source_target_pairs={{128,0},{192,64},{256,128},{320,192},{384,256},{448,320},{0,384},{... | collective-permute-start | bytes 196616 | tf_op jit(solution)/shard_map/ppermute | solution.py:75
  122.6 1.9 %collective-permute-start.2 = (bf16[128,256]{1,0:T(8,128)(2,1)S(1)}, bf16[128,256]{1,0:T(8,128)(2,1)S(1)}, u32[]{:S(2)}, u32[]{:S(2)}) collective-permute-start(bf16[128,256]{1,0:T(8,128)(2,1)S(1)} %fusion.5), channel_id=1, source_target_pairs={{64,0},{128,64},{192,128},{256,192},{320,256},{384,320},{448,384},... | collective-permute-start | bytes 196616 | tf_op jit(solution)/shard_map/ppermute | solution.py:75
  124.6 0.7 broadcast_in_dim.87
  125.2 6.0 %all-to-all-start.6 = ((bf16[8,32,256]{2,1,0:T(8,128)(2,1)}), bf16[8,32,256]{2,1,0:T(8,128)(2,1)S(1)}, u32[]{:S(2)}, u32[]{:S(2)}) async-start(bf16[8,32,256]{2,1,0:T(8,128)(2,1)} %broadcast_in_dim.87), calls=%async_computation.6 | async-start | bytes 262144 | tf_op jit(solution)/shard_map/all_to_all | solution.py:79
  131.2 0.0 collective-permute-done.3
  131.3 0.0 collective-permute-done.2
  131.3 0.7 fusion.3
  132.0 7.4 %all-to-all-done.6 = bf16[8,32,256]{2,1,0:T(8,128)(2,1)S(1)} async-done(((bf16[8,32,256]{2,1,0:T(8,128)(2,1)}), bf16[8,32,256]{2,1,0:T(8,128)(2,1)S(1)}, u32[]{:S(2)}, u32[]{:S(2)}) %all-to-all-start.6) | async-done | bytes 131104 | tf_op jit(solution)/shard_map/all_to_all | solution.py:79
  139.4 0.7 bitcast_convert_fusion
  (15 shorter events, 0.3 us)
Async XLA Ops:
  0.6 62.5 %copy-start = (bf16[256,256]{1,0:T(8,128)(2,1)S(1)}, bf16[256,256]{1,0:T(8,128)(2,1)}, u32[]{:S(2)}) copy-start(bf16[256,256]{1,0:T(8,128)(2,1)} %param.12) | copy-start | bytes 393220
  2.3 8.5 %collective-permute-start.1 = (bf16[128,256]{1,0:T(8,128)(2,1)S(1)}, bf16[128,256]{1,0:T(8,128)(2,1)S(1)}, u32[]{:S(2)}, u32[]{:S(2)}) collective-permute-start(bf16[128,256]{1,0:T(8,128)(2,1)S(1)} %multiply_convert_fusion.2), channel_id=1, source_target_pairs={{384,0},{448,64},{0,128},{64,192},{128,256},{192,320},{256,384},{3... | collective-permute-start | bytes 196616 | tf_op jit(solution)/shard_map/ppermute | solution.py:75
  7.3 6.2 %collective-permute-start = (bf16[128,256]{1,0:T(8,128)(2,1)S(1)}, bf16[128,256]{1,0:T(8,128)(2,1)S(1)}, u32[]{:S(2)}, u32[]{:S(2)}) collective-permute-start(bf16[128,256]{1,0:T(8,128)(2,1)S(1)} %multiply_convert_fusion.2), channel_id=1, source_target_pairs={{448,0},{0,64},{64,128},{128,192},{192,256},{256,320},{320,384},{3... | collective-permute-start | bytes 196616 | tf_op jit(solution)/shard_map/ppermute | solution.py:75
  10.8 9.7 %copy-start.1 = (s32[1,16,8]{1,2,0:T(8,128)S(1)}, s32[1,16,8]{1,2,0:T(8,128)}, u32[]{:S(2)}) copy-start(s32[1,16,8]{1,2,0:T(8,128)} %param.10) | copy-start | bytes 1540
  14.7 19.2 %all-to-all-start = ((bf16[8,2,128,256]{3,2,1,0:T(8,128)(2,1)}), bf16[8,2,128,256]{3,2,1,0:T(8,128)(2,1)S(1)}, u32[]{:S(2)}, u32[]{:S(2)}) async-start(bf16[8,2,128,256]{3,2,1,0:T(8,128)(2,1)} %pad_maximum_fusion.1), calls=%async_computation | async-start | bytes 2097152 | tf_op jit(solution)/shard_map/all_to_all | solution.py:101
  37.4 25.7 %copy-start.2 = (bf16[128,256]{1,0:T(8,128)(2,1)S(1)}, bf16[128,256]{1,0:T(8,128)(2,1)}, u32[]{:S(2)}) copy-start(bf16[128,256]{1,0:T(8,128)(2,1)} %param.13) | copy-start | bytes 196612
  65.2 14.7 %all-to-all-start.3 = ((bf16[4,192,256]{2,1,0:T(8,128)(2,1)}), bf16[4,192,256]{2,1,0:T(8,128)(2,1)S(1)}, u32[]{:S(2)}, u32[]{:S(2)}) async-start(bf16[4,192,256]{2,1,0:T(8,128)(2,1)} %pad_maximum_fusion.2), calls=%async_computation.3 | async-start | bytes 786432 | tf_op jit(solution)/shard_map/all_to_all | solution.py:124
  85.3 13.6 %all-to-all-start.4 = ((bf16[8,32,256]{2,1,0:T(8,128)(2,1)}), bf16[8,32,256]{2,1,0:T(8,128)(2,1)S(1)}, u32[]{:S(2)}, u32[]{:S(2)}) async-start(bf16[8,32,256]{2,1,0:T(8,128)(2,1)} %broadcast_in_dim.83), calls=%async_computation.4 | async-start | bytes 262144 | tf_op jit(solution)/shard_map/all_to_all | solution.py:79
  100.1 18.4 %all-to-all-start.5 = ((bf16[8,288,256]{2,1,0:T(8,128)(2,1)}), bf16[8,288,256]{2,1,0:T(8,128)(2,1)S(1)}, u32[]{:S(2)}, u32[]{:S(2)}) async-start(bf16[8,288,256]{2,1,0:T(8,128)(2,1)} %pad_maximum_fusion), calls=%async_computation.5 | async-start | bytes 2359296 | tf_op jit(solution)/shard_map/all_to_all | solution.py:140
  118.9 12.4 %collective-permute-start.3 = (bf16[128,256]{1,0:T(8,128)(2,1)S(1)}, bf16[128,256]{1,0:T(8,128)(2,1)S(1)}, u32[]{:S(2)}, u32[]{:S(2)}) collective-permute-start(bf16[128,256]{1,0:T(8,128)(2,1)S(1)} %fusion.6), channel_id=1, source_target_pairs={{128,0},{192,64},{256,128},{320,192},{384,256},{448,320},{0,384},{... | collective-permute-start | bytes 196616 | tf_op jit(solution)/shard_map/ppermute | solution.py:75
  122.6 8.7 %collective-permute-start.2 = (bf16[128,256]{1,0:T(8,128)(2,1)S(1)}, bf16[128,256]{1,0:T(8,128)(2,1)S(1)}, u32[]{:S(2)}, u32[]{:S(2)}) collective-permute-start(bf16[128,256]{1,0:T(8,128)(2,1)S(1)} %fusion.5), channel_id=1, source_target_pairs={{64,0},{128,64},{192,128},{256,192},{320,256},{384,320},{448,384},... | collective-permute-start | bytes 196616 | tf_op jit(solution)/shard_map/ppermute | solution.py:75
  125.2 14.1 %all-to-all-start.6 = ((bf16[8,32,256]{2,1,0:T(8,128)(2,1)}), bf16[8,32,256]{2,1,0:T(8,128)(2,1)S(1)}, u32[]{:S(2)}, u32[]{:S(2)}) async-start(bf16[8,32,256]{2,1,0:T(8,128)(2,1)} %broadcast_in_dim.87), calls=%async_computation.6 | async-start | bytes 262144 | tf_op jit(solution)/shard_map/all_to_all | solution.py:79

commit v3 on v2

--- a/solution.py
+++ b/solution.py
@@ -13,9 +13,10 @@
 ROW, COL, REP = "y", ("x", "zl"), ("zh", "core")
 N_ROW, N_COL, N_ZH, N_CORE = 8, 8, 4, 2
 N_REP = N_ZH * N_CORE
+DEGREE_ROWS = 16
 
 
-def arrange_kernel(rows_ref, counts_ref, col_ref, tile_hbm, out_ref, flip_ref, tiles, arrived):
+def arrange_kernel(rows_ref, counts_ref, here_ref, tile_hbm, out_ref, flip_ref, tiles, arrived):
     _, span, cap, block, _ = tile_hbm.shape
 
     def fetch(distance):
@@ -25,7 +26,7 @@
 
     for distance in range(span):
         fetch(distance).start()
-    col = col_ref[0]
+    col, core = here_ref[0], here_ref[1]
 
     def place_distance(distance, carry):
         fetch(distance).wait()
@@ -38,18 +39,20 @@
         at_col = pl.ds(pl.multiple_of((source * 2 + slot) * block, block), block)
         for k in range(cap):
             owner = rows_ref[0, distance, k]
-            row = lax.rem(owner, N_CORE) * N_ZH + lax.div(owner, N_CORE)
-            at_row = pl.ds(pl.multiple_of(row * block, block), block)
+            owner_core, owner_zh = lax.rem(owner, N_CORE), lax.div(owner, N_CORE)
+            far = jnp.where(owner_core == core, 0, N_ZH)
+            at_row = pl.ds(pl.multiple_of((far + owner_zh) * block, block), block)
+            at_flip = pl.ds(pl.multiple_of((owner_core * N_ZH + owner_zh) * block, block), block)
             tile = tiles[distance, k]
             tile = jnp.where(k < live_count, tile, jnp.zeros_like(tile))
             out_ref[at_row, at_col] = tile
-            flip_ref[at_col, at_row] = tile.T
+            flip_ref[at_col, at_flip] = tile.T
         return carry
 
     lax.fori_loop(0, span, place_distance, 0)
 
 
-def arrange(tile_values, tile_rows, tile_counts, col):
+def arrange(tile_values, tile_rows, tile_counts, here):
     _, span, cap, rows, cols = tile_values.shape
     size = span * cap * rows * cols
     whole = pl.BlockSpec(memory_space=pltpu.VMEM)
@@ -68,7 +71,7 @@
         ],
         cost_estimate=pl.CostEstimate(flops=size, bytes_accessed=4 * size, transcendentals=0),
         name="arrange_tiles",
-    )(tile_rows, tile_counts, col, tile_values)
+    )(tile_rows, tile_counts, here, tile_values)
 
 
 def shifted(block, distance):
@@ -88,49 +91,47 @@
 
 def per_device(features, degrees, tile_values, tile_rows, tile_counts, weight, cotangent):
     own_rows, width = features.shape
-    col = lax.axis_index(COL)
+    col, core, zh = lax.axis_index(COL), lax.axis_index("core"), lax.axis_index("zh")
     columns = jnp.arange(N_COL, dtype=jnp.int32)[:, None, None]
     inv_root = lax.rsqrt(degrees.astype(F32))[:, None]
     scaled = (features.astype(F32) * inv_root).astype(BF)
 
     one_back = shifted(scaled, 1)
     two_back = shifted(scaled, 2)
-    adjacency, flipped = arrange(tile_values, tile_rows, tile_counts, col[None])
+    adjacency, flipped = arrange(
+        tile_values, tile_rows, tile_counts, jnp.stack([col, core])
+    )
     own_or_two = jnp.where(columns >= col, scaled[None], two_back[None])
     offer = jnp.stack([jnp.broadcast_to(one_back[None], own_or_two.shape), own_or_two], axis=1)
     window = lax.all_to_all(offer, COL, 0, 0).reshape(-1, width)
 
-    partial = jnp.dot(adjacency, window, preferred_element_type=F32).astype(BF)
-    core = lax.axis_index("core")
-    halves = lax.all_to_all(partial.reshape(N_CORE, -1, width), "core", 0, 0)
-    half = summed_in_f32(halves).astype(BF)
-    shares = lax.all_to_all(half.reshape(N_ZH, own_rows, width), "zh", 0, 0)
-    own_sum = summed_in_f32(shares)
+    partial = jnp.dot(adjacency, window, preferred_element_type=F32)
+    kept, sent = jnp.split(partial, 2, axis=0)
+    other = lax.ppermute(sent.astype(BF), "core", [(0, 1), (1, 0)])
+    half = (kept + other.astype(F32)).astype(BF)
+    degree_rows = jnp.zeros((DEGREE_ROWS, width), BF).at[0, :own_rows].set(degrees.astype(BF))
+    told = copies_to(jnp.concatenate([half, cotangent, degree_rows], axis=0), "zh", N_ZH)
+    zh_rows = N_ZH * own_rows
+    zh_sum = summed_in_f32(told[:, :zh_rows])
+    zh_cotangent = told[:, zh_rows : zh_rows + own_rows].reshape(zh_rows, width)
+    zh_degrees = told[:, zh_rows + own_rows, :own_rows].reshape(zh_rows)
+    zh_inv_root = lax.rsqrt(zh_degrees.astype(F32))[:, None]
 
-    aggregated = (own_sum * inv_root).astype(BF)
+    aggregated = (zh_sum * zh_inv_root).astype(BF)
     pre_act = jnp.dot(aggregated, weight, preferred_element_type=F32)
     sigma = jax.nn.sigmoid(pre_act)
-    activations = (pre_act * sigma).astype(BF)
-    act_grad = (cotangent.astype(F32) * sigma * (1.0 + pre_act * (1.0 - sigma))).astype(BF)
+    activations = lax.dynamic_slice_in_dim((pre_act * sigma).astype(BF), zh * own_rows, own_rows)
+    act_grad = (zh_cotangent.astype(F32) * sigma * (1.0 + pre_act * (1.0 - sigma))).astype(BF)
+    zh_weight = lax.dot_general(
+        aggregated, act_grad, (((0,), (0,)), ((), ())), preferred_element_type=F32
+    )
     back_grad = lax.dot_general(
         act_grad, weight, (((1,), (1,)), ((), ())), preferred_element_type=F32
     )
-    back_scaled = (back_grad * inv_root).astype(BF)
-    local_weight = lax.dot_general(
-        aggregated, act_grad, (((0,), (0,)), ((), ())), preferred_element_type=F32
-    ).astype(BF)
-    copies = jnp.broadcast_to(back_scaled[None], (N_ZH,) + back_scaled.shape)
-    offer = jnp.concatenate([copies, local_weight.reshape(N_ZH, -1, width)], axis=1)
-    given = lax.all_to_all(offer, "zh", 0, 0)
-    along_zh = given[:, :own_rows].reshape(-1, width)
-    weight_part = summed_in_f32(given[:, own_rows:]).astype(BF)
-    pair = lax.all_gather(
-        jnp.concatenate([along_zh, weight_part], axis=0), "core", axis=0, tiled=False
-    )
-    gathered = along_zh.shape[0]
-    slab_grads = pair[:, :gathered].reshape(-1, width)
-    weight_pair = pair[:, gathered:].reshape(N_CORE, N_CORE, -1, width)
-    weight_rows = summed_in_f32(lax.dynamic_index_in_dim(weight_pair, core, 1, keepdims=False))
+    back_scaled = (back_grad * zh_inv_root).astype(BF)
+    slab_grads = lax.all_gather(back_scaled, "core", axis=0, tiled=True)
+    share = width // N_ZH
+    weight_rows = lax.dynamic_slice_in_dim(zh_weight, zh * share, share)
 
     along_y = copies_to(weight_rows.astype(BF), ROW, N_ROW)
     weight_rows = summed_in_f32(along_y).astype(BF)
@@ -141,7 +142,8 @@
     node_total = own_rows * N_ROW * N_COL * N_REP
     weight_rows = (summed_in_f32(home[:, 2 * own_rows :]) / math.sqrt(node_total)).astype(BF)
     along_rep = copies_to(weight_rows, REP, N_REP)
-    grad_weight = along_rep.reshape(-1, width).astype(F32)
+    along_rep = along_rep.reshape(N_ZH, N_CORE, share, width).astype(F32)
+    grad_weight = (along_rep[:, 0] + along_rep[:, 1]).reshape(-1, width)
 
     arrived = home[:, : 2 * own_rows].reshape(N_COL, 2, own_rows, width)
     for_one = summed_in_f32(arrived[:, 0]).astype(BF)

time: 141 us -> 150 us (1.064)
  blocking collectives: 30.2 us -> 6.5 us
  starting transfers between devices: 39 us -> 54.2 us
  waiting for transfers between devices: 44.6 us -> 58.8 us
  other arithmetic: 6.8 us -> 8.4 us
    all_to_all x2 -> x0, blocking collectives: 25.6 us -> none  [the longest x1 18.3 us: per_device(): shares = lax.all_to_all(half.reshape(N_ZH, own_rows, width), 'zh', 0, 0)]
    all_to_all x2 -> x3, waiting for transfers between devices: 11.8 us -> 35.1 us  [copies_to(): lax.all_to_all(jnp.broadcast_to(block[None], (count,) + block.shape), axi...]
    all_to_all x1 -> x0, waiting for transfers between devices: 10.6 us -> none  [per_device(): given = lax.all_to_all(offer, 'zh', 0, 0)]
    all_to_all x2 -> x3, starting transfers between devices: 11.7 us -> 21 us  [copies_to(): lax.all_to_all(jnp.broadcast_to(block[None], (count,) + block.shape), axi...]
    ppermute x0 -> x1, starting transfers between devices: none -> 5.26 us  [per_device(): other = lax.ppermute(sent.astype(BF), 'core', [(0, 1), (1, 0)])]
    all_to_all x1 -> x0, starting transfers between devices: 4.03 us -> none  [per_device(): given = lax.all_to_all(offer, 'zh', 0, 0)]
    ppermute x4, starting transfers between devices: 13.9 us -> 16.9 us  [shifted(): lax.ppermute(block, ROW, [((i - distance) % N_ROW, i) for i in range(N_RO...]
    all_gather x1, blocking collectives: 4.6 us -> 6.5 us  [per_device(): slab_grads = lax.all_gather(back_scaled, 'core', axis=0, tiled=True)]
  transfers between devices with their start and end apart: 9 -> 10, of which waited for: 7 -> 8; matrix products, arithmetic and copies ran while one was open for 4% -> 5% of each run, Pallas kernels for 6% -> 6%
where the time goes in v3:
time: 150 us
  waiting for transfers between devices  58.8 us (39%)
  starting transfers between devices  54.2 us (36%)
  matrix products  8.73 us (6%)
  Pallas kernels  8.6 us (6%)
  other arithmetic  8.4 us (6%)
  blocking collectives  6.5 us (4%)
  local copies, waits for them, and re-layouts  3.51 us (2%)
    all_to_all x3, waiting for transfers between devices, copies_to(): lax.all_to_all(jnp.broadcast_to(block[None], (count,) + block.shape), axi...  35.1 us
    all_to_all x3, starting transfers between devices, copies_to(): lax.all_to_all(jnp.broadcast_to(block[None], (count,) + block.shape), axi...  21 us
    ppermute x4, starting transfers between devices, shifted(): lax.ppermute(block, ROW, [((i - distance) % N_ROW, i) for i in range(N_RO...  16.9 us
    all_to_all x1, waiting for transfers between devices, per_device(): lax.all_to_all(jnp.concatenate([returned, copies], axis=1), COL, 0, 0)  15.1 us
    pallas_call x1, Pallas kernels, arrange(): pl.pallas_call(arrange_kernel, out_shape=(jax.ShapeDtypeStruct((cap * row...  8.6 us
    all_gather x1, blocking collectives, per_device(): slab_grads = lax.all_gather(back_scaled, 'core', axis=0, tiled=True)  6.5 us
    all_to_all x1, starting transfers between devices, per_device(): window = lax.all_to_all(offer, COL, 0, 0).reshape(-1, width)  5.83 us
    ppermute x1, starting transfers between devices, per_device(): other = lax.ppermute(sent.astype(BF), 'core', [(0, 1), (1, 0)])  5.26 us
  transfers between devices with their start and end apart: 10, of which 8 were waited for; matrix products, arithmetic and copies ran while one was open for 5% of the time, Pallas kernels for 6%

profile of v3, /device:TPU:1, one launch (start us, length us, event | category | flops | bytes accessed | tf_op | source)
XLA Modules:
  0.0 149.6 jit_solution(16474557822176181951)
XLA Ops:
  0.6 0.0 copy-start
  0.6 0.7 convert_rsqrt_fusion
  1.3 0.9 multiply_convert_fusion
  2.3 5.0 %collective-permute-start.1 = (bf16[128,256]{1,0:T(8,128)(2,1)S(1)}, bf16[128,256]{1,0:T(8,128)(2,1)S(1)}, u32[]{:S(2)}, u32[]{:S(2)}) collective-permute-start(bf16[128,256]{1,0:T(8,128)(2,1)S(1)} %multiply_convert_fusion), channel_id=1, source_target_pairs={{384,0},{448,64},{0,128},{64,192},{128,256},{192,320},{256,384},{3... | collective-permute-start | bytes 196616 | tf_op jit(solution)/shard_map/ppermute | solution.py:78
  7.3 3.2 %collective-permute-start = (bf16[128,256]{1,0:T(8,128)(2,1)S(1)}, bf16[128,256]{1,0:T(8,128)(2,1)S(1)}, u32[]{:S(2)}, u32[]{:S(2)}) collective-permute-start(bf16[128,256]{1,0:T(8,128)(2,1)S(1)} %multiply_convert_fusion), channel_id=1, source_target_pairs={{448,0},{0,64},{64,128},{128,192},{192,256},{256,320},{320,384},{3... | collective-permute-start | bytes 196616 | tf_op jit(solution)/shard_map/ppermute | solution.py:78
  10.6 0.0 copy-start.2
  10.6 0.2 collective-permute-done.1
  10.7 0.1 broadcast_select_fusion.2
  10.8 2.7 %collective-permute-done = bf16[128,256]{1,0:T(8,128)(2,1)S(1)} collective-permute-done((bf16[128,256]{1,0:T(8,128)(2,1)S(1)}, bf16[128,256]{1,0:T(8,128)(2,1)S(1)}, u32[]{:S(2)}, u32[]{:S(2)}) %collective-permute-start) | collective-permute-done | bytes 65568 | tf_op jit(solution)/shard_map/ppermute | solution.py:78
  13.6 1.2 pad_maximum_fusion.1
  14.7 5.8 %all-to-all-start = ((bf16[8,2,128,256]{3,2,1,0:T(8,128)(2,1)}), bf16[8,2,128,256]{3,2,1,0:T(8,128)(2,1)S(1)}, u32[]{:S(2)}, u32[]{:S(2)}) async-start(bf16[8,2,128,256]{3,2,1,0:T(8,128)(2,1)} %pad_maximum_fusion.1), calls=%async_computation | async-start | bytes 2097152 | tf_op jit(solution)/shard_map/all_to_all | solution.py:106
  20.6 0.7 copy.11.rows_ref
  21.2 0.6 pad_add_fusion.here_ref
  21.8 8.6 %arrange_tiles.1 = (bf16[1024,2048]{1,0:T(8,128)(2,1)}, bf16[2048,1024]{1,0:T(8,128)(2,1)}) custom-call(s32[1,16,8]{2,1,0:T(8,128)} %copy.11.rows_ref, s32[1,16]{1,0:T(1,128)} %counts_ref.1, s32[2]{0:T(128)} %pad_add_fusion.here_ref, bf16[1,16,8,128,128]{4,3,2,1,0:T(8,128)(2,1)} %tile_hbm.1), custom_call_target="tpu_custom_call" | custom-call | flops 2097152 | bytes 8388608 | tf_op jit(solution)/shard_map/arrange_tiles/pallas_call | solution.py:60
  30.4 3.5 %all-to-all-done = bf16[8,2,128,256]{3,2,1,0:T(8,128)(2,1)S(1)} async-done(((bf16[8,2,128,256]{3,2,1,0:T(8,128)(2,1)}), bf16[8,2,128,256]{3,2,1,0:T(8,128)(2,1)S(1)}, u32[]{:S(2)}, u32[]{:S(2)}) %all-to-all-start) | async-done | bytes 1048608 | tf_op jit(solution)/shard_map/all_to_all | solution.py:106
  33.9 3.5 %fusion.16 = f32[1024,256]{1,0:T(8,128)S(1)} fusion(bf16[1024,2048]{1,0:T(8,128)(2,1)} %get-tuple-element.17, bf16[2048,256]{1,0:T(8,128)(2,1)S(1)} %bitcast.53), kind=kOutput, calls=%fused_computation.45 | convolution fusion | flops 1073741824 | bytes 6291456 | tf_op jit(solution)/shard_map/dot_general | solution.py:108
  37.4 5.3 %collective-permute-start.2 = (bf16[512,256]{1,0:T(8,128)(2,1)S(1)}, bf16[512,256]{1,0:T(8,128)(2,1)S(1)}, u32[]{:S(2)}, u32[]{:S(2)}) collective-permute-start(bf16[512,256]{1,0:T(8,128)(2,1)S(1)} %split.15), channel_id=1, source_target_pairs={{0,1},{1,0},{2,3},{3,2},{4,5},{5,4},{6,7},{7,6},{8,9},{9,8},{10,11... | collective-permute-start | bytes 786440 | tf_op jit(solution)/shard_map/ppermute | solution.py:110
  42.7 1.1 collective-permute-done.2
  43.9 0.1 fusion.2
  44.0 1.2 broadcast_in_dim.80
  45.2 9.1 %all-to-all-start.1 = ((bf16[4,656,256]{2,1,0:T(8,128)(2,1)}), bf16[4,656,256]{2,1,0:T(8,128)(2,1)S(1)}, u32[]{:S(2)}, u32[]{:S(2)}) async-start(bf16[4,656,256]{2,1,0:T(8,128)(2,1)} %broadcast_in_dim.80), calls=%async_computation.1 | async-start | bytes 2686976 | tf_op jit(solution)/shard_map/all_to_all | solution.py:82
  54.3 31.4 %all-to-all-done.1 = bf16[4,656,256]{2,1,0:T(8,128)(2,1)S(1)} async-done(((bf16[4,656,256]{2,1,0:T(8,128)(2,1)}), bf16[4,656,256]{2,1,0:T(8,128)(2,1)S(1)}, u32[]{:S(2)}, u32[]{:S(2)}) %all-to-all-start.1) | async-done | bytes 1343520 | tf_op jit(solution)/shard_map/all_to_all | solution.py:82
  85.7 0.2 fusion.5
  85.9 1.3 fusion.4
  87.1 0.3 fusion
  87.4 0.3 fusion.17
  87.7 0.7 broadcast_in_dim.81
  88.4 5.3 %all-to-all-start.2 = ((bf16[8,64,256]{2,1,0:T(8,128)(2,1)}), bf16[8,64,256]{2,1,0:T(8,128)(2,1)S(1)}, u32[]{:S(2)}, u32[]{:S(2)}) async-start(bf16[8,64,256]{2,1,0:T(8,128)(2,1)} %broadcast_in_dim.81), calls=%async_computation.2 | async-start | bytes 524288 | tf_op jit(solution)/shard_map/all_to_all | solution.py:82
  93.7 6.5 %all_gather.3 = bf16[1024,256]{1,0:T(8,128)(2,1)S(1)} all-gather(bf16[512,256]{1,0:T(8,128)(2,1)S(1)} %fusion), channel_id=1, replica_groups=mesh['y'=8,'x'=4,'zl'=2,'zh'=4,'core'=2] {'core'}, dimensions={0}, use_global_device_ids=true | all-gather | bytes 786432 | tf_op jit(solution)/shard_map/all_gather | solution.py:132
  100.2 3.4 %convolution_convert_fusion = bf16[2048,256]{1,0:T(8,128)(2,1)S(1)} fusion(bf16[2048,1024]{1,0:T(8,128)(2,1)} %get-tuple-element.18, bf16[1024,256]{1,0:T(8,128)(2,1)S(1)} %all_gather.3), kind=kOutput, calls=%fused_computation | convolution fusion | flops 1074266112 | bytes 5767168 | tf_op jit(solution)/shard_map/dot_general | solution.py:138
  103.7 0.0 all-to-all-done.2
  103.8 1.2 pad_maximum_fusion
  104.9 5.1 %all-to-all-start.3 = ((bf16[8,320,256]{2,1,0:T(8,128)(2,1)}), bf16[8,320,256]{2,1,0:T(8,128)(2,1)S(1)}, u32[]{:S(2)}, u32[]{:S(2)}) async-start(bf16[8,320,256]{2,1,0:T(8,128)(2,1)} %pad_maximum_fusion), calls=%async_computation.3 | async-start | bytes 2621440 | tf_op jit(solution)/shard_map/all_to_all | solution.py:141
  110.1 15.1 %all-to-all-done.3 = bf16[8,320,256]{2,1,0:T(8,128)(2,1)S(1)} async-done(((bf16[8,320,256]{2,1,0:T(8,128)(2,1)}), bf16[8,320,256]{2,1,0:T(8,128)(2,1)S(1)}, u32[]{:S(2)}, u32[]{:S(2)}) %all-to-all-start.3) | async-done | bytes 1310752 | tf_op jit(solution)/shard_map/all_to_all | solution.py:141
  125.2 0.1 slice.134
  125.2 0.1 broadcast_select_fusion.1
  125.4 0.1 fusion.12
  125.5 6.0 %collective-permute-start.4 = (bf16[128,256]{1,0:T(8,128)(2,1)S(1)}, bf16[128,256]{1,0:T(8,128)(2,1)S(1)}, u32[]{:S(2)}, u32[]{:S(2)}) collective-permute-start(bf16[128,256]{1,0:T(8,128)(2,1)S(1)} %fusion.12), channel_id=1, source_target_pairs={{128,0},{192,64},{256,128},{320,192},{384,256},{448,320},{0,384},{... | collective-permute-start | bytes 196616 | tf_op jit(solution)/shard_map/ppermute | solution.py:78
  131.5 0.7 broadcast_in_dim.85
  132.2 6.6 %all-to-all-start.4 = ((bf16[8,64,256]{2,1,0:T(8,128)(2,1)}), bf16[8,64,256]{2,1,0:T(8,128)(2,1)S(1)}, u32[]{:S(2)}, u32[]{:S(2)}) async-start(bf16[8,64,256]{2,1,0:T(8,128)(2,1)} %broadcast_in_dim.85), calls=%async_computation.4 | async-start | bytes 524288 | tf_op jit(solution)/shard_map/all_to_all | solution.py:82
  138.8 0.1 fusion.11
  138.8 2.7 %collective-permute-start.3 = (bf16[128,256]{1,0:T(8,128)(2,1)S(1)}, bf16[128,256]{1,0:T(8,128)(2,1)S(1)}, u32[]{:S(2)}, u32[]{:S(2)}) collective-permute-start(bf16[128,256]{1,0:T(8,128)(2,1)S(1)} %fusion.11), channel_id=1, source_target_pairs={{64,0},{128,64},{192,128},{256,192},{320,256},{384,320},{448,384},... | collective-permute-start | bytes 196616 | tf_op jit(solution)/shard_map/ppermute | solution.py:78
  141.6 1.6 %fusion.7 = bf16[128,256]{1,0:T(8,128)(2,1)} fusion(f32[512,256]{1,0:T(8,128)} %get-tuple-element.22, s32[]{:T(128)S(6)} %select_n.25, f32[512,256]{1,0:T(8,128)} %get-tuple-element.23), kind=kLoop, calls=%fused_computation.23 | loop fusion | flops 65536 | bytes 327684 | tf_op jit(solution)/shard_map/convert_element_type | solution.py:123
  143.2 0.0 collective-permute-done.4
  143.2 1.2 collective-permute-done.3
  144.4 0.7 fusion.10
  145.1 3.7 %all-to-all-done.4 = bf16[8,64,256]{2,1,0:T(8,128)(2,1)S(1)} async-done(((bf16[8,64,256]{2,1,0:T(8,128)(2,1)}), bf16[8,64,256]{2,1,0:T(8,128)(2,1)S(1)}, u32[]{:S(2)}, u32[]{:S(2)}) %all-to-all-start.4) | async-done | bytes 262176 | tf_op jit(solution)/shard_map/all_to_all | solution.py:82
  148.8 0.7 slice_add_fusion.1
  (19 shorter events, 0.3 us)
Async XLA Ops:
  0.6 85.2 %copy-start = (bf16[256,256]{1,0:T(8,128)(2,1)S(1)}, bf16[256,256]{1,0:T(8,128)(2,1)}, u32[]{:S(2)}) copy-start(bf16[256,256]{1,0:T(8,128)(2,1)} %param.14) | copy-start | bytes 393220
  2.3 8.5 %collective-permute-start.1 = (bf16[128,256]{1,0:T(8,128)(2,1)S(1)}, bf16[128,256]{1,0:T(8,128)(2,1)S(1)}, u32[]{:S(2)}, u32[]{:S(2)}) collective-permute-start(bf16[128,256]{1,0:T(8,128)(2,1)S(1)} %multiply_convert_fusion), channel_id=1, source_target_pairs={{384,0},{448,64},{0,128},{64,192},{128,256},{192,320},{256,384},{3... | collective-permute-start | bytes 196616 | tf_op jit(solution)/shard_map/ppermute | solution.py:78
  7.3 6.2 %collective-permute-start = (bf16[128,256]{1,0:T(8,128)(2,1)S(1)}, bf16[128,256]{1,0:T(8,128)(2,1)S(1)}, u32[]{:S(2)}, u32[]{:S(2)}) collective-permute-start(bf16[128,256]{1,0:T(8,128)(2,1)S(1)} %multiply_convert_fusion), channel_id=1, source_target_pairs={{448,0},{0,64},{64,128},{128,192},{192,256},{256,320},{320,384},{3... | collective-permute-start | bytes 196616 | tf_op jit(solution)/shard_map/ppermute | solution.py:78
  10.6 10.0 %copy-start.2 = (s32[1,16,8]{1,2,0:T(8,128)S(1)}, s32[1,16,8]{1,2,0:T(8,128)}, u32[]{:S(2)}) copy-start(s32[1,16,8]{1,2,0:T(8,128)} %param.12) | copy-start | bytes 1540
  14.7 19.2 %all-to-all-start = ((bf16[8,2,128,256]{3,2,1,0:T(8,128)(2,1)}), bf16[8,2,128,256]{3,2,1,0:T(8,128)(2,1)S(1)}, u32[]{:S(2)}, u32[]{:S(2)}) async-start(bf16[8,2,128,256]{3,2,1,0:T(8,128)(2,1)} %pad_maximum_fusion.1), calls=%async_computation | async-start | bytes 2097152 | tf_op jit(solution)/shard_map/all_to_all | solution.py:106
  33.9 8.8 %copy-start.3 = (s32[128]{0:T(128)S(1)}, s32[128]{0:T(128)}, u32[]{:S(2)}) copy-start(s32[128]{0:T(128)} %param.10) | copy-start | bytes 1540
  33.9 10.0 %copy-start.1 = (bf16[128,256]{1,0:T(8,128)(2,1)S(1)}, bf16[128,256]{1,0:T(8,128)(2,1)}, u32[]{:S(2)}) copy-start(bf16[128,256]{1,0:T(8,128)(2,1)} %param.15) | copy-start | bytes 196612
  37.4 6.4 %collective-permute-start.2 = (bf16[512,256]{1,0:T(8,128)(2,1)S(1)}, bf16[512,256]{1,0:T(8,128)(2,1)S(1)}, u32[]{:S(2)}, u32[]{:S(2)}) collective-permute-start(bf16[512,256]{1,0:T(8,128)(2,1)S(1)} %split.15), channel_id=1, source_target_pairs={{0,1},{1,0},{2,3},{3,2},{4,5},{5,4},{6,7},{7,6},{8,9},{9,8},{10,11... | collective-permute-start | bytes 786440 | tf_op jit(solution)/shard_map/ppermute | solution.py:110
  45.2 40.5 %all-to-all-start.1 = ((bf16[4,656,256]{2,1,0:T(8,128)(2,1)}), bf16[4,656,256]{2,1,0:T(8,128)(2,1)S(1)}, u32[]{:S(2)}, u32[]{:S(2)}) async-start(bf16[4,656,256]{2,1,0:T(8,128)(2,1)} %broadcast_in_dim.80), calls=%async_computation.1 | async-start | bytes 2686976 | tf_op jit(solution)/shard_map/all_to_all | solution.py:82
  88.4 15.3 %all-to-all-start.2 = ((bf16[8,64,256]{2,1,0:T(8,128)(2,1)}), bf16[8,64,256]{2,1,0:T(8,128)(2,1)S(1)}, u32[]{:S(2)}, u32[]{:S(2)}) async-start(bf16[8,64,256]{2,1,0:T(8,128)(2,1)} %broadcast_in_dim.81), calls=%async_computation.2 | async-start | bytes 524288 | tf_op jit(solution)/shard_map/all_to_all | solution.py:82
  104.9 20.2 %all-to-all-start.3 = ((bf16[8,320,256]{2,1,0:T(8,128)(2,1)}), bf16[8,320,256]{2,1,0:T(8,128)(2,1)S(1)}, u32[]{:S(2)}, u32[]{:S(2)}) async-start(bf16[8,320,256]{2,1,0:T(8,128)(2,1)} %pad_maximum_fusion), calls=%async_computation.3 | async-start | bytes 2621440 | tf_op jit(solution)/shard_map/all_to_all | solution.py:141
  125.5 17.7 %collective-permute-start.4 = (bf16[128,256]{1,0:T(8,128)(2,1)S(1)}, bf16[128,256]{1,0:T(8,128)(2,1)S(1)}, u32[]{:S(2)}, u32[]{:S(2)}) collective-permute-start(bf16[128,256]{1,0:T(8,128)(2,1)S(1)} %fusion.12), channel_id=1, source_target_pairs={{128,0},{192,64},{256,128},{320,192},{384,256},{448,320},{0,384},{... | collective-permute-start | bytes 196616 | tf_op jit(solution)/shard_map/ppermute | solution.py:78
  132.2 16.6 %all-to-all-start.4 = ((bf16[8,64,256]{2,1,0:T(8,128)(2,1)}), bf16[8,64,256]{2,1,0:T(8,128)(2,1)S(1)}, u32[]{:S(2)}, u32[]{:S(2)}) async-start(bf16[8,64,256]{2,1,0:T(8,128)(2,1)} %broadcast_in_dim.85), calls=%async_computation.4 | async-start | bytes 524288 | tf_op jit(solution)/shard_map/all_to_all | solution.py:82
  138.8 5.5 %collective-permute-start.3 = (bf16[128,256]{1,0:T(8,128)(2,1)S(1)}, bf16[128,256]{1,0:T(8,128)(2,1)S(1)}, u32[]{:S(2)}, u32[]{:S(2)}) collective-permute-start(bf16[128,256]{1,0:T(8,128)(2,1)S(1)} %fusion.11), channel_id=1, source_target_pairs={{64,0},{128,64},{192,128},{256,192},{320,256},{384,320},{448,384},... | collective-permute-start | bytes 196616 | tf_op jit(solution)/shard_map/ppermute | solution.py:78

commit v4 on v3

--- a/solution.py
+++ b/solution.py
@@ -13,7 +13,6 @@
 ROW, COL, REP = "y", ("x", "zl"), ("zh", "core")
 N_ROW, N_COL, N_ZH, N_CORE = 8, 8, 4, 2
 N_REP = N_ZH * N_CORE
-DEGREE_ROWS = 16
 
 
 def arrange_kernel(rows_ref, counts_ref, here_ref, tile_hbm, out_ref, flip_ref, tiles, arrived):
@@ -91,7 +90,7 @@
 
 def per_device(features, degrees, tile_values, tile_rows, tile_counts, weight, cotangent):
     own_rows, width = features.shape
-    col, core, zh = lax.axis_index(COL), lax.axis_index("core"), lax.axis_index("zh")
+    col, core = lax.axis_index(COL), lax.axis_index("core")
     columns = jnp.arange(N_COL, dtype=jnp.int32)[:, None, None]
     inv_root = lax.rsqrt(degrees.astype(F32))[:, None]
     scaled = (features.astype(F32) * inv_root).astype(BF)
@@ -109,29 +108,28 @@
     kept, sent = jnp.split(partial, 2, axis=0)
     other = lax.ppermute(sent.astype(BF), "core", [(0, 1), (1, 0)])
     half = (kept + other.astype(F32)).astype(BF)
-    degree_rows = jnp.zeros((DEGREE_ROWS, width), BF).at[0, :own_rows].set(degrees.astype(BF))
-    told = copies_to(jnp.concatenate([half, cotangent, degree_rows], axis=0), "zh", N_ZH)
-    zh_rows = N_ZH * own_rows
-    zh_sum = summed_in_f32(told[:, :zh_rows])
-    zh_cotangent = told[:, zh_rows : zh_rows + own_rows].reshape(zh_rows, width)
-    zh_degrees = told[:, zh_rows + own_rows, :own_rows].reshape(zh_rows)
-    zh_inv_root = lax.rsqrt(zh_degrees.astype(F32))[:, None]
+    shares = lax.all_to_all(half.reshape(N_ZH, own_rows, width), "zh", 0, 0)
+    own_sum = summed_in_f32(shares)
 
-    aggregated = (zh_sum * zh_inv_root).astype(BF)
+    aggregated = (own_sum * inv_root).astype(BF)
     pre_act = jnp.dot(aggregated, weight, preferred_element_type=F32)
     sigma = jax.nn.sigmoid(pre_act)
-    activations = lax.dynamic_slice_in_dim((pre_act * sigma).astype(BF), zh * own_rows, own_rows)
-    act_grad = (zh_cotangent.astype(F32) * sigma * (1.0 + pre_act * (1.0 - sigma))).astype(BF)
-    zh_weight = lax.dot_general(
-        aggregated, act_grad, (((0,), (0,)), ((), ())), preferred_element_type=F32
-    )
+    activations = (pre_act * sigma).astype(BF)
+    act_grad = (cotangent.astype(F32) * sigma * (1.0 + pre_act * (1.0 - sigma))).astype(BF)
     back_grad = lax.dot_general(
         act_grad, weight, (((1,), (1,)), ((), ())), preferred_element_type=F32
     )
-    back_scaled = (back_grad * zh_inv_root).astype(BF)
-    slab_grads = lax.all_gather(back_scaled, "core", axis=0, tiled=True)
-    share = width // N_ZH
-    weight_rows = lax.dynamic_slice_in_dim(zh_weight, zh * share, share)
+    back_scaled = (back_grad * inv_root).astype(BF)
+    local_weight = lax.dot_general(
+        aggregated, act_grad, (((0,), (0,)), ((), ())), preferred_element_type=F32
+    ).astype(BF)
+    copies = jnp.broadcast_to(back_scaled[None], (N_ZH,) + back_scaled.shape)
+    offer = jnp.concatenate([copies, local_weight.reshape(N_ZH, -1, width)], axis=1)
+    given = lax.all_to_all(offer, "zh", 0, 0)
+    along_zh = given[:, :own_rows].reshape(-1, width)
+    weight_rows = summed_in_f32(given[:, own_rows:])
+    share = weight_rows.shape[0]
+    slab_grads = lax.all_gather(along_zh, "core", axis=0, tiled=True)
 
     along_y = copies_to(weight_rows.astype(BF), ROW, N_ROW)
     weight_rows = summed_in_f32(along_y).astype(BF)

time: 150 us -> 136 us (0.907)
  waiting for transfers between devices: 58.8 us -> 26 us
  blocking collectives: 6.5 us -> 39 us
  starting transfers between devices: 54.2 us -> 44 us
  other arithmetic: 8.4 us -> 6.72 us
    all_to_all x0 -> x2, blocking collectives: none -> 33.9 us  [the longest x1 18.3 us: per_device(): shares = lax.all_to_all(half.reshape(N_ZH, own_rows, width), 'zh', 0, 0)]
    all_to_all x3 -> x2, waiting for transfers between devices: 35.1 us -> 1.67 us  [copies_to(): lax.all_to_all(jnp.broadcast_to(block[None], (count,) + block.shape), axi...]
    all_to_all x3 -> x2, starting transfers between devices: 21 us -> 15.1 us  [copies_to(): lax.all_to_all(jnp.broadcast_to(block[None], (count,) + block.shape), axi...]
    ppermute x4, starting transfers between devices: 16.9 us -> 14.2 us  [shifted(): lax.ppermute(block, ROW, [((i - distance) % N_ROW, i) for i in range(N_RO...]
    convert_element_type x2 -> x1, other arithmetic: 1.77 us -> 0.09 us  [per_device(): aggregated = (own_sum * inv_root).astype(BF)]
    all_to_all x1, starting transfers between devices: 5.13 us -> 3.59 us  [per_device(): lax.all_to_all(jnp.concatenate([returned, copies], axis=1), COL, 0, 0)]
  transfers between devices with their start and end apart: 10 -> 9, of which waited for: 8 -> 9; matrix products, arithmetic and copies ran while one was open for 5% -> 4% of each run, Pallas kernels for 6% -> 6%
where the time goes in v4:
time: 136 us
  starting transfers between devices  44 us (32%)
  blocking collectives  39 us (29%)
  waiting for transfers between devices  26 us (19%)
  Pallas kernels  8.59 us (6%)
  matrix products  8.18 us (6%)
  other arithmetic  6.72 us (5%)
  local copies, waits for them, and re-layouts  2.32 us (2%)
    all_to_all x1, blocking collectives, per_device(): shares = lax.all_to_all(half.reshape(N_ZH, own_rows, width), 'zh', 0, 0)  18.3 us
    all_to_all x1, blocking collectives, per_device(): given = lax.all_to_all(offer, 'zh', 0, 0)  15.6 us
    all_to_all x2, starting transfers between devices, copies_to(): lax.all_to_all(jnp.broadcast_to(block[None], (count,) + block.shape), axi...  15.1 us
    all_to_all x1, waiting for transfers between devices, per_device(): lax.all_to_all(jnp.concatenate([returned, copies], axis=1), COL, 0, 0)  14.4 us
    ppermute x4, starting transfers between devices, shifted(): lax.ppermute(block, ROW, [((i - distance) % N_ROW, i) for i in range(N_RO...  14.2 us
    pallas_call x1, Pallas kernels, arrange(): pl.pallas_call(arrange_kernel, out_shape=(jax.ShapeDtypeStruct((cap * row...  8.59 us
    all_to_all x1, starting transfers between devices, per_device(): window = lax.all_to_all(offer, COL, 0, 0).reshape(-1, width)  5.83 us
    ppermute x4, waiting for transfers between devices, shifted(): lax.ppermute(block, ROW, [((i - distance) % N_ROW, i) for i in range(N_RO...  5.29 us
  transfers between devices with their start and end apart: 9, of which 9 were waited for; matrix products, arithmetic and copies ran while one was open for 4% of the time, Pallas kernels for 6%

profile of v4, /device:TPU:1, one launch (start us, length us, event | category | flops | bytes accessed | tf_op | source)
XLA Modules:
  0.0 135.7 jit_solution(10607669452899481439)
XLA Ops:
  0.6 0.0 copy-start
  0.6 0.7 convert_rsqrt_fusion
  1.3 0.9 multiply_convert_fusion.2
  2.3 5.0 %collective-permute-start.1 = (bf16[128,256]{1,0:T(8,128)(2,1)S(1)}, bf16[128,256]{1,0:T(8,128)(2,1)S(1)}, u32[]{:S(2)}, u32[]{:S(2)}) collective-permute-start(bf16[128,256]{1,0:T(8,128)(2,1)S(1)} %multiply_convert_fusion.2), channel_id=1, source_target_pairs={{384,0},{448,64},{0,128},{64,192},{128,256},{192,320},{256,384},{3... | collective-permute-start | bytes 196616 | tf_op jit(solution)/shard_map/ppermute | solution.py:77
  7.3 3.2 %collective-permute-start = (bf16[128,256]{1,0:T(8,128)(2,1)S(1)}, bf16[128,256]{1,0:T(8,128)(2,1)S(1)}, u32[]{:S(2)}, u32[]{:S(2)}) collective-permute-start(bf16[128,256]{1,0:T(8,128)(2,1)S(1)} %multiply_convert_fusion.2), channel_id=1, source_target_pairs={{448,0},{0,64},{64,128},{128,192},{192,256},{256,320},{320,384},{3... | collective-permute-start | bytes 196616 | tf_op jit(solution)/shard_map/ppermute | solution.py:77
  10.5 0.0 copy-start.1
  10.6 0.2 collective-permute-done.1
  10.7 0.1 broadcast_select_fusion.2
  10.8 2.7 %collective-permute-done = bf16[128,256]{1,0:T(8,128)(2,1)S(1)} collective-permute-done((bf16[128,256]{1,0:T(8,128)(2,1)S(1)}, bf16[128,256]{1,0:T(8,128)(2,1)S(1)}, u32[]{:S(2)}, u32[]{:S(2)}) %collective-permute-start) | collective-permute-done | bytes 65568 | tf_op jit(solution)/shard_map/ppermute | solution.py:77
  13.6 1.1 pad_maximum_fusion.1
  14.7 5.8 %all-to-all-start = ((bf16[8,2,128,256]{3,2,1,0:T(8,128)(2,1)}), bf16[8,2,128,256]{3,2,1,0:T(8,128)(2,1)S(1)}, u32[]{:S(2)}, u32[]{:S(2)}) async-start(bf16[8,2,128,256]{3,2,1,0:T(8,128)(2,1)} %pad_maximum_fusion.1), calls=%async_computation | async-start | bytes 2097152 | tf_op jit(solution)/shard_map/all_to_all | solution.py:105
  20.5 0.0 copy-done.1
  20.6 0.7 copy.11.rows_ref
  21.2 0.6 pad_add_fusion.here_ref
  21.8 8.6 %arrange_tiles.1 = (bf16[1024,2048]{1,0:T(8,128)(2,1)}, bf16[2048,1024]{1,0:T(8,128)(2,1)}) custom-call(s32[1,16,8]{2,1,0:T(8,128)} %copy.11.rows_ref, s32[1,16]{1,0:T(1,128)} %counts_ref.1, s32[2]{0:T(128)} %pad_add_fusion.here_ref, bf16[1,16,8,128,128]{4,3,2,1,0:T(8,128)(2,1)} %tile_hbm.1), custom_call_target="tpu_custom_call" | custom-call | flops 2097152 | bytes 8388608 | tf_op jit(solution)/shard_map/arrange_tiles/pallas_call | solution.py:59
  30.4 3.5 %all-to-all-done = bf16[8,2,128,256]{3,2,1,0:T(8,128)(2,1)S(1)} async-done(((bf16[8,2,128,256]{3,2,1,0:T(8,128)(2,1)}), bf16[8,2,128,256]{3,2,1,0:T(8,128)(2,1)S(1)}, u32[]{:S(2)}, u32[]{:S(2)}) %all-to-all-start) | async-done | bytes 1048608 | tf_op jit(solution)/shard_map/all_to_all | solution.py:105
  33.9 3.5 %fusion.11 = f32[1024,256]{1,0:T(8,128)S(1)} fusion(bf16[1024,2048]{1,0:T(8,128)(2,1)} %get-tuple-element.5, bf16[2048,256]{1,0:T(8,128)(2,1)S(1)} %bitcast.53), kind=kOutput, calls=%fused_computation.39 | convolution fusion | flops 1073741824 | bytes 6291456 | tf_op jit(solution)/shard_map/dot_general | solution.py:107
  37.4 5.3 %collective-permute-start.2 = (bf16[512,256]{1,0:T(8,128)(2,1)S(1)}, bf16[512,256]{1,0:T(8,128)(2,1)S(1)}, u32[]{:S(2)}, u32[]{:S(2)}) collective-permute-start(bf16[512,256]{1,0:T(8,128)(2,1)S(1)} %split.15), channel_id=1, source_target_pairs={{0,1},{1,0},{2,3},{3,2},{4,5},{5,4},{6,7},{7,6},{8,9},{9,8},{10,11... | collective-permute-start | bytes 786440 | tf_op jit(solution)/shard_map/ppermute | solution.py:109
  42.7 1.1 collective-permute-done.2
  43.8 0.1 fusion.1
  43.9 18.3 %all_to_all.30 = bf16[4,128,256]{2,1,0:T(8,128)(2,1)S(1)} all-to-all(bf16[4,128,256]{2,1,0:T(8,128)(2,1)S(1)} %bitcast.55), channel_id=1, replica_groups=mesh['y'=8,'x'=4,'zl'=2,'zh'=4,'core'=2] {'zh'}, dimensions={0} | all-to-all | bytes 524288 | tf_op jit(solution)/shard_map/all_to_all | solution.py:111
  62.2 0.1 fusion.5
  62.3 0.0 copy-done
  62.3 0.9 multiply_convert_fusion
  63.2 0.2 convolution_convert_fusion.1
  63.4 0.2 fusion
  63.7 15.6 %all_to_all.31 = bf16[4,192,256]{2,1,0:T(8,128)(2,1)S(1)} all-to-all(bf16[4,192,256]{2,1,0:T(8,128)(2,1)S(1)} %pad_maximum_fusion.2), channel_id=1, replica_groups=mesh['y'=8,'x'=4,'zl'=2,'zh'=4,'core'=2] {'zh'}, dimensions={0} | all-to-all | bytes 786432 | tf_op jit(solution)/shard_map/all_to_all | solution.py:128
  79.3 0.7 broadcast_in_dim.82
  80.0 4.7 %all-to-all-start.3 = ((bf16[8,64,256]{2,1,0:T(8,128)(2,1)}), bf16[8,64,256]{2,1,0:T(8,128)(2,1)S(1)}, u32[]{:S(2)}, u32[]{:S(2)}) async-start(bf16[8,64,256]{2,1,0:T(8,128)(2,1)} %broadcast_in_dim.82), calls=%async_computation.3 | async-start | bytes 524288 | tf_op jit(solution)/shard_map/all_to_all | solution.py:81
  84.7 5.1 %all_gather.3 = bf16[1024,256]{1,0:T(8,128)(2,1)S(1)} all-gather(bf16[512,256]{1,0:T(8,128)(2,1)S(1)} %bitcast.52), channel_id=1, replica_groups=mesh['y'=8,'x'=4,'zl'=2,'zh'=4,'core'=2] {'core'}, dimensions={0}, use_global_device_ids=true | all-gather | bytes 786432 | tf_op jit(solution)/shard_map/all_gather | solution.py:132
  89.8 3.4 %convolution_convert_fusion = bf16[2048,256]{1,0:T(8,128)(2,1)S(1)} fusion(bf16[2048,1024]{1,0:T(8,128)(2,1)} %get-tuple-element.6, bf16[1024,256]{1,0:T(8,128)(2,1)S(1)} %all_gather.3), kind=kOutput, calls=%fused_computation | convolution fusion | flops 1074266112 | bytes 5767168 | tf_op jit(solution)/shard_map/dot_general | solution.py:136
  93.3 0.8 all-to-all-done.3
  94.2 1.2 pad_maximum_fusion
  95.4 3.6 %all-to-all-start.4 = ((bf16[8,320,256]{2,1,0:T(8,128)(2,1)}), bf16[8,320,256]{2,1,0:T(8,128)(2,1)S(1)}, u32[]{:S(2)}, u32[]{:S(2)}) async-start(bf16[8,320,256]{2,1,0:T(8,128)(2,1)} %pad_maximum_fusion), calls=%async_computation.4 | async-start | bytes 2621440 | tf_op jit(solution)/shard_map/all_to_all | solution.py:139
  99.0 14.4 %all-to-all-done.4 = bf16[8,320,256]{2,1,0:T(8,128)(2,1)S(1)} async-done(((bf16[8,320,256]{2,1,0:T(8,128)(2,1)}), bf16[8,320,256]{2,1,0:T(8,128)(2,1)S(1)}, u32[]{:S(2)}, u32[]{:S(2)}) %all-to-all-start.4) | async-done | bytes 1310752 | tf_op jit(solution)/shard_map/all_to_all | solution.py:139
  113.4 0.1 slice.122
  113.4 0.1 fusion.6
  113.5 0.1 broadcast_select_fusion.1
  113.7 0.7 broadcast_in_dim.86
  114.4 10.4 %all-to-all-start.5 = ((bf16[8,64,256]{2,1,0:T(8,128)(2,1)}), bf16[8,64,256]{2,1,0:T(8,128)(2,1)S(1)}, u32[]{:S(2)}, u32[]{:S(2)}) async-start(bf16[8,64,256]{2,1,0:T(8,128)(2,1)} %broadcast_in_dim.86), calls=%async_computation.5 | async-start | bytes 524288 | tf_op jit(solution)/shard_map/all_to_all | solution.py:81
  124.9 0.1 fusion.7
  124.9 3.4 %collective-permute-start.4 = (bf16[128,256]{1,0:T(8,128)(2,1)S(1)}, bf16[128,256]{1,0:T(8,128)(2,1)S(1)}, u32[]{:S(2)}, u32[]{:S(2)}) collective-permute-start(bf16[128,256]{1,0:T(8,128)(2,1)S(1)} %fusion.7), channel_id=1, source_target_pairs={{128,0},{192,64},{256,128},{320,192},{384,256},{448,320},{0,384},{... | collective-permute-start | bytes 196616 | tf_op jit(solution)/shard_map/ppermute | solution.py:77
  128.3 2.6 %collective-permute-start.3 = (bf16[128,256]{1,0:T(8,128)(2,1)S(1)}, bf16[128,256]{1,0:T(8,128)(2,1)S(1)}, u32[]{:S(2)}, u32[]{:S(2)}) collective-permute-start(bf16[128,256]{1,0:T(8,128)(2,1)S(1)} %fusion.6), channel_id=1, source_target_pairs={{64,0},{128,64},{192,128},{256,192},{320,256},{384,320},{448,384},... | collective-permute-start | bytes 196616 | tf_op jit(solution)/shard_map/ppermute | solution.py:77
  130.9 1.8 %collective-permute-done.4 = bf16[128,256]{1,0:T(8,128)(2,1)S(1)} collective-permute-done((bf16[128,256]{1,0:T(8,128)(2,1)S(1)}, bf16[128,256]{1,0:T(8,128)(2,1)S(1)}, u32[]{:S(2)}, u32[]{:S(2)}) %collective-permute-start.4) | collective-permute-done | bytes 65568 | tf_op jit(solution)/shard_map/ppermute | solution.py:77
  132.7 0.6 collective-permute-done.3
  133.3 0.7 fusion.4
  134.0 0.8 all-to-all-done.5
  134.9 0.7 slice_add_fusion.1
  (14 shorter events, 0.3 us)
Async XLA Ops:
  0.6 61.7 %copy-start = (bf16[256,256]{1,0:T(8,128)(2,1)S(1)}, bf16[256,256]{1,0:T(8,128)(2,1)}, u32[]{:S(2)}) copy-start(bf16[256,256]{1,0:T(8,128)(2,1)} %param.12) | copy-start | bytes 393220
  2.3 8.5 %collective-permute-start.1 = (bf16[128,256]{1,0:T(8,128)(2,1)S(1)}, bf16[128,256]{1,0:T(8,128)(2,1)S(1)}, u32[]{:S(2)}, u32[]{:S(2)}) collective-permute-start(bf16[128,256]{1,0:T(8,128)(2,1)S(1)} %multiply_convert_fusion.2), channel_id=1, source_target_pairs={{384,0},{448,64},{0,128},{64,192},{128,256},{192,320},{256,384},{3... | collective-permute-start | bytes 196616 | tf_op jit(solution)/shard_map/ppermute | solution.py:77
  7.3 6.2 %collective-permute-start = (bf16[128,256]{1,0:T(8,128)(2,1)S(1)}, bf16[128,256]{1,0:T(8,128)(2,1)S(1)}, u32[]{:S(2)}, u32[]{:S(2)}) collective-permute-start(bf16[128,256]{1,0:T(8,128)(2,1)S(1)} %multiply_convert_fusion.2), channel_id=1, source_target_pairs={{448,0},{0,64},{64,128},{128,192},{192,256},{256,320},{320,384},{3... | collective-permute-start | bytes 196616 | tf_op jit(solution)/shard_map/ppermute | solution.py:77
  10.5 10.0 %copy-start.1 = (s32[1,16,8]{1,2,0:T(8,128)S(1)}, s32[1,16,8]{1,2,0:T(8,128)}, u32[]{:S(2)}) copy-start(s32[1,16,8]{1,2,0:T(8,128)} %param.10) | copy-start | bytes 1540
  14.7 19.2 %all-to-all-start = ((bf16[8,2,128,256]{3,2,1,0:T(8,128)(2,1)}), bf16[8,2,128,256]{3,2,1,0:T(8,128)(2,1)S(1)}, u32[]{:S(2)}, u32[]{:S(2)}) async-start(bf16[8,2,128,256]{3,2,1,0:T(8,128)(2,1)} %pad_maximum_fusion.1), calls=%async_computation | async-start | bytes 2097152 | tf_op jit(solution)/shard_map/all_to_all | solution.py:105
  33.9 28.4 %copy-start.2 = (bf16[128,256]{1,0:T(8,128)(2,1)S(1)}, bf16[128,256]{1,0:T(8,128)(2,1)}, u32[]{:S(2)}) copy-start(bf16[128,256]{1,0:T(8,128)(2,1)} %param.13) | copy-start | bytes 196612
  37.4 6.4 %collective-permute-start.2 = (bf16[512,256]{1,0:T(8,128)(2,1)S(1)}, bf16[512,256]{1,0:T(8,128)(2,1)S(1)}, u32[]{:S(2)}, u32[]{:S(2)}) collective-permute-start(bf16[512,256]{1,0:T(8,128)(2,1)S(1)} %split.15), channel_id=1, source_target_pairs={{0,1},{1,0},{2,3},{3,2},{4,5},{5,4},{6,7},{7,6},{8,9},{9,8},{10,11... | collective-permute-start | bytes 786440 | tf_op jit(solution)/shard_map/ppermute | solution.py:109
  80.0 14.1 %all-to-all-start.3 = ((bf16[8,64,256]{2,1,0:T(8,128)(2,1)}), bf16[8,64,256]{2,1,0:T(8,128)(2,1)S(1)}, u32[]{:S(2)}, u32[]{:S(2)}) async-start(bf16[8,64,256]{2,1,0:T(8,128)(2,1)} %broadcast_in_dim.82), calls=%async_computation.3 | async-start | bytes 524288 | tf_op jit(solution)/shard_map/all_to_all | solution.py:81
  95.4 18.0 %all-to-all-start.4 = ((bf16[8,320,256]{2,1,0:T(8,128)(2,1)}), bf16[8,320,256]{2,1,0:T(8,128)(2,1)S(1)}, u32[]{:S(2)}, u32[]{:S(2)}) async-start(bf16[8,320,256]{2,1,0:T(8,128)(2,1)} %pad_maximum_fusion), calls=%async_computation.4 | async-start | bytes 2621440 | tf_op jit(solution)/shard_map/all_to_all | solution.py:139
  114.4 20.5 %all-to-all-start.5 = ((bf16[8,64,256]{2,1,0:T(8,128)(2,1)}), bf16[8,64,256]{2,1,0:T(8,128)(2,1)S(1)}, u32[]{:S(2)}, u32[]{:S(2)}) async-start(bf16[8,64,256]{2,1,0:T(8,128)(2,1)} %broadcast_in_dim.86), calls=%async_computation.5 | async-start | bytes 524288 | tf_op jit(solution)/shard_map/all_to_all | solution.py:81
  124.9 7.8 %collective-permute-start.4 = (bf16[128,256]{1,0:T(8,128)(2,1)S(1)}, bf16[128,256]{1,0:T(8,128)(2,1)S(1)}, u32[]{:S(2)}, u32[]{:S(2)}) collective-permute-start(bf16[128,256]{1,0:T(8,128)(2,1)S(1)} %fusion.7), channel_id=1, source_target_pairs={{128,0},{192,64},{256,128},{320,192},{384,256},{448,320},{0,384},{... | collective-permute-start | bytes 196616 | tf_op jit(solution)/shard_map/ppermute | solution.py:77
  128.3 5.0 %collective-permute-start.3 = (bf16[128,256]{1,0:T(8,128)(2,1)S(1)}, bf16[128,256]{1,0:T(8,128)(2,1)S(1)}, u32[]{:S(2)}, u32[]{:S(2)}) collective-permute-start(bf16[128,256]{1,0:T(8,128)(2,1)S(1)} %fusion.6), channel_id=1, source_target_pairs={{64,0},{128,64},{192,128},{256,192},{320,256},{384,320},{448,384},... | collective-permute-start | bytes 196616 | tf_op jit(solution)/shard_map/ppermute | solution.py:77

commit v5 on v4

--- a/solution.py
+++ b/solution.py
@@ -10,8 +10,8 @@
 
 BF = jnp.bfloat16
 F32 = jnp.float32
-ROW, COL, REP = "y", ("x", "zl"), ("zh", "core")
-N_ROW, N_COL, N_ZH, N_CORE = 8, 8, 4, 2
+PAIR, GROUP, REP = "yp", ("ye", "x", "zl"), ("zh", "core")
+N_PAIR, N_GROUP, N_ZH, N_CORE = 4, 16, 4, 2
 N_REP = N_ZH * N_CORE
 
 
@@ -25,17 +25,13 @@
 
     for distance in range(span):
         fetch(distance).start()
-    col, core = here_ref[0], here_ref[1]
+    place, core = here_ref[0], here_ref[1]
 
     def place_distance(distance, carry):
         fetch(distance).wait()
         live_count = counts_ref[0, distance]
-        wrapped = lax.rem(distance, N_COL)
-        same_turn = col >= wrapped
-        source = jnp.where(same_turn, col - wrapped, col - wrapped + N_COL)
-        near = distance < N_COL
-        slot = jnp.where(same_turn == near, 1, 0)
-        at_col = pl.ds(pl.multiple_of((source * 2 + slot) * block, block), block)
+        source = lax.rem(place + (span - distance), span)
+        at_col = pl.ds(pl.multiple_of(source * block, block), block)
         for k in range(cap):
             owner = rows_ref[0, distance, k]
             owner_core, owner_zh = lax.rem(owner, N_CORE), lax.div(owner, N_CORE)
@@ -74,7 +70,7 @@
 
 
 def shifted(block, distance):
-    return lax.ppermute(block, ROW, [((i - distance) % N_ROW, i) for i in range(N_ROW)])
+    return lax.ppermute(block, PAIR, [((i - distance) % N_PAIR, i) for i in range(N_PAIR)])
 
 
 def copies_to(block, axis, count):
@@ -90,19 +86,17 @@
 
 def per_device(features, degrees, tile_values, tile_rows, tile_counts, weight, cotangent):
     own_rows, width = features.shape
-    col, core = lax.axis_index(COL), lax.axis_index("core")
-    columns = jnp.arange(N_COL, dtype=jnp.int32)[:, None, None]
+    place, core = lax.axis_index(GROUP), lax.axis_index("core")
+    places = jnp.arange(N_GROUP, dtype=jnp.int32)[:, None, None]
     inv_root = lax.rsqrt(degrees.astype(F32))[:, None]
     scaled = (features.astype(F32) * inv_root).astype(BF)
 
-    one_back = shifted(scaled, 1)
-    two_back = shifted(scaled, 2)
+    pair_back = shifted(scaled, 1)
     adjacency, flipped = arrange(
-        tile_values, tile_rows, tile_counts, jnp.stack([col, core])
+        tile_values, tile_rows, tile_counts, jnp.stack([place, core])
     )
-    own_or_two = jnp.where(columns >= col, scaled[None], two_back[None])
-    offer = jnp.stack([jnp.broadcast_to(one_back[None], own_or_two.shape), own_or_two], axis=1)
-    window = lax.all_to_all(offer, COL, 0, 0).reshape(-1, width)
+    offer = jnp.where(places >= place, scaled[None], pair_back[None])
+    window = lax.all_to_all(offer, GROUP, 0, 0).reshape(-1, width)
 
     partial = jnp.dot(adjacency, window, preferred_element_type=F32)
     kept, sent = jnp.split(partial, 2, axis=0)
@@ -131,35 +125,33 @@
     share = weight_rows.shape[0]
     slab_grads = lax.all_gather(along_zh, "core", axis=0, tiled=True)
 
-    along_y = copies_to(weight_rows.astype(BF), ROW, N_ROW)
+    along_y = copies_to(weight_rows.astype(BF), PAIR, N_PAIR)
     weight_rows = summed_in_f32(along_y).astype(BF)
     returned = jnp.dot(flipped, slab_grads, preferred_element_type=F32).astype(BF)
-    returned = returned.reshape(N_COL, 2 * own_rows, width)
-    copies = jnp.broadcast_to(weight_rows[None], (N_COL,) + weight_rows.shape)
-    home = lax.all_to_all(jnp.concatenate([returned, copies], axis=1), COL, 0, 0)
-    node_total = own_rows * N_ROW * N_COL * N_REP
-    weight_rows = (summed_in_f32(home[:, 2 * own_rows :]) / math.sqrt(node_total)).astype(BF)
+    returned = returned.reshape(N_GROUP, own_rows, width)
+    copies = jnp.broadcast_to(weight_rows[None], (N_GROUP,) + weight_rows.shape)
+    home = lax.all_to_all(jnp.concatenate([returned, copies], axis=1), GROUP, 0, 0)
+    node_total = own_rows * N_PAIR * N_GROUP * N_REP
+    weight_rows = (summed_in_f32(home[:, own_rows:]) / math.sqrt(node_total)).astype(BF)
     along_rep = copies_to(weight_rows, REP, N_REP)
     along_rep = along_rep.reshape(N_ZH, N_CORE, share, width).astype(F32)
     grad_weight = (along_rep[:, 0] + along_rep[:, 1]).reshape(-1, width)
 
-    arrived = home[:, : 2 * own_rows].reshape(N_COL, 2, own_rows, width)
-    for_one = summed_in_f32(arrived[:, 0]).astype(BF)
+    arrived = home[:, :own_rows]
     nothing = jnp.zeros((), BF)
-    for_two = summed_in_f32(jnp.where(columns < col, arrived[:, 1], nothing)).astype(BF)
-    for_own = summed_in_f32(jnp.where(columns >= col, arrived[:, 1], nothing))
-    from_two = shifted(for_two, -2)
-    from_one = shifted(for_one, -1)
-    back_total = for_own + from_one.astype(F32) + from_two.astype(F32)
+    for_back = summed_in_f32(jnp.where(places < place, arrived, nothing)).astype(BF)
+    for_own = summed_in_f32(jnp.where(places >= place, arrived, nothing))
+    from_next = shifted(for_back, -1)
+    back_total = for_own + from_next.astype(F32)
     grad_features = (back_total * inv_root).astype(BF)
     return (activations, grad_weight, grad_features)
 
 
 def solution(mesh):
     fine = Mesh(
-        mesh.devices.reshape(N_ROW, 4, 2, N_ZH, N_CORE), ("y", "x", "zl", "zh", "core")
+        mesh.devices.reshape(N_PAIR, 2, 4, 2, N_ZH, N_CORE), (PAIR,) + GROUP + REP
     )
-    nodes = ("y", "x", "zl", "zh", "core")
+    nodes = (PAIR,) + GROUP + REP
     placed = (
         P(nodes, None),
         P(nodes),

time: 136 us -> 137 us (level)
  the two profiles are of different devices: /device:TPU:1 before, /device:TPU:46 now
where the time goes in v5:
time: 137 us
  waiting for transfers between devices  41.6 us (30%)
  blocking collectives  38.3 us (28%)
  starting transfers between devices  30.1 us (22%)
  Pallas kernels  8.5 us (6%)
  matrix products  8.16 us (6%)
  other arithmetic  6.93 us (5%)
  local copies, waits for them, and re-layouts  2.19 us (2%)
    all_to_all x1, waiting for transfers between devices, per_device(): lax.all_to_all(jnp.concatenate([returned, copies], axis=1), GROUP, 0, 0)  21.4 us
    all_to_all x1, blocking collectives, per_device(): shares = lax.all_to_all(half.reshape(N_ZH, own_rows, width), 'zh', 0, 0)  20.3 us
    all_to_all x1, blocking collectives, per_device(): given = lax.all_to_all(offer, 'zh', 0, 0)  15.7 us
    ppermute x2, waiting for transfers between devices, shifted(): lax.ppermute(block, PAIR, [((i - distance) % N_PAIR, i) for i in range(N_...  12 us
    all_to_all x2, starting transfers between devices, copies_to(): lax.all_to_all(jnp.broadcast_to(block[None], (count,) + block.shape), axi...  10.6 us
    pallas_call x1, Pallas kernels, arrange(): pl.pallas_call(arrange_kernel, out_shape=(jax.ShapeDtypeStruct((cap * row...  8.5 us
    all_to_all x1, starting transfers between devices, per_device(): window = lax.all_to_all(offer, GROUP, 0, 0).reshape(-1, width)  7.5 us
    all_to_all x1, starting transfers between devices, per_device(): lax.all_to_all(jnp.concatenate([returned, copies], axis=1), GROUP, 0, 0)  5.43 us
  transfers between devices with their start and end apart: 7, of which 6 were waited for; matrix products, arithmetic and copies ran while one was open for 4% of the time, Pallas kernels for 6%

profile of v5, /device:TPU:46, one launch (start us, length us, event | category | flops | bytes accessed | tf_op | source)
XLA Modules:
  0.0 136.6 jit_solution(18042722121654976062)
XLA Ops:
  0.6 0.0 copy-start
  0.6 0.0 copy-start.1
  0.7 0.7 convert_rsqrt_fusion
  1.4 0.9 multiply_convert_fusion.2
  2.3 2.7 %collective-permute-start = (bf16[128,256]{1,0:T(8,128)(2,1)S(1)}, bf16[128,256]{1,0:T(8,128)(2,1)S(1)}, u32[]{:S(2)}, u32[]{:S(2)}) collective-permute-start(bf16[128,256]{1,0:T(8,128)(2,1)S(1)} %multiply_convert_fusion.2), channel_id=1, source_target_pairs={{384,0},{0,128},{128,256},{256,384},{385,1},{1,129},{129,257},{257... | collective-permute-start | bytes 196616 | tf_op jit(solution)/shard_map/ppermute | solution.py:73
  5.0 6.7 %collective-permute-done = bf16[128,256]{1,0:T(8,128)(2,1)S(1)} collective-permute-done((bf16[128,256]{1,0:T(8,128)(2,1)S(1)}, bf16[128,256]{1,0:T(8,128)(2,1)S(1)}, u32[]{:S(2)}, u32[]{:S(2)}) %collective-permute-start) | collective-permute-done | bytes 65568 | tf_op jit(solution)/shard_map/ppermute | solution.py:73
  11.7 1.2 broadcast_select_fusion.2
  12.9 7.5 %all-to-all-start = ((bf16[16,128,256]{2,1,0:T(8,128)(2,1)}), bf16[16,128,256]{2,1,0:T(8,128)(2,1)S(1)}, u32[]{:S(2)}, u32[]{:S(2)}) async-start(bf16[16,128,256]{2,1,0:T(8,128)(2,1)} %broadcast_select_fusion.2), calls=%async_computation | async-start | bytes 2097152 | tf_op jit(solution)/shard_map/all_to_all | solution.py:99
  20.4 0.0 copy-done.1
  20.4 0.7 copy.11.rows_ref
  21.1 0.6 pad_add_fusion.here_ref
  21.7 8.5 %arrange_tiles.1 = (bf16[1024,2048]{1,0:T(8,128)(2,1)}, bf16[2048,1024]{1,0:T(8,128)(2,1)}) custom-call(s32[1,16,8]{2,1,0:T(8,128)} %copy.11.rows_ref, s32[1,16]{1,0:T(1,128)} %counts_ref.1, s32[2]{0:T(128)} %pad_add_fusion.here_ref, bf16[1,16,8,128,128]{4,3,2,1,0:T(8,128)(2,1)} %tile_hbm.1), custom_call_target="tpu_custom_call" | custom-call | flops 2097152 | bytes 8388608 | tf_op jit(solution)/shard_map/arrange_tiles/pallas_call | solution.py:55
  30.2 2.4 %all-to-all-done = bf16[16,128,256]{2,1,0:T(8,128)(2,1)S(1)} async-done(((bf16[16,128,256]{2,1,0:T(8,128)(2,1)}), bf16[16,128,256]{2,1,0:T(8,128)(2,1)S(1)}, u32[]{:S(2)}, u32[]{:S(2)}) %all-to-all-start) | async-done | bytes 1048608 | tf_op jit(solution)/shard_map/all_to_all | solution.py:99
  32.6 0.0 copy-start.2
  32.6 3.5 %fusion.10 = f32[1024,256]{1,0:T(8,128)S(1)} fusion(bf16[1024,2048]{1,0:T(8,128)(2,1)} %get-tuple-element.5, bf16[2048,256]{1,0:T(8,128)(2,1)S(1)} %bitcast.47), kind=kOutput, calls=%fused_computation.37 | convolution fusion | flops 1073741824 | bytes 6291456 | tf_op jit(solution)/shard_map/dot_general | solution.py:101
  36.1 1.9 %collective-permute-start.1 = (bf16[512,256]{1,0:T(8,128)(2,1)S(1)}, bf16[512,256]{1,0:T(8,128)(2,1)S(1)}, u32[]{:S(2)}, u32[]{:S(2)}) collective-permute-start(bf16[512,256]{1,0:T(8,128)(2,1)S(1)} %split.15), channel_id=1, source_target_pairs={{0,1},{1,0},{2,3},{3,2},{4,5},{5,4},{6,7},{7,6},{8,9},{9,8},{10,11... | collective-permute-start | bytes 786440 | tf_op jit(solution)/shard_map/ppermute | solution.py:103
  38.1 1.5 %collective-permute-done.1 = bf16[512,256]{1,0:T(8,128)(2,1)S(1)} collective-permute-done((bf16[512,256]{1,0:T(8,128)(2,1)S(1)}, bf16[512,256]{1,0:T(8,128)(2,1)S(1)}, u32[]{:S(2)}, u32[]{:S(2)}) %collective-permute-start.1) | collective-permute-done | bytes 262176 | tf_op jit(solution)/shard_map/ppermute | solution.py:103
  39.6 0.1 fusion.1
  39.6 20.3 %all_to_all.30 = bf16[4,128,256]{2,1,0:T(8,128)(2,1)S(1)} all-to-all(bf16[4,128,256]{2,1,0:T(8,128)(2,1)S(1)} %bitcast.48), channel_id=1, replica_groups=mesh['yp'=4,'ye'=2,'x'=4,'zl'=2,'zh'=4,'core'=2] {'zh'}, dimensions={0} | all-to-all | bytes 524288 | tf_op jit(solution)/shard_map/all_to_all | solution.py:105
  60.0 0.1 fusion.6
  60.1 0.0 copy-done
  60.1 0.0 copy-done.2
  60.1 0.9 multiply_convert_fusion
  60.9 0.2 convolution_convert_fusion.1
  61.2 0.2 fusion
  61.4 15.7 %all_to_all.31 = bf16[4,192,256]{2,1,0:T(8,128)(2,1)S(1)} all-to-all(bf16[4,192,256]{2,1,0:T(8,128)(2,1)S(1)} %pad_maximum_fusion.1), channel_id=1, replica_groups=mesh['yp'=4,'ye'=2,'x'=4,'zl'=2,'zh'=4,'core'=2] {'zh'}, dimensions={0} | all-to-all | bytes 786432 | tf_op jit(solution)/shard_map/all_to_all | solution.py:122
  77.2 0.7 broadcast_in_dim.79
  77.9 7.2 %all-to-all-start.3 = ((bf16[4,64,256]{2,1,0:T(8,128)(2,1)}), bf16[4,64,256]{2,1,0:T(8,128)(2,1)S(1)}, u32[]{:S(2)}, u32[]{:S(2)}) async-start(bf16[4,64,256]{2,1,0:T(8,128)(2,1)} %broadcast_in_dim.79), calls=%async_computation.3 | async-start | bytes 262144 | tf_op jit(solution)/shard_map/all_to_all | solution.py:77
  85.1 2.2 %all_gather.3 = bf16[1024,256]{1,0:T(8,128)(2,1)S(1)} all-gather(bf16[512,256]{1,0:T(8,128)(2,1)S(1)} %bitcast.46), channel_id=1, replica_groups=mesh['yp'=4,'ye'=2,'x'=4,'zl'=2,'zh'=4,'core'=2] {'core'}, dimensions={0}, use_global_device_ids=true | all-gather | bytes 786432 | tf_op jit(solution)/shard_map/all_gather | solution.py:126
  87.3 3.4 %convolution_convert_fusion = bf16[2048,256]{1,0:T(8,128)(2,1)S(1)} fusion(bf16[2048,1024]{1,0:T(8,128)(2,1)} %get-tuple-element.6, bf16[1024,256]{1,0:T(8,128)(2,1)S(1)} %all_gather.3), kind=kOutput, calls=%fused_computation | convolution fusion | flops 1074266112 | bytes 5767168 | tf_op jit(solution)/shard_map/dot_general | solution.py:130
  90.7 0.0 all-to-all-done.3
  90.8 1.3 pad_maximum_fusion
  92.1 5.4 %all-to-all-start.4 = ((bf16[16,192,256]{2,1,0:T(8,128)(2,1)}), bf16[16,192,256]{2,1,0:T(8,128)(2,1)S(1)}, u32[]{:S(2)}, u32[]{:S(2)}) async-start(bf16[16,192,256]{2,1,0:T(8,128)(2,1)} %pad_maximum_fusion), calls=%async_computation.4 | async-start | bytes 3145728 | tf_op jit(solution)/shard_map/all_to_all | solution.py:133
  97.5 21.4 %all-to-all-done.4 = bf16[16,192,256]{2,1,0:T(8,128)(2,1)S(1)} async-done(((bf16[16,192,256]{2,1,0:T(8,128)(2,1)}), bf16[16,192,256]{2,1,0:T(8,128)(2,1)S(1)}, u32[]{:S(2)}, u32[]{:S(2)}) %all-to-all-start.4) | async-done | bytes 1572896 | tf_op jit(solution)/shard_map/all_to_all | solution.py:133
  119.0 0.1 fusion.9
  119.0 0.7 broadcast_in_dim.83
  119.8 3.4 %all-to-all-start.5 = ((bf16[8,64,256]{2,1,0:T(8,128)(2,1)}), bf16[8,64,256]{2,1,0:T(8,128)(2,1)S(1)}, u32[]{:S(2)}, u32[]{:S(2)}) async-start(bf16[8,64,256]{2,1,0:T(8,128)(2,1)} %broadcast_in_dim.83), calls=%async_computation.5 | async-start | bytes 524288 | tf_op jit(solution)/shard_map/all_to_all | solution.py:77
  123.2 0.2 broadcast_select_fusion.1
  123.4 0.1 fusion.2
  123.5 1.9 %collective-permute-start.2 = (bf16[128,256]{1,0:T(8,128)(2,1)S(1)}, bf16[128,256]{1,0:T(8,128)(2,1)S(1)}, u32[]{:S(2)}, u32[]{:S(2)}) collective-permute-start(bf16[128,256]{1,0:T(8,128)(2,1)S(1)} %fusion.2), channel_id=1, source_target_pairs={{128,0},{256,128},{384,256},{0,384},{129,1},{257,129},{385,257},{1... | collective-permute-start | bytes 196616 | tf_op jit(solution)/shard_map/ppermute | solution.py:73
  125.5 5.4 %collective-permute-done.2 = bf16[128,256]{1,0:T(8,128)(2,1)S(1)} collective-permute-done((bf16[128,256]{1,0:T(8,128)(2,1)S(1)}, bf16[128,256]{1,0:T(8,128)(2,1)S(1)}, u32[]{:S(2)}, u32[]{:S(2)}) %collective-permute-start.2) | collective-permute-done | bytes 65568 | tf_op jit(solution)/shard_map/ppermute | solution.py:73
  130.8 0.8 fusion.5
  131.6 4.2 %all-to-all-done.5 = bf16[8,64,256]{2,1,0:T(8,128)(2,1)S(1)} async-done(((bf16[8,64,256]{2,1,0:T(8,128)(2,1)}), bf16[8,64,256]{2,1,0:T(8,128)(2,1)S(1)}, u32[]{:S(2)}, u32[]{:S(2)}) %all-to-all-start.5) | async-done | bytes 262176 | tf_op jit(solution)/shard_map/all_to_all | solution.py:77
  135.9 0.7 slice_add_fusion.1
  (10 shorter events, 0.2 us)
Async XLA Ops:
  0.6 59.4 %copy-start = (bf16[256,256]{1,0:T(8,128)(2,1)S(1)}, bf16[256,256]{1,0:T(8,128)(2,1)}, u32[]{:S(2)}) copy-start(bf16[256,256]{1,0:T(8,128)(2,1)} %param.12) | copy-start | bytes 393220
  0.6 19.8 %copy-start.1 = (s32[1,16,8]{1,2,0:T(8,128)S(1)}, s32[1,16,8]{1,2,0:T(8,128)}, u32[]{:S(2)}) copy-start(s32[1,16,8]{1,2,0:T(8,128)} %param.10) | copy-start | bytes 1540
  2.3 9.4 %collective-permute-start = (bf16[128,256]{1,0:T(8,128)(2,1)S(1)}, bf16[128,256]{1,0:T(8,128)(2,1)S(1)}, u32[]{:S(2)}, u32[]{:S(2)}) collective-permute-start(bf16[128,256]{1,0:T(8,128)(2,1)S(1)} %multiply_convert_fusion.2), channel_id=1, source_target_pairs={{384,0},{0,128},{128,256},{256,384},{385,1},{1,129},{129,257},{257... | collective-permute-start | bytes 196616 | tf_op jit(solution)/shard_map/ppermute | solution.py:73
  12.9 19.7 %all-to-all-start = ((bf16[16,128,256]{2,1,0:T(8,128)(2,1)}), bf16[16,128,256]{2,1,0:T(8,128)(2,1)S(1)}, u32[]{:S(2)}, u32[]{:S(2)}) async-start(bf16[16,128,256]{2,1,0:T(8,128)(2,1)} %broadcast_select_fusion.2), calls=%async_computation | async-start | bytes 2097152 | tf_op jit(solution)/shard_map/all_to_all | solution.py:99
  32.6 27.5 %copy-start.2 = (bf16[128,256]{1,0:T(8,128)(2,1)S(1)}, bf16[128,256]{1,0:T(8,128)(2,1)}, u32[]{:S(2)}) copy-start(bf16[128,256]{1,0:T(8,128)(2,1)} %param.13) | copy-start | bytes 196612
  36.1 3.4 %collective-permute-start.1 = (bf16[512,256]{1,0:T(8,128)(2,1)S(1)}, bf16[512,256]{1,0:T(8,128)(2,1)S(1)}, u32[]{:S(2)}, u32[]{:S(2)}) collective-permute-start(bf16[512,256]{1,0:T(8,128)(2,1)S(1)} %split.15), channel_id=1, source_target_pairs={{0,1},{1,0},{2,3},{3,2},{4,5},{5,4},{6,7},{7,6},{8,9},{9,8},{10,11... | collective-permute-start | bytes 786440 | tf_op jit(solution)/shard_map/ppermute | solution.py:103
  77.9 12.9 %all-to-all-start.3 = ((bf16[4,64,256]{2,1,0:T(8,128)(2,1)}), bf16[4,64,256]{2,1,0:T(8,128)(2,1)S(1)}, u32[]{:S(2)}, u32[]{:S(2)}) async-start(bf16[4,64,256]{2,1,0:T(8,128)(2,1)} %broadcast_in_dim.79), calls=%async_computation.3 | async-start | bytes 262144 | tf_op jit(solution)/shard_map/all_to_all | solution.py:77
  92.1 26.9 %all-to-all-start.4 = ((bf16[16,192,256]{2,1,0:T(8,128)(2,1)}), bf16[16,192,256]{2,1,0:T(8,128)(2,1)S(1)}, u32[]{:S(2)}, u32[]{:S(2)}) async-start(bf16[16,192,256]{2,1,0:T(8,128)(2,1)} %pad_maximum_fusion), calls=%async_computation.4 | async-start | bytes 3145728 | tf_op jit(solution)/shard_map/all_to_all | solution.py:133
  119.8 16.1 %all-to-all-start.5 = ((bf16[8,64,256]{2,1,0:T(8,128)(2,1)}), bf16[8,64,256]{2,1,0:T(8,128)(2,1)S(1)}, u32[]{:S(2)}, u32[]{:S(2)}) async-start(bf16[8,64,256]{2,1,0:T(8,128)(2,1)} %broadcast_in_dim.83), calls=%async_computation.5 | async-start | bytes 524288 | tf_op jit(solution)/shard_map/all_to_all | solution.py:77
  123.5 7.3 %collective-permute-start.2 = (bf16[128,256]{1,0:T(8,128)(2,1)S(1)}, bf16[128,256]{1,0:T(8,128)(2,1)S(1)}, u32[]{:S(2)}, u32[]{:S(2)}) collective-permute-start(bf16[128,256]{1,0:T(8,128)(2,1)S(1)} %fusion.2), channel_id=1, source_target_pairs={{128,0},{256,128},{384,256},{0,384},{129,1},{257,129},{385,257},{1... | collective-permute-start | bytes 196616 | tf_op jit(solution)/shard_map/ppermute | solution.py:73

commit v6 on v4

--- a/solution.py
+++ b/solution.py
@@ -73,6 +73,52 @@
     )(tile_rows, tile_counts, here, tile_values)
 
 
+def product_kernel(adjacency_hbm, window_ref, kept_ref, sent_ref, blocks, arrived):
+    count, step, _ = blocks.shape
+    half = kept_ref.shape[0]
+
+    def fetch(index):
+        return pltpu.make_async_copy(
+            adjacency_hbm.at[pl.ds(index * step, step)], blocks.at[index], arrived.at[index]
+        )
+
+    for index in range(count):
+        fetch(index).start()
+    for index in range(count):
+        fetch(index).wait()
+        rows = jnp.dot(blocks[index], window_ref[...], preferred_element_type=F32)
+        start = index * step
+        if start < half:
+            kept_ref[start : start + step] = rows
+        else:
+            sent_ref[start - half : start - half + step] = rows.astype(BF)
+
+
+def product(adjacency, window):
+    rows, depth = adjacency.shape
+    width = window.shape[1]
+    whole = pl.BlockSpec(memory_space=pltpu.VMEM)
+    return pl.pallas_call(
+        product_kernel,
+        out_shape=(
+            pltpu.VMEM((rows // 2, width), F32),
+            pltpu.VMEM((rows // 2, width), BF),
+        ),
+        in_specs=[pl.BlockSpec(memory_space=pltpu.HBM), whole],
+        out_specs=(whole, whole),
+        scratch_shapes=[
+            pltpu.VMEM((N_ZH, rows // N_ZH, depth), BF),
+            pltpu.SemaphoreType.DMA((N_ZH,)),
+        ],
+        cost_estimate=pl.CostEstimate(
+            flops=2 * rows * depth * width,
+            bytes_accessed=2 * rows * depth,
+            transcendentals=0,
+        ),
+        name="forward_product",
+    )(adjacency, window)
+
+
 def shifted(block, distance):
     return lax.ppermute(block, ROW, [((i - distance) % N_ROW, i) for i in range(N_ROW)])
 
@@ -104,9 +150,8 @@
     offer = jnp.stack([jnp.broadcast_to(one_back[None], own_or_two.shape), own_or_two], axis=1)
     window = lax.all_to_all(offer, COL, 0, 0).reshape(-1, width)
 
-    partial = jnp.dot(adjacency, window, preferred_element_type=F32)
-    kept, sent = jnp.split(partial, 2, axis=0)
-    other = lax.ppermute(sent.astype(BF), "core", [(0, 1), (1, 0)])
+    kept, sent = product(adjacency, window)
+    other = lax.ppermute(sent, "core", [(0, 1), (1, 0)])
     half = (kept + other.astype(F32)).astype(BF)
     shares = lax.all_to_all(half.reshape(N_ZH, own_rows, width), "zh", 0, 0)
     own_sum = summed_in_f32(shares)
@@ -127,9 +172,12 @@
     offer = jnp.concatenate([copies, local_weight.reshape(N_ZH, -1, width)], axis=1)
     given = lax.all_to_all(offer, "zh", 0, 0)
     along_zh = given[:, :own_rows].reshape(-1, width)
-    weight_rows = summed_in_f32(given[:, own_rows:])
-    share = weight_rows.shape[0]
-    slab_grads = lax.all_gather(along_zh, "core", axis=0, tiled=True)
+    weight_part = summed_in_f32(given[:, own_rows:]).astype(BF)
+    zh_rows = N_ZH * own_rows
+    pair = lax.all_gather(jnp.concatenate([along_zh, weight_part], axis=0), "core")
+    slab_grads = pair[:, :zh_rows].reshape(-1, width)
+    weight_pair = pair[:, zh_rows:].reshape(N_CORE, N_CORE, -1, width)
+    weight_rows = summed_in_f32(lax.dynamic_index_in_dim(weight_pair, core, 1, keepdims=False))
 
     along_y = copies_to(weight_rows.astype(BF), ROW, N_ROW)
     weight_rows = summed_in_f32(along_y).astype(BF)
@@ -140,8 +188,7 @@
     node_total = own_rows * N_ROW * N_COL * N_REP
     weight_rows = (summed_in_f32(home[:, 2 * own_rows :]) / math.sqrt(node_total)).astype(BF)
     along_rep = copies_to(weight_rows, REP, N_REP)
-    along_rep = along_rep.reshape(N_ZH, N_CORE, share, width).astype(F32)
-    grad_weight = (along_rep[:, 0] + along_rep[:, 1]).reshape(-1, width)
+    grad_weight = along_rep.reshape(-1, width).astype(F32)
 
     arrived = home[:, : 2 * own_rows].reshape(N_COL, 2, own_rows, width)
     for_one = summed_in_f32(arrived[:, 0]).astype(BF)

time: 136 us -> 143 us (1.051)
  waiting for transfers between devices: 26 us -> 44.8 us
  blocking collectives: 39 us -> 22.9 us
  Pallas kernels: 8.59 us -> 13.9 us
  matrix products: 8.18 us -> 4.7 us
    all_to_all x1 -> x0, blocking collectives: 15.6 us -> none  [per_device(): given = lax.all_to_all(offer, 'zh', 0, 0)]
    all_to_all x0 -> x1, waiting for transfers between devices: none -> 10.7 us  [per_device(): given = lax.all_to_all(offer, 'zh', 0, 0)]
    all_to_all x2, waiting for transfers between devices: 1.67 us -> 11.8 us  [copies_to(): lax.all_to_all(jnp.broadcast_to(block[None], (count,) + block.shape), axi...]
    pallas_call x0 -> x1, Pallas kernels: none -> 5.27 us  [product(): pl.pallas_call(product_kernel, out_shape=(pltpu.VMEM((rows // 2, width),...]
    all_to_all x0 -> x1, starting transfers between devices: none -> 4.03 us  [per_device(): given = lax.all_to_all(offer, 'zh', 0, 0)]
    dot_general x1 -> x0, matrix products: 3.48 us -> none  [per_device(): partial = jnp.dot(adjacency, window, preferred_element_type=F32)]
    all_to_all x2, starting transfers between devices: 15.1 us -> 11.7 us  [copies_to(): lax.all_to_all(jnp.broadcast_to(block[None], (count,) + block.shape), axi...]
    ppermute x4, waiting for transfers between devices: 5.29 us -> 2.87 us  [shifted(): lax.ppermute(block, ROW, [((i - distance) % N_ROW, i) for i in range(N_RO...]
  transfers between devices with their start and end apart: 9 -> 10, of which waited for: 9 -> 8; matrix products, arithmetic and copies ran while one was open for 4% -> 4% of each run, Pallas kernels for 6% -> 6%
where the time goes in v6:
time: 143 us; the launch traced here: 142 us
  waiting for transfers between devices  44.8 us (31%)
  starting transfers between devices  44.3 us (31%)
  blocking collectives  22.9 us (16%)
  Pallas kernels  13.9 us (10%)
  other arithmetic  7.37 us (5%)
  matrix products  4.7 us (3%)
  local copies, waits for them, and re-layouts  3.28 us (2%)
    all_to_all x1, blocking collectives, per_device(): shares = lax.all_to_all(half.reshape(N_ZH, own_rows, width), 'zh', 0, 0)  18.3 us
    all_to_all x1, waiting for transfers between devices, per_device(): lax.all_to_all(jnp.concatenate([returned, copies], axis=1), COL, 0, 0)  14.9 us
    ppermute x4, starting transfers between devices, shifted(): lax.ppermute(block, ROW, [((i - distance) % N_ROW, i) for i in range(N_RO...  13.9 us
    all_to_all x2, waiting for transfers between devices, copies_to(): lax.all_to_all(jnp.broadcast_to(block[None], (count,) + block.shape), axi...  11.8 us
    all_to_all x2, starting transfers between devices, copies_to(): lax.all_to_all(jnp.broadcast_to(block[None], (count,) + block.shape), axi...  11.7 us
    all_to_all x1, waiting for transfers between devices, per_device(): given = lax.all_to_all(offer, 'zh', 0, 0)  10.7 us
    pallas_call x1, Pallas kernels, arrange(): pl.pallas_call(arrange_kernel, out_shape=(jax.ShapeDtypeStruct((cap * row...  8.61 us
    all_to_all x1, starting transfers between devices, per_device(): window = lax.all_to_all(offer, COL, 0, 0).reshape(-1, width)  5.83 us
  transfers between devices with their start and end apart: 10, of which 8 were waited for; matrix products, arithmetic and copies ran while one was open for 4% of the time, Pallas kernels for 6%

profile of v6, /device:TPU:1, one launch (start us, length us, event | category | flops | bytes accessed | tf_op | source)
XLA Modules:
  0.0 142.1 jit_solution(5020215101252437540)
XLA Ops:
  0.6 0.0 copy-start
  0.6 0.7 convert_rsqrt_fusion
  1.3 0.9 multiply_convert_fusion.2
  2.3 5.0 %collective-permute-start.1 = (bf16[128,256]{1,0:T(8,128)(2,1)S(1)}, bf16[128,256]{1,0:T(8,128)(2,1)S(1)}, u32[]{:S(2)}, u32[]{:S(2)}) collective-permute-start(bf16[128,256]{1,0:T(8,128)(2,1)S(1)} %multiply_convert_fusion.2), channel_id=1, source_target_pairs={{384,0},{448,64},{0,128},{64,192},{128,256},{192,320},{256,384},{3... | collective-permute-start | bytes 196616 | tf_op jit(solution)/shard_map/ppermute | solution.py:123
  7.3 3.2 %collective-permute-start = (bf16[128,256]{1,0:T(8,128)(2,1)S(1)}, bf16[128,256]{1,0:T(8,128)(2,1)S(1)}, u32[]{:S(2)}, u32[]{:S(2)}) collective-permute-start(bf16[128,256]{1,0:T(8,128)(2,1)S(1)} %multiply_convert_fusion.2), channel_id=1, source_target_pairs={{448,0},{0,64},{64,128},{128,192},{192,256},{256,320},{320,384},{3... | collective-permute-start | bytes 196616 | tf_op jit(solution)/shard_map/ppermute | solution.py:123
  10.5 0.2 collective-permute-done.1
  10.7 0.1 broadcast_select_fusion.2
  10.8 0.0 copy-start.2
  10.8 2.7 %collective-permute-done = bf16[128,256]{1,0:T(8,128)(2,1)S(1)} collective-permute-done((bf16[128,256]{1,0:T(8,128)(2,1)S(1)}, bf16[128,256]{1,0:T(8,128)(2,1)S(1)}, u32[]{:S(2)}, u32[]{:S(2)}) %collective-permute-start) | collective-permute-done | bytes 65568 | tf_op jit(solution)/shard_map/ppermute | solution.py:123
  13.6 1.2 pad_maximum_fusion.1
  14.7 5.8 %all-to-all-start = ((bf16[8,2,128,256]{3,2,1,0:T(8,128)(2,1)}), bf16[8,2,128,256]{3,2,1,0:T(8,128)(2,1)S(1)}, u32[]{:S(2)}, u32[]{:S(2)}) async-start(bf16[8,2,128,256]{3,2,1,0:T(8,128)(2,1)} %pad_maximum_fusion.1), calls=%async_computation | async-start | bytes 2097152 | tf_op jit(solution)/shard_map/all_to_all | solution.py:151
  20.6 0.7 copy.10.rows_ref
  21.2 0.6 pad_add_fusion.here_ref
  21.8 8.6 %arrange_tiles.1 = (bf16[1024,2048]{1,0:T(8,128)(2,1)}, bf16[2048,1024]{1,0:T(8,128)(2,1)}) custom-call(s32[1,16,8]{2,1,0:T(8,128)} %copy.10.rows_ref, s32[1,16]{1,0:T(1,128)} %counts_ref.1, s32[2]{0:T(128)} %pad_add_fusion.here_ref, bf16[1,16,8,128,128]{4,3,2,1,0:T(8,128)(2,1)} %tile_hbm.1), custom_call_target="tpu_custom_call" | custom-call | flops 2097152 | bytes 8388608 | tf_op jit(solution)/shard_map/arrange_tiles/pallas_call | solution.py:59
  30.4 3.5 %all-to-all-done = bf16[8,2,128,256]{3,2,1,0:T(8,128)(2,1)S(1)} async-done(((bf16[8,2,128,256]{3,2,1,0:T(8,128)(2,1)}), bf16[8,2,128,256]{3,2,1,0:T(8,128)(2,1)S(1)}, u32[]{:S(2)}, u32[]{:S(2)}) %all-to-all-start) | async-done | bytes 1048608 | tf_op jit(solution)/shard_map/all_to_all | solution.py:151
  33.9 1.1 copy-done.1
  35.0 5.3 %forward_product.1 = (f32[512,256]{1,0:T(8,128)S(1)}, bf16[512,256]{1,0:T(8,128)(2,1)S(1)}) custom-call(bf16[1024,2048]{1,0:T(8,128)(2,1)} %get-tuple-element.7.adjacency_hbm, bf16[2048,256]{1,0:T(8,128)(2,1)} %bitcast.52), custom_call_target="tpu_custom_call" | custom-call | flops 1073741824 | bytes 4194304 | tf_op jit(solution)/shard_map/forward_product/pallas_call | solution.py:101
  40.2 5.3 %collective-permute-start.2 = (bf16[512,256]{1,0:T(8,128)(2,1)S(1)}, bf16[512,256]{1,0:T(8,128)(2,1)S(1)}, u32[]{:S(2)}, u32[]{:S(2)}) collective-permute-start(bf16[512,256]{1,0:T(8,128)(2,1)S(1)} %get-tuple-element.9), channel_id=1, source_target_pairs={{0,1},{1,0},{2,3},{3,2},{4,5},{5,4},{6,7},{7,6},{8,9},{9,8},{10,11... | collective-permute-start | bytes 786440 | tf_op jit(solution)/shard_map/ppermute | solution.py:154
  45.5 1.1 collective-permute-done.2
  46.7 0.1 add_convert_fusion
  46.7 18.3 %all_to_all.30 = bf16[4,128,256]{2,1,0:T(8,128)(2,1)S(1)} all-to-all(bf16[4,128,256]{2,1,0:T(8,128)(2,1)S(1)} %bitcast.59), channel_id=1, replica_groups=mesh['y'=8,'x'=4,'zl'=2,'zh'=4,'core'=2] {'zh'}, dimensions={0} | all-to-all | bytes 524288 | tf_op jit(solution)/shard_map/all_to_all | solution.py:156
  65.0 0.1 fusion.4
  65.1 0.9 multiply_convert_fusion
  66.0 0.2 convolution_convert_fusion.1
  66.2 0.2 fusion
  66.4 0.8 pad_maximum_fusion.2
  67.2 4.0 %all-to-all-start.2 = ((bf16[4,192,256]{2,1,0:T(8,128)(2,1)}), bf16[4,192,256]{2,1,0:T(8,128)(2,1)S(1)}, u32[]{:S(2)}, u32[]{:S(2)}) async-start(bf16[4,192,256]{2,1,0:T(8,128)(2,1)} %pad_maximum_fusion.2), calls=%async_computation.2 | async-start | bytes 786432 | tf_op jit(solution)/shard_map/all_to_all | solution.py:173
  71.2 10.7 %all-to-all-done.2 = bf16[4,192,256]{2,1,0:T(8,128)(2,1)S(1)} async-done(((bf16[4,192,256]{2,1,0:T(8,128)(2,1)}), bf16[4,192,256]{2,1,0:T(8,128)(2,1)S(1)}, u32[]{:S(2)}, u32[]{:S(2)}) %all-to-all-start.2) | async-done | bytes 393248 | tf_op jit(solution)/shard_map/all_to_all | solution.py:173
  82.0 4.6 %all-gather = bf16[1152,256]{1,0:T(8,128)(2,1)S(1)} all-gather(bf16[576,256]{1,0:T(8,128)(2,1)S(1)} %pad_maximum_fusion.3), channel_id=2, replica_groups=mesh['y'=8,'x'=4,'zl'=2,'zh'=4,'core'=2] {'core'}, dimensions={0}, use_global_device_ids=true | all-gather | bytes 884736 | tf_op jit(solution)/shard_map/all_gather | solution.py:177
  86.6 0.7 broadcast_in_dim.79
  87.3 5.7 %all-to-all-start.3 = ((bf16[8,32,256]{2,1,0:T(8,128)(2,1)}), bf16[8,32,256]{2,1,0:T(8,128)(2,1)S(1)}, u32[]{:S(2)}, u32[]{:S(2)}) async-start(bf16[8,32,256]{2,1,0:T(8,128)(2,1)} %broadcast_in_dim.79), calls=%async_computation.3 | async-start | bytes 262144 | tf_op jit(solution)/shard_map/all_to_all | solution.py:127
  93.0 3.4 %convolution_convert_fusion = bf16[2048,256]{1,0:T(8,128)(2,1)S(1)} fusion(bf16[2048,1024]{1,0:T(8,128)(2,1)} %get-tuple-element.10, bf16[1024,256]{1,0:T(8,128)(2,1)S(1)} %bitcast.60), kind=kOutput, calls=%fused_computation | convolution fusion | flops 1074266112 | bytes 5767168 | tf_op jit(solution)/shard_map/dot_general | solution.py:184
  96.5 4.4 %all-to-all-done.3 = bf16[8,32,256]{2,1,0:T(8,128)(2,1)S(1)} async-done(((bf16[8,32,256]{2,1,0:T(8,128)(2,1)}), bf16[8,32,256]{2,1,0:T(8,128)(2,1)S(1)}, u32[]{:S(2)}, u32[]{:S(2)}) %all-to-all-start.3) | async-done | bytes 131104 | tf_op jit(solution)/shard_map/all_to_all | solution.py:127
  100.9 1.1 pad_maximum_fusion
  102.1 3.6 %all-to-all-start.4 = ((bf16[8,288,256]{2,1,0:T(8,128)(2,1)}), bf16[8,288,256]{2,1,0:T(8,128)(2,1)S(1)}, u32[]{:S(2)}, u32[]{:S(2)}) async-start(bf16[8,288,256]{2,1,0:T(8,128)(2,1)} %pad_maximum_fusion), calls=%async_computation.4 | async-start | bytes 2359296 | tf_op jit(solution)/shard_map/all_to_all | solution.py:187
  105.6 14.9 %all-to-all-done.4 = bf16[8,288,256]{2,1,0:T(8,128)(2,1)S(1)} async-done(((bf16[8,288,256]{2,1,0:T(8,128)(2,1)}), bf16[8,288,256]{2,1,0:T(8,128)(2,1)S(1)}, u32[]{:S(2)}, u32[]{:S(2)}) %all-to-all-start.4) | async-done | bytes 1179680 | tf_op jit(solution)/shard_map/all_to_all | solution.py:187
  120.5 0.1 slice.132
  120.6 0.1 fusion.5
  120.7 0.1 broadcast_select_fusion.1
  120.8 0.1 fusion.6
  120.9 3.7 %collective-permute-start.4 = (bf16[128,256]{1,0:T(8,128)(2,1)S(1)}, bf16[128,256]{1,0:T(8,128)(2,1)S(1)}, u32[]{:S(2)}, u32[]{:S(2)}) collective-permute-start(bf16[128,256]{1,0:T(8,128)(2,1)S(1)} %fusion.6), channel_id=1, source_target_pairs={{128,0},{192,64},{256,128},{320,192},{384,256},{448,320},{0,384},{... | collective-permute-start | bytes 196616 | tf_op jit(solution)/shard_map/ppermute | solution.py:123
  124.6 1.9 %collective-permute-start.3 = (bf16[128,256]{1,0:T(8,128)(2,1)S(1)}, bf16[128,256]{1,0:T(8,128)(2,1)S(1)}, u32[]{:S(2)}, u32[]{:S(2)}) collective-permute-start(bf16[128,256]{1,0:T(8,128)(2,1)S(1)} %fusion.5), channel_id=1, source_target_pairs={{64,0},{128,64},{192,128},{256,192},{320,256},{384,320},{448,384},... | collective-permute-start | bytes 196616 | tf_op jit(solution)/shard_map/ppermute | solution.py:123
  126.6 0.7 broadcast_in_dim.83
  127.2 6.0 %all-to-all-start.5 = ((bf16[8,32,256]{2,1,0:T(8,128)(2,1)}), bf16[8,32,256]{2,1,0:T(8,128)(2,1)S(1)}, u32[]{:S(2)}, u32[]{:S(2)}) async-start(bf16[8,32,256]{2,1,0:T(8,128)(2,1)} %broadcast_in_dim.83), calls=%async_computation.5 | async-start | bytes 262144 | tf_op jit(solution)/shard_map/all_to_all | solution.py:127
  133.3 0.0 collective-permute-done.4
  133.3 0.7 fusion.3
  134.0 7.4 %all-to-all-done.5 = bf16[8,32,256]{2,1,0:T(8,128)(2,1)S(1)} async-done(((bf16[8,32,256]{2,1,0:T(8,128)(2,1)}), bf16[8,32,256]{2,1,0:T(8,128)(2,1)S(1)}, u32[]{:S(2)}, u32[]{:S(2)}) %all-to-all-start.5) | async-done | bytes 131104 | tf_op jit(solution)/shard_map/all_to_all | solution.py:127
  141.4 0.7 bitcast_convert_fusion
  (19 shorter events, 0.3 us)
Async XLA Ops:
  0.6 64.5 %copy-start = (bf16[256,256]{1,0:T(8,128)(2,1)S(1)}, bf16[256,256]{1,0:T(8,128)(2,1)}, u32[]{:S(2)}) copy-start(bf16[256,256]{1,0:T(8,128)(2,1)} %param.12) | copy-start | bytes 393220
  2.3 8.5 %collective-permute-start.1 = (bf16[128,256]{1,0:T(8,128)(2,1)S(1)}, bf16[128,256]{1,0:T(8,128)(2,1)S(1)}, u32[]{:S(2)}, u32[]{:S(2)}) collective-permute-start(bf16[128,256]{1,0:T(8,128)(2,1)S(1)} %multiply_convert_fusion.2), channel_id=1, source_target_pairs={{384,0},{448,64},{0,128},{64,192},{128,256},{192,320},{256,384},{3... | collective-permute-start | bytes 196616 | tf_op jit(solution)/shard_map/ppermute | solution.py:123
  7.3 6.2 %collective-permute-start = (bf16[128,256]{1,0:T(8,128)(2,1)S(1)}, bf16[128,256]{1,0:T(8,128)(2,1)S(1)}, u32[]{:S(2)}, u32[]{:S(2)}) collective-permute-start(bf16[128,256]{1,0:T(8,128)(2,1)S(1)} %multiply_convert_fusion.2), channel_id=1, source_target_pairs={{448,0},{0,64},{64,128},{128,192},{192,256},{256,320},{320,384},{3... | collective-permute-start | bytes 196616 | tf_op jit(solution)/shard_map/ppermute | solution.py:123
  10.8 9.7 %copy-start.2 = (s32[1,16,8]{1,2,0:T(8,128)S(1)}, s32[1,16,8]{1,2,0:T(8,128)}, u32[]{:S(2)}) copy-start(s32[1,16,8]{1,2,0:T(8,128)} %param.10) | copy-start | bytes 1540
  14.7 19.2 %all-to-all-start = ((bf16[8,2,128,256]{3,2,1,0:T(8,128)(2,1)}), bf16[8,2,128,256]{3,2,1,0:T(8,128)(2,1)S(1)}, u32[]{:S(2)}, u32[]{:S(2)}) async-start(bf16[8,2,128,256]{3,2,1,0:T(8,128)(2,1)} %pad_maximum_fusion.1), calls=%async_computation | async-start | bytes 2097152 | tf_op jit(solution)/shard_map/all_to_all | solution.py:151
  33.9 1.1 copy-start.1
  35.0 30.2 %copy-start.3 = (bf16[128,256]{1,0:T(8,128)(2,1)S(1)}, bf16[128,256]{1,0:T(8,128)(2,1)}, u32[]{:S(2)}) copy-start(bf16[128,256]{1,0:T(8,128)(2,1)} %param.13) | copy-start | bytes 196612
  40.2 6.4 %collective-permute-start.2 = (bf16[512,256]{1,0:T(8,128)(2,1)S(1)}, bf16[512,256]{1,0:T(8,128)(2,1)S(1)}, u32[]{:S(2)}, u32[]{:S(2)}) collective-permute-start(bf16[512,256]{1,0:T(8,128)(2,1)S(1)} %get-tuple-element.9), channel_id=1, source_target_pairs={{0,1},{1,0},{2,3},{3,2},{4,5},{5,4},{6,7},{7,6},{8,9},{9,8},{10,11... | collective-permute-start | bytes 786440 | tf_op jit(solution)/shard_map/ppermute | solution.py:154
  67.2 14.7 %all-to-all-start.2 = ((bf16[4,192,256]{2,1,0:T(8,128)(2,1)}), bf16[4,192,256]{2,1,0:T(8,128)(2,1)S(1)}, u32[]{:S(2)}, u32[]{:S(2)}) async-start(bf16[4,192,256]{2,1,0:T(8,128)(2,1)} %pad_maximum_fusion.2), calls=%async_computation.2 | async-start | bytes 786432 | tf_op jit(solution)/shard_map/all_to_all | solution.py:173
  87.3 13.6 %all-to-all-start.3 = ((bf16[8,32,256]{2,1,0:T(8,128)(2,1)}), bf16[8,32,256]{2,1,0:T(8,128)(2,1)S(1)}, u32[]{:S(2)}, u32[]{:S(2)}) async-start(bf16[8,32,256]{2,1,0:T(8,128)(2,1)} %broadcast_in_dim.79), calls=%async_computation.3 | async-start | bytes 262144 | tf_op jit(solution)/shard_map/all_to_all | solution.py:127
  102.1 18.4 %all-to-all-start.4 = ((bf16[8,288,256]{2,1,0:T(8,128)(2,1)}), bf16[8,288,256]{2,1,0:T(8,128)(2,1)S(1)}, u32[]{:S(2)}, u32[]{:S(2)}) async-start(bf16[8,288,256]{2,1,0:T(8,128)(2,1)} %pad_maximum_fusion), calls=%async_computation.4 | async-start | bytes 2359296 | tf_op jit(solution)/shard_map/all_to_all | solution.py:187
  120.9 12.4 %collective-permute-start.4 = (bf16[128,256]{1,0:T(8,128)(2,1)S(1)}, bf16[128,256]{1,0:T(8,128)(2,1)S(1)}, u32[]{:S(2)}, u32[]{:S(2)}) collective-permute-start(bf16[128,256]{1,0:T(8,128)(2,1)S(1)} %fusion.6), channel_id=1, source_target_pairs={{128,0},{192,64},{256,128},{320,192},{384,256},{448,320},{0,384},{... | collective-permute-start | bytes 196616 | tf_op jit(solution)/shard_map/ppermute | solution.py:123
  124.6 8.6 %collective-permute-start.3 = (bf16[128,256]{1,0:T(8,128)(2,1)S(1)}, bf16[128,256]{1,0:T(8,128)(2,1)S(1)}, u32[]{:S(2)}, u32[]{:S(2)}) collective-permute-start(bf16[128,256]{1,0:T(8,128)(2,1)S(1)} %fusion.5), channel_id=1, source_target_pairs={{64,0},{128,64},{192,128},{256,192},{320,256},{384,320},{448,384},... | collective-permute-start | bytes 196616 | tf_op jit(solution)/shard_map/ppermute | solution.py:123
  127.2 14.1 %all-to-all-start.5 = ((bf16[8,32,256]{2,1,0:T(8,128)(2,1)}), bf16[8,32,256]{2,1,0:T(8,128)(2,1)S(1)}, u32[]{:S(2)}, u32[]{:S(2)}) async-start(bf16[8,32,256]{2,1,0:T(8,128)(2,1)} %broadcast_in_dim.83), calls=%async_computation.5 | async-start | bytes 262144 | tf_op jit(solution)/shard_map/all_to_all | solution.py:127

commit v7 on v4

--- a/solution.py
+++ b/solution.py
@@ -127,23 +127,23 @@
     offer = jnp.concatenate([copies, local_weight.reshape(N_ZH, -1, width)], axis=1)
     given = lax.all_to_all(offer, "zh", 0, 0)
     along_zh = given[:, :own_rows].reshape(-1, width)
-    weight_rows = summed_in_f32(given[:, own_rows:])
-    share = weight_rows.shape[0]
-    slab_grads = lax.all_gather(along_zh, "core", axis=0, tiled=True)
+    weight_part = summed_in_f32(given[:, own_rows:]).astype(BF)
+    zh_rows = N_ZH * own_rows
+    pair = lax.all_gather(jnp.concatenate([along_zh, weight_part], axis=0), "core")
+    slab_grads = pair[:, :zh_rows].reshape(-1, width)
+    weight_pair = pair[:, zh_rows:].reshape(N_CORE, N_CORE, -1, width)
+    weight_rows = summed_in_f32(lax.dynamic_index_in_dim(weight_pair, core, 1, keepdims=False))
 
-    along_y = copies_to(weight_rows.astype(BF), ROW, N_ROW)
-    weight_rows = summed_in_f32(along_y).astype(BF)
+    along_col = copies_to(weight_rows.astype(BF), COL, N_COL)
+    weight_rows = summed_in_f32(along_col)
     returned = jnp.dot(flipped, slab_grads, preferred_element_type=F32).astype(BF)
-    returned = returned.reshape(N_COL, 2 * own_rows, width)
-    copies = jnp.broadcast_to(weight_rows[None], (N_COL,) + weight_rows.shape)
-    home = lax.all_to_all(jnp.concatenate([returned, copies], axis=1), COL, 0, 0)
+    arrived = lax.all_to_all(returned.reshape(N_COL, 2, own_rows, width), COL, 0, 0)
+    along_y = lax.all_gather(weight_rows.astype(BF), ROW)
     node_total = own_rows * N_ROW * N_COL * N_REP
-    weight_rows = (summed_in_f32(home[:, 2 * own_rows :]) / math.sqrt(node_total)).astype(BF)
+    weight_rows = (summed_in_f32(along_y) / math.sqrt(node_total)).astype(BF)
     along_rep = copies_to(weight_rows, REP, N_REP)
-    along_rep = along_rep.reshape(N_ZH, N_CORE, share, width).astype(F32)
-    grad_weight = (along_rep[:, 0] + along_rep[:, 1]).reshape(-1, width)
+    grad_weight = along_rep.reshape(-1, width).astype(F32)
 
-    arrived = home[:, : 2 * own_rows].reshape(N_COL, 2, own_rows, width)
     for_one = summed_in_f32(arrived[:, 0]).astype(BF)
     nothing = jnp.zeros((), BF)
     for_two = summed_in_f32(jnp.where(columns < col, arrived[:, 1], nothing)).astype(BF)

time: 136 us -> 139 us (1.022)
  waiting for transfers between devices: 26 us -> 21.3 us
  blocking collectives: 39 us -> 42.7 us
  starting transfers between devices: 44 us -> 47.1 us
    all_gather x1 -> x2, blocking collectives: 5.14 us -> 24.4 us  [the longest x1 19.7 us: per_device(): along_y = lax.all_gather(weight_rows.astype(BF), ROW)]
    all_to_all x1 -> x0, blocking collectives: 15.6 us -> none  [per_device(): given = lax.all_to_all(offer, 'zh', 0, 0)]
    all_to_all x1 -> x2, starting transfers between devices: 3.59 us -> 7.88 us  [the longest x1 4.04 us: per_device(): given = lax.all_to_all(offer, 'zh', 0, 0)]
    all_to_all x1 -> x2, waiting for transfers between devices: 14.4 us -> 10.6 us  [the longest x1 10.6 us: per_device(): given = lax.all_to_all(offer, 'zh', 0, 0)]
    ppermute x4, waiting for transfers between devices: 5.29 us -> 2.88 us  [shifted(): lax.ppermute(block, ROW, [((i - distance) % N_ROW, i) for i in range(N_RO...]
    all_to_all x2, starting transfers between devices: 15.1 us -> 13.4 us  [copies_to(): lax.all_to_all(jnp.broadcast_to(block[None], (count,) + block.shape), axi...]
    all_to_all x2, waiting for transfers between devices: 1.67 us -> 3.12 us  [copies_to(): lax.all_to_all(jnp.broadcast_to(block[None], (count,) + block.shape), axi...]
  transfers between devices with their start and end apart: 9 -> 10, of which waited for: 9 -> 7; matrix products, arithmetic and copies ran while one was open for 4% -> 5% of each run, Pallas kernels for 6% -> 6%
where the time goes in v7:
time: 139 us; the launch traced here: 138 us
  starting transfers between devices  47.1 us (34%)
  blocking collectives  42.7 us (31%)
  waiting for transfers between devices  21.3 us (15%)
  matrix products  9.15 us (7%)
  Pallas kernels  8.59 us (6%)
  other arithmetic  6.28 us (5%)
  local copies, waits for them, and re-layouts  2.16 us (2%)
    all_gather x1, blocking collectives, per_device(): along_y = lax.all_gather(weight_rows.astype(BF), ROW)  19.7 us
    all_to_all x1, blocking collectives, per_device(): shares = lax.all_to_all(half.reshape(N_ZH, own_rows, width), 'zh', 0, 0)  18.3 us
    ppermute x4, starting transfers between devices, shifted(): lax.ppermute(block, ROW, [((i - distance) % N_ROW, i) for i in range(N_RO...  14.7 us
    all_to_all x2, starting transfers between devices, copies_to(): lax.all_to_all(jnp.broadcast_to(block[None], (count,) + block.shape), axi...  13.4 us
    all_to_all x1, waiting for transfers between devices, per_device(): given = lax.all_to_all(offer, 'zh', 0, 0)  10.6 us
    pallas_call x1, Pallas kernels, arrange(): pl.pallas_call(arrange_kernel, out_shape=(jax.ShapeDtypeStruct((cap * row...  8.59 us
    all_to_all x1, starting transfers between devices, per_device(): window = lax.all_to_all(offer, COL, 0, 0).reshape(-1, width)  5.83 us
    ppermute x1, starting transfers between devices, per_device(): other = lax.ppermute(sent.astype(BF), 'core', [(0, 1), (1, 0)])  5.27 us
  transfers between devices with their start and end apart: 10, of which 7 were waited for; matrix products, arithmetic and copies ran while one was open for 5% of the time, Pallas kernels for 6%

profile of v7, /device:TPU:1, one launch (start us, length us, event | category | flops | bytes accessed | tf_op | source)
XLA Modules:
  0.0 138.1 jit_solution(11735255095464034438)
XLA Ops:
  0.6 0.0 copy-start
  0.7 0.7 convert_rsqrt_fusion
  1.4 0.9 multiply_convert_fusion.2
  2.3 5.0 %collective-permute-start.1 = (bf16[128,256]{1,0:T(8,128)(2,1)S(1)}, bf16[128,256]{1,0:T(8,128)(2,1)S(1)}, u32[]{:S(2)}, u32[]{:S(2)}) collective-permute-start(bf16[128,256]{1,0:T(8,128)(2,1)S(1)} %multiply_convert_fusion.2), channel_id=1, source_target_pairs={{384,0},{448,64},{0,128},{64,192},{128,256},{192,320},{256,384},{3... | collective-permute-start | bytes 196616 | tf_op jit(solution)/shard_map/ppermute | solution.py:77
  7.3 3.2 %collective-permute-start = (bf16[128,256]{1,0:T(8,128)(2,1)S(1)}, bf16[128,256]{1,0:T(8,128)(2,1)S(1)}, u32[]{:S(2)}, u32[]{:S(2)}) collective-permute-start(bf16[128,256]{1,0:T(8,128)(2,1)S(1)} %multiply_convert_fusion.2), channel_id=1, source_target_pairs={{448,0},{0,64},{64,128},{128,192},{192,256},{256,320},{320,384},{3... | collective-permute-start | bytes 196616 | tf_op jit(solution)/shard_map/ppermute | solution.py:77
  10.6 0.2 collective-permute-done.1
  10.7 0.1 broadcast_select_fusion.2
  10.9 2.7 %collective-permute-done = bf16[128,256]{1,0:T(8,128)(2,1)S(1)} collective-permute-done((bf16[128,256]{1,0:T(8,128)(2,1)S(1)}, bf16[128,256]{1,0:T(8,128)(2,1)S(1)}, u32[]{:S(2)}, u32[]{:S(2)}) %collective-permute-start) | collective-permute-done | bytes 65568 | tf_op jit(solution)/shard_map/ppermute | solution.py:77
  13.6 1.2 pad_maximum_fusion
  14.8 5.8 %all-to-all-start = ((bf16[8,2,128,256]{3,2,1,0:T(8,128)(2,1)}), bf16[8,2,128,256]{3,2,1,0:T(8,128)(2,1)S(1)}, u32[]{:S(2)}, u32[]{:S(2)}) async-start(bf16[8,2,128,256]{3,2,1,0:T(8,128)(2,1)} %pad_maximum_fusion), calls=%async_computation | async-start | bytes 2097152 | tf_op jit(solution)/shard_map/all_to_all | solution.py:105
  20.6 0.7 copy.11.rows_ref
  21.3 0.6 pad_add_fusion.here_ref
  21.9 8.6 %arrange_tiles.1 = (bf16[1024,2048]{1,0:T(8,128)(2,1)}, bf16[2048,1024]{1,0:T(8,128)(2,1)}) custom-call(s32[1,16,8]{2,1,0:T(8,128)} %copy.11.rows_ref, s32[1,16]{1,0:T(1,128)} %counts_ref.1, s32[2]{0:T(128)} %pad_add_fusion.here_ref, bf16[1,16,8,128,128]{4,3,2,1,0:T(8,128)(2,1)} %tile_hbm.1), custom_call_target="tpu_custom_call" | custom-call | flops 2097152 | bytes 8388608 | tf_op jit(solution)/shard_map/arrange_tiles/pallas_call | solution.py:59
  30.4 3.5 %all-to-all-done = bf16[8,2,128,256]{3,2,1,0:T(8,128)(2,1)S(1)} async-done(((bf16[8,2,128,256]{3,2,1,0:T(8,128)(2,1)}), bf16[8,2,128,256]{3,2,1,0:T(8,128)(2,1)S(1)}, u32[]{:S(2)}, u32[]{:S(2)}) %all-to-all-start) | async-done | bytes 1048608 | tf_op jit(solution)/shard_map/all_to_all | solution.py:105
  33.9 3.5 %fusion.11 = f32[1024,256]{1,0:T(8,128)S(1)} fusion(bf16[1024,2048]{1,0:T(8,128)(2,1)} %get-tuple-element.5, bf16[2048,256]{1,0:T(8,128)(2,1)S(1)} %bitcast.53), kind=kOutput, calls=%fused_computation.40 | convolution fusion | flops 1073741824 | bytes 6291456 | tf_op jit(solution)/shard_map/dot_general | solution.py:107
  37.5 5.3 %collective-permute-start.2 = (bf16[512,256]{1,0:T(8,128)(2,1)S(1)}, bf16[512,256]{1,0:T(8,128)(2,1)S(1)}, u32[]{:S(2)}, u32[]{:S(2)}) collective-permute-start(bf16[512,256]{1,0:T(8,128)(2,1)S(1)} %split.15), channel_id=1, source_target_pairs={{0,1},{1,0},{2,3},{3,2},{4,5},{5,4},{6,7},{7,6},{8,9},{9,8},{10,11... | collective-permute-start | bytes 786440 | tf_op jit(solution)/shard_map/ppermute | solution.py:109
  42.7 1.1 collective-permute-done.2
  43.9 0.1 fusion.1
  43.9 18.3 %all_to_all.30 = bf16[4,128,256]{2,1,0:T(8,128)(2,1)S(1)} all-to-all(bf16[4,128,256]{2,1,0:T(8,128)(2,1)S(1)} %bitcast.55), channel_id=1, replica_groups=mesh['y'=8,'x'=4,'zl'=2,'zh'=4,'core'=2] {'zh'}, dimensions={0} | all-to-all | bytes 524288 | tf_op jit(solution)/shard_map/all_to_all | solution.py:111
  62.2 0.1 fusion.5
  62.3 0.0 copy-done
  62.3 0.0 copy-done.2
  62.4 0.9 multiply_convert_fusion
  63.2 0.2 convolution_convert_fusion.1
  63.4 0.2 fusion
  63.7 0.8 pad_maximum_fusion.1
  64.4 4.0 %all-to-all-start.2 = ((bf16[4,192,256]{2,1,0:T(8,128)(2,1)}), bf16[4,192,256]{2,1,0:T(8,128)(2,1)S(1)}, u32[]{:S(2)}, u32[]{:S(2)}) async-start(bf16[4,192,256]{2,1,0:T(8,128)(2,1)} %pad_maximum_fusion.1), calls=%async_computation.2 | async-start | bytes 786432 | tf_op jit(solution)/shard_map/all_to_all | solution.py:128
  68.5 10.6 %all-to-all-done.2 = bf16[4,192,256]{2,1,0:T(8,128)(2,1)S(1)} async-done(((bf16[4,192,256]{2,1,0:T(8,128)(2,1)}), bf16[4,192,256]{2,1,0:T(8,128)(2,1)S(1)}, u32[]{:S(2)}, u32[]{:S(2)}) %all-to-all-start.2) | async-done | bytes 393248 | tf_op jit(solution)/shard_map/all_to_all | solution.py:128
  79.2 4.7 %all-gather = bf16[1152,256]{1,0:T(8,128)(2,1)S(1)} all-gather(bf16[576,256]{1,0:T(8,128)(2,1)S(1)} %pad_maximum_fusion.2), channel_id=2, replica_groups=mesh['y'=8,'x'=4,'zl'=2,'zh'=4,'core'=2] {'core'}, dimensions={0}, use_global_device_ids=true | all-gather | bytes 884736 | tf_op jit(solution)/shard_map/all_gather | solution.py:132
  83.9 0.7 broadcast_in_dim.71
  84.6 3.4 %all-to-all-start.3 = ((bf16[8,32,256]{2,1,0:T(8,128)(2,1)}), bf16[8,32,256]{2,1,0:T(8,128)(2,1)S(1)}, u32[]{:S(2)}, u32[]{:S(2)}) async-start(bf16[8,32,256]{2,1,0:T(8,128)(2,1)} %broadcast_in_dim.71), calls=%async_computation.3 | async-start | bytes 262144 | tf_op jit(solution)/shard_map/all_to_all | solution.py:81
  88.0 4.4 %convolution_convert_fusion = bf16[2048,256]{1,0:T(8,128)(2,1)} fusion(bf16[2048,1024]{1,0:T(8,128)(2,1)} %get-tuple-element.6, bf16[1024,256]{1,0:T(8,128)(2,1)S(1)} %bitcast.56), kind=kOutput, calls=%fused_computation | convolution fusion | flops 1074266112 | bytes 5767168 | tf_op jit(solution)/shard_map/dot_general | solution.py:139
  92.4 1.2 all-to-all-done.3
  93.6 3.8 %all-to-all-start.5 = ((bf16[8,2,128,256]{3,2,1,0:T(8,128)(2,1)}), bf16[8,2,128,256]{3,2,1,0:T(8,128)(2,1)S(1)}, u32[]{:S(2)}, u32[]{:S(2)}) async-start(bf16[8,2,128,256]{3,2,1,0:T(8,128)(2,1)} %bitcast.14), calls=%async_computation.5 | async-start | bytes 2097152 | tf_op jit(solution)/shard_map/all_to_all | solution.py:140
  97.5 19.7 %all_gather.12 = bf16[8,32,256]{2,1,0:T(8,128)(2,1)S(1)} all-gather(bf16[1,32,256]{2,1,0:T(8,128)(2,1)S(1)} %add_convert_fusion.3), channel_id=1, replica_groups=mesh['y'=8,'x'=4,'zl'=2,'zh'=4,'core'=2] {'y'}, dimensions={0}, use_global_device_ids=true | all-gather | bytes 147456 | tf_op jit(solution)/shard_map/all_gather | solution.py:141
  117.2 0.0 all-to-all-done.5
  117.2 0.7 broadcast_in_dim.73
  117.9 10.0 %all-to-all-start.4 = ((bf16[8,32,256]{2,1,0:T(8,128)(2,1)}), bf16[8,32,256]{2,1,0:T(8,128)(2,1)S(1)}, u32[]{:S(2)}, u32[]{:S(2)}) async-start(bf16[8,32,256]{2,1,0:T(8,128)(2,1)} %broadcast_in_dim.73), calls=%async_computation.4 | async-start | bytes 262144 | tf_op jit(solution)/shard_map/all_to_all | solution.py:81
  127.9 0.1 broadcast_select_fusion.1
  128.1 0.1 fusion.7
  128.2 3.8 %collective-permute-start.4 = (bf16[128,256]{1,0:T(8,128)(2,1)S(1)}, bf16[128,256]{1,0:T(8,128)(2,1)S(1)}, u32[]{:S(2)}, u32[]{:S(2)}) collective-permute-start(bf16[128,256]{1,0:T(8,128)(2,1)S(1)} %fusion.7), channel_id=1, source_target_pairs={{128,0},{192,64},{256,128},{320,192},{384,256},{448,320},{0,384},{... | collective-permute-start | bytes 196616 | tf_op jit(solution)/shard_map/ppermute | solution.py:77
  131.9 0.1 fusion.6
  132.0 2.7 %collective-permute-start.3 = (bf16[128,256]{1,0:T(8,128)(2,1)S(1)}, bf16[128,256]{1,0:T(8,128)(2,1)S(1)}, u32[]{:S(2)}, u32[]{:S(2)}) collective-permute-start(bf16[128,256]{1,0:T(8,128)(2,1)S(1)} %fusion.6), channel_id=1, source_target_pairs={{64,0},{128,64},{192,128},{256,192},{320,256},{384,320},{448,384},... | collective-permute-start | bytes 196616 | tf_op jit(solution)/shard_map/ppermute | solution.py:77
  134.7 1.9 %all-to-all-done.4 = bf16[8,32,256]{2,1,0:T(8,128)(2,1)S(1)} async-done(((bf16[8,32,256]{2,1,0:T(8,128)(2,1)}), bf16[8,32,256]{2,1,0:T(8,128)(2,1)S(1)}, u32[]{:S(2)}, u32[]{:S(2)}) %all-to-all-start.4) | async-done | bytes 131104 | tf_op jit(solution)/shard_map/all_to_all | solution.py:81
  136.6 0.7 bitcast_convert_fusion
  137.4 0.0 collective-permute-done.4
  137.4 0.0 collective-permute-done.3
  137.4 0.7 fusion.4
  (16 shorter events, 0.3 us)
Async XLA Ops:
  0.6 61.7 %copy-start = (bf16[256,256]{1,0:T(8,128)(2,1)S(1)}, bf16[256,256]{1,0:T(8,128)(2,1)}, u32[]{:S(2)}) copy-start(bf16[256,256]{1,0:T(8,128)(2,1)} %param.12) | copy-start | bytes 393220
  0.6 19.9 %copy-start.1 = (s32[1,16,8]{1,2,0:T(8,128)S(1)}, s32[1,16,8]{1,2,0:T(8,128)}, u32[]{:S(2)}) copy-start(s32[1,16,8]{1,2,0:T(8,128)} %param.10) | copy-start | bytes 1540
  2.3 8.5 %collective-permute-start.1 = (bf16[128,256]{1,0:T(8,128)(2,1)S(1)}, bf16[128,256]{1,0:T(8,128)(2,1)S(1)}, u32[]{:S(2)}, u32[]{:S(2)}) collective-permute-start(bf16[128,256]{1,0:T(8,128)(2,1)S(1)} %multiply_convert_fusion.2), channel_id=1, source_target_pairs={{384,0},{448,64},{0,128},{64,192},{128,256},{192,320},{256,384},{3... | collective-permute-start | bytes 196616 | tf_op jit(solution)/shard_map/ppermute | solution.py:77
  7.3 6.2 %collective-permute-start = (bf16[128,256]{1,0:T(8,128)(2,1)S(1)}, bf16[128,256]{1,0:T(8,128)(2,1)S(1)}, u32[]{:S(2)}, u32[]{:S(2)}) collective-permute-start(bf16[128,256]{1,0:T(8,128)(2,1)S(1)} %multiply_convert_fusion.2), channel_id=1, source_target_pairs={{448,0},{0,64},{64,128},{128,192},{192,256},{256,320},{320,384},{3... | collective-permute-start | bytes 196616 | tf_op jit(solution)/shard_map/ppermute | solution.py:77
  14.8 19.2 %all-to-all-start = ((bf16[8,2,128,256]{3,2,1,0:T(8,128)(2,1)}), bf16[8,2,128,256]{3,2,1,0:T(8,128)(2,1)S(1)}, u32[]{:S(2)}, u32[]{:S(2)}) async-start(bf16[8,2,128,256]{3,2,1,0:T(8,128)(2,1)} %pad_maximum_fusion), calls=%async_computation | async-start | bytes 2097152 | tf_op jit(solution)/shard_map/all_to_all | solution.py:105
  33.9 28.4 %copy-start.2 = (bf16[128,256]{1,0:T(8,128)(2,1)S(1)}, bf16[128,256]{1,0:T(8,128)(2,1)}, u32[]{:S(2)}) copy-start(bf16[128,256]{1,0:T(8,128)(2,1)} %param.13) | copy-start | bytes 196612
  37.5 6.4 %collective-permute-start.2 = (bf16[512,256]{1,0:T(8,128)(2,1)S(1)}, bf16[512,256]{1,0:T(8,128)(2,1)S(1)}, u32[]{:S(2)}, u32[]{:S(2)}) collective-permute-start(bf16[512,256]{1,0:T(8,128)(2,1)S(1)} %split.15), channel_id=1, source_target_pairs={{0,1},{1,0},{2,3},{3,2},{4,5},{5,4},{6,7},{7,6},{8,9},{9,8},{10,11... | collective-permute-start | bytes 786440 | tf_op jit(solution)/shard_map/ppermute | solution.py:109
  64.4 14.7 %all-to-all-start.2 = ((bf16[4,192,256]{2,1,0:T(8,128)(2,1)}), bf16[4,192,256]{2,1,0:T(8,128)(2,1)S(1)}, u32[]{:S(2)}, u32[]{:S(2)}) async-start(bf16[4,192,256]{2,1,0:T(8,128)(2,1)} %pad_maximum_fusion.1), calls=%async_computation.2 | async-start | bytes 786432 | tf_op jit(solution)/shard_map/all_to_all | solution.py:128
  84.6 9.0 %all-to-all-start.3 = ((bf16[8,32,256]{2,1,0:T(8,128)(2,1)}), bf16[8,32,256]{2,1,0:T(8,128)(2,1)S(1)}, u32[]{:S(2)}, u32[]{:S(2)}) async-start(bf16[8,32,256]{2,1,0:T(8,128)(2,1)} %broadcast_in_dim.71), calls=%async_computation.3 | async-start | bytes 262144 | tf_op jit(solution)/shard_map/all_to_all | solution.py:81
  93.6 23.6 %all-to-all-start.5 = ((bf16[8,2,128,256]{3,2,1,0:T(8,128)(2,1)}), bf16[8,2,128,256]{3,2,1,0:T(8,128)(2,1)S(1)}, u32[]{:S(2)}, u32[]{:S(2)}) async-start(bf16[8,2,128,256]{3,2,1,0:T(8,128)(2,1)} %bitcast.14), calls=%async_computation.5 | async-start | bytes 2097152 | tf_op jit(solution)/shard_map/all_to_all | solution.py:140
  117.9 18.7 %all-to-all-start.4 = ((bf16[8,32,256]{2,1,0:T(8,128)(2,1)}), bf16[8,32,256]{2,1,0:T(8,128)(2,1)S(1)}, u32[]{:S(2)}, u32[]{:S(2)}) async-start(bf16[8,32,256]{2,1,0:T(8,128)(2,1)} %broadcast_in_dim.73), calls=%async_computation.4 | async-start | bytes 262144 | tf_op jit(solution)/shard_map/all_to_all | solution.py:81
  128.2 9.2 %collective-permute-start.4 = (bf16[128,256]{1,0:T(8,128)(2,1)S(1)}, bf16[128,256]{1,0:T(8,128)(2,1)S(1)}, u32[]{:S(2)}, u32[]{:S(2)}) collective-permute-start(bf16[128,256]{1,0:T(8,128)(2,1)S(1)} %fusion.7), channel_id=1, source_target_pairs={{128,0},{192,64},{256,128},{320,192},{384,256},{448,320},{0,384},{... | collective-permute-start | bytes 196616 | tf_op jit(solution)/shard_map/ppermute | solution.py:77
  132.0 5.4 %collective-permute-start.3 = (bf16[128,256]{1,0:T(8,128)(2,1)S(1)}, bf16[128,256]{1,0:T(8,128)(2,1)S(1)}, u32[]{:S(2)}, u32[]{:S(2)}) collective-permute-start(bf16[128,256]{1,0:T(8,128)(2,1)S(1)} %fusion.6), channel_id=1, source_target_pairs={{64,0},{128,64},{192,128},{256,192},{320,256},{384,320},{448,384},... | collective-permute-start | bytes 196616 | tf_op jit(solution)/shard_map/ppermute | solution.py:77

commit v8 on v7

--- a/solution.py
+++ b/solution.py
@@ -10,8 +10,8 @@
 
 BF = jnp.bfloat16
 F32 = jnp.float32
-ROW, COL, REP = "y", ("x", "zl"), ("zh", "core")
-N_ROW, N_COL, N_ZH, N_CORE = 8, 8, 4, 2
+ROW, COL, REP = ("yp", "ye"), ("x", "zl"), ("zh", "core")
+N_PAIR, N_ROW, N_COL, N_ZH, N_CORE = 4, 8, 8, 4, 2
 N_REP = N_ZH * N_CORE
 
 
@@ -134,13 +134,17 @@
     weight_pair = pair[:, zh_rows:].reshape(N_CORE, N_CORE, -1, width)
     weight_rows = summed_in_f32(lax.dynamic_index_in_dim(weight_pair, core, 1, keepdims=False))
 
-    along_col = copies_to(weight_rows.astype(BF), COL, N_COL)
+    along_col = copies_to(weight_rows.astype(BF), ("ye",) + COL, N_ROW // N_PAIR * N_COL)
     weight_rows = summed_in_f32(along_col)
     returned = jnp.dot(flipped, slab_grads, preferred_element_type=F32).astype(BF)
     arrived = lax.all_to_all(returned.reshape(N_COL, 2, own_rows, width), COL, 0, 0)
-    along_y = lax.all_gather(weight_rows.astype(BF), ROW)
+    own_part = weight_rows.astype(BF)
+    parts = [own_part]
+    for away in range(1, N_PAIR):
+        route = [((i - away) % N_PAIR, i) for i in range(N_PAIR)]
+        parts.append(lax.ppermute(own_part, "yp", route))
     node_total = own_rows * N_ROW * N_COL * N_REP
-    weight_rows = (summed_in_f32(along_y) / math.sqrt(node_total)).astype(BF)
+    weight_rows = (summed_in_f32(parts) / math.sqrt(node_total)).astype(BF)
     along_rep = copies_to(weight_rows, REP, N_REP)
     grad_weight = along_rep.reshape(-1, width).astype(F32)
 
@@ -157,9 +161,9 @@
 
 def solution(mesh):
     fine = Mesh(
-        mesh.devices.reshape(N_ROW, 4, 2, N_ZH, N_CORE), ("y", "x", "zl", "zh", "core")
+        mesh.devices.reshape(N_PAIR, 2, 4, 2, N_ZH, N_CORE), ROW + COL + REP
     )
-    nodes = ("y", "x", "zl", "zh", "core")
+    nodes = ROW + COL + REP
     placed = (
         P(nodes, None),
         P(nodes),

time: 139 us -> 134 us (0.964)
  blocking collectives: 42.7 us -> 23 us
  starting transfers between devices: 47.1 us -> 58.9 us
  waiting for transfers between devices: 21.3 us -> 23.6 us
    all_gather x1 -> x0, blocking collectives: 19.7 us -> none  [per_device(): along_y = lax.all_gather(weight_rows.astype(BF), ROW)]
    ppermute x0 -> x3, starting transfers between devices: none -> 13.7 us  [per_device(): parts.append(lax.ppermute(own_part, 'yp', route))]
    all_to_all x2, starting transfers between devices: 13.4 us -> 10.3 us  [copies_to(): lax.all_to_all(jnp.broadcast_to(block[None], (count,) + block.shape), axi...]
    ppermute x4, waiting for transfers between devices: 2.88 us -> 4.78 us  [shifted(): lax.ppermute(block, ROW, [((i - distance) % N_ROW, i) for i in range(N_RO...]
    ppermute x4, starting transfers between devices: 14.7 us -> 16.2 us  [shifted(): lax.ppermute(block, ROW, [((i - distance) % N_ROW, i) for i in range(N_RO...]
  transfers between devices with their start and end apart: 10 -> 13, of which waited for: 7 -> 9; matrix products, arithmetic and copies ran while one was open for 5% -> 5% of each run, Pallas kernels for 6% -> 7%
where the time goes in v8:
time: 134 us; the launch traced here: 133 us
  starting transfers between devices  58.9 us (44%)
  waiting for transfers between devices  23.6 us (18%)
  blocking collectives  23 us (17%)
  matrix products  9.16 us (7%)
  Pallas kernels  8.63 us (6%)
  other arithmetic  6.3 us (5%)
  local copies, waits for them, and re-layouts  2.23 us (2%)
    all_to_all x1, blocking collectives, per_device(): shares = lax.all_to_all(half.reshape(N_ZH, own_rows, width), 'zh', 0, 0)  18.3 us
    ppermute x4, starting transfers between devices, shifted(): lax.ppermute(block, ROW, [((i - distance) % N_ROW, i) for i in range(N_RO...  16.2 us
    ppermute x3, starting transfers between devices, per_device(): parts.append(lax.ppermute(own_part, 'yp', route))  13.7 us
    all_to_all x1, waiting for transfers between devices, per_device(): given = lax.all_to_all(offer, 'zh', 0, 0)  10.6 us
    all_to_all x2, starting transfers between devices, copies_to(): lax.all_to_all(jnp.broadcast_to(block[None], (count,) + block.shape), axi...  10.3 us
    pallas_call x1, Pallas kernels, arrange(): pl.pallas_call(arrange_kernel, out_shape=(jax.ShapeDtypeStruct((cap * row...  8.63 us
    all_to_all x1, starting transfers between devices, per_device(): window = lax.all_to_all(offer, COL, 0, 0).reshape(-1, width)  5.83 us
    ppermute x1, starting transfers between devices, per_device(): other = lax.ppermute(sent.astype(BF), 'core', [(0, 1), (1, 0)])  5.26 us
  transfers between devices with their start and end apart: 13, of which 9 were waited for; matrix products, arithmetic and copies ran while one was open for 5% of the time, Pallas kernels for 7%

profile of v8, /device:TPU:1, one launch (start us, length us, event | category | flops | bytes accessed | tf_op | source)
XLA Modules:
  0.0 132.7 jit_solution(6853780104291010317)
XLA Ops:
  0.6 0.0 copy-start
  0.7 0.7 convert_rsqrt_fusion
  1.4 0.9 multiply_convert_fusion.2
  2.3 5.0 %collective-permute-start.1 = (bf16[128,256]{1,0:T(8,128)(2,1)S(1)}, bf16[128,256]{1,0:T(8,128)(2,1)S(1)}, u32[]{:S(2)}, u32[]{:S(2)}) collective-permute-start(bf16[128,256]{1,0:T(8,128)(2,1)S(1)} %multiply_convert_fusion.2), channel_id=1, source_target_pairs={{384,0},{448,64},{0,128},{64,192},{128,256},{192,320},{256,384},{3... | collective-permute-start | bytes 196616 | tf_op jit(solution)/shard_map/ppermute | solution.py:77
  7.3 3.2 %collective-permute-start = (bf16[128,256]{1,0:T(8,128)(2,1)S(1)}, bf16[128,256]{1,0:T(8,128)(2,1)S(1)}, u32[]{:S(2)}, u32[]{:S(2)}) collective-permute-start(bf16[128,256]{1,0:T(8,128)(2,1)S(1)} %multiply_convert_fusion.2), channel_id=1, source_target_pairs={{448,0},{0,64},{64,128},{128,192},{192,256},{256,320},{320,384},{3... | collective-permute-start | bytes 196616 | tf_op jit(solution)/shard_map/ppermute | solution.py:77
  10.6 0.2 collective-permute-done.1
  10.7 0.1 broadcast_select_fusion.2
  10.9 2.7 %collective-permute-done = bf16[128,256]{1,0:T(8,128)(2,1)S(1)} collective-permute-done((bf16[128,256]{1,0:T(8,128)(2,1)S(1)}, bf16[128,256]{1,0:T(8,128)(2,1)S(1)}, u32[]{:S(2)}, u32[]{:S(2)}) %collective-permute-start) | collective-permute-done | bytes 65568 | tf_op jit(solution)/shard_map/ppermute | solution.py:77
  13.6 1.1 pad_maximum_fusion
  14.7 5.8 %all-to-all-start = ((bf16[8,2,128,256]{3,2,1,0:T(8,128)(2,1)}), bf16[8,2,128,256]{3,2,1,0:T(8,128)(2,1)S(1)}, u32[]{:S(2)}, u32[]{:S(2)}) async-start(bf16[8,2,128,256]{3,2,1,0:T(8,128)(2,1)} %pad_maximum_fusion), calls=%async_computation | async-start | bytes 2097152 | tf_op jit(solution)/shard_map/all_to_all | solution.py:105
  20.6 0.7 copy.10.rows_ref
  21.2 0.6 pad_add_fusion.here_ref
  21.8 8.6 %arrange_tiles.1 = (bf16[1024,2048]{1,0:T(8,128)(2,1)}, bf16[2048,1024]{1,0:T(8,128)(2,1)}) custom-call(s32[1,16,8]{2,1,0:T(8,128)} %copy.10.rows_ref, s32[1,16]{1,0:T(1,128)} %counts_ref.1, s32[2]{0:T(128)} %pad_add_fusion.here_ref, bf16[1,16,8,128,128]{4,3,2,1,0:T(8,128)(2,1)} %tile_hbm.1), custom_call_target="tpu_custom_call" | custom-call | flops 2097152 | bytes 8388608 | tf_op jit(solution)/shard_map/arrange_tiles/pallas_call | solution.py:59
  30.5 3.4 %all-to-all-done = bf16[8,2,128,256]{3,2,1,0:T(8,128)(2,1)S(1)} async-done(((bf16[8,2,128,256]{3,2,1,0:T(8,128)(2,1)}), bf16[8,2,128,256]{3,2,1,0:T(8,128)(2,1)S(1)}, u32[]{:S(2)}, u32[]{:S(2)}) %all-to-all-start) | async-done | bytes 1048608 | tf_op jit(solution)/shard_map/all_to_all | solution.py:105
  33.9 3.5 %fusion.11 = f32[1024,256]{1,0:T(8,128)S(1)} fusion(bf16[1024,2048]{1,0:T(8,128)(2,1)} %get-tuple-element.5, bf16[2048,256]{1,0:T(8,128)(2,1)S(1)} %bitcast.62), kind=kOutput, calls=%fused_computation.41 | convolution fusion | flops 1073741824 | bytes 6291456 | tf_op jit(solution)/shard_map/dot_general | solution.py:107
  37.4 5.3 %collective-permute-start.2 = (bf16[512,256]{1,0:T(8,128)(2,1)S(1)}, bf16[512,256]{1,0:T(8,128)(2,1)S(1)}, u32[]{:S(2)}, u32[]{:S(2)}) collective-permute-start(bf16[512,256]{1,0:T(8,128)(2,1)S(1)} %split.15), channel_id=1, source_target_pairs={{0,1},{1,0},{2,3},{3,2},{4,5},{5,4},{6,7},{7,6},{8,9},{9,8},{10,11... | collective-permute-start | bytes 786440 | tf_op jit(solution)/shard_map/ppermute | solution.py:109
  42.7 1.1 collective-permute-done.2
  43.8 0.1 fusion.1
  43.9 18.3 %all_to_all.30 = bf16[4,128,256]{2,1,0:T(8,128)(2,1)S(1)} all-to-all(bf16[4,128,256]{2,1,0:T(8,128)(2,1)S(1)} %bitcast.64), channel_id=1, replica_groups=mesh['yp'=4,'ye'=2,'x'=4,'zl'=2,'zh'=4,'core'=2] {'zh'}, dimensions={0} | all-to-all | bytes 524288 | tf_op jit(solution)/shard_map/all_to_all | solution.py:111
  62.2 0.1 fusion.5
  62.3 0.9 multiply_convert_fusion
  63.2 0.2 convolution_convert_fusion.1
  63.4 0.2 fusion
  63.6 0.8 pad_maximum_fusion.1
  64.4 4.0 %all-to-all-start.2 = ((bf16[4,192,256]{2,1,0:T(8,128)(2,1)}), bf16[4,192,256]{2,1,0:T(8,128)(2,1)S(1)}, u32[]{:S(2)}, u32[]{:S(2)}) async-start(bf16[4,192,256]{2,1,0:T(8,128)(2,1)} %pad_maximum_fusion.1), calls=%async_computation.2 | async-start | bytes 786432 | tf_op jit(solution)/shard_map/all_to_all | solution.py:128
  68.5 10.6 %all-to-all-done.2 = bf16[4,192,256]{2,1,0:T(8,128)(2,1)S(1)} async-done(((bf16[4,192,256]{2,1,0:T(8,128)(2,1)}), bf16[4,192,256]{2,1,0:T(8,128)(2,1)S(1)}, u32[]{:S(2)}, u32[]{:S(2)}) %all-to-all-start.2) | async-done | bytes 393248 | tf_op jit(solution)/shard_map/all_to_all | solution.py:128
  79.2 4.7 %all-gather = bf16[1152,256]{1,0:T(8,128)(2,1)S(1)} all-gather(bf16[576,256]{1,0:T(8,128)(2,1)S(1)} %pad_maximum_fusion.2), channel_id=2, replica_groups=mesh['yp'=4,'ye'=2,'x'=4,'zl'=2,'zh'=4,'core'=2] {'core'}, dimensions={0}, use_global_device_ids=true | all-gather | bytes 884736 | tf_op jit(solution)/shard_map/all_gather | solution.py:132
  83.8 0.7 broadcast_in_dim.69
  84.6 3.5 %all-to-all-start.3 = ((bf16[16,32,256]{2,1,0:T(8,128)(2,1)}), bf16[16,32,256]{2,1,0:T(8,128)(2,1)S(1)}, u32[]{:S(2)}, u32[]{:S(2)}) async-start(bf16[16,32,256]{2,1,0:T(8,128)(2,1)} %broadcast_in_dim.69), calls=%async_computation.3 | async-start | bytes 524288 | tf_op jit(solution)/shard_map/all_to_all | solution.py:81
  88.2 4.4 %convolution_convert_fusion = bf16[2048,256]{1,0:T(8,128)(2,1)} fusion(bf16[2048,1024]{1,0:T(8,128)(2,1)} %get-tuple-element.6, bf16[1024,256]{1,0:T(8,128)(2,1)S(1)} %bitcast.65), kind=kOutput, calls=%fused_computation | convolution fusion | flops 1074266112 | bytes 5767168 | tf_op jit(solution)/shard_map/dot_general | solution.py:139
  92.6 2.4 %all-to-all-done.3 = bf16[16,32,256]{2,1,0:T(8,128)(2,1)S(1)} async-done(((bf16[16,32,256]{2,1,0:T(8,128)(2,1)}), bf16[16,32,256]{2,1,0:T(8,128)(2,1)S(1)}, u32[]{:S(2)}, u32[]{:S(2)}) %all-to-all-start.3) | async-done | bytes 262176 | tf_op jit(solution)/shard_map/all_to_all | solution.py:81
  95.0 3.6 %all-to-all-start.5 = ((bf16[8,2,128,256]{3,2,1,0:T(8,128)(2,1)}), bf16[8,2,128,256]{3,2,1,0:T(8,128)(2,1)S(1)}, u32[]{:S(2)}, u32[]{:S(2)}) async-start(bf16[8,2,128,256]{3,2,1,0:T(8,128)(2,1)} %bitcast.15), calls=%async_computation.5 | async-start | bytes 2097152 | tf_op jit(solution)/shard_map/all_to_all | solution.py:140
  98.6 4.1 %collective-permute-start.3 = (bf16[32,256]{1,0:T(8,128)(2,1)S(1)}, bf16[32,256]{1,0:T(8,128)(2,1)S(1)}, u32[]{:S(2)}, u32[]{:S(2)}) collective-permute-start(bf16[32,256]{1,0:T(8,128)(2,1)S(1)} %fusion.9), channel_id=1, source_target_pairs={{384,0},{0,128},{128,256},{256,384},{385,1},{1,129},{129,257},{257... | collective-permute-start | bytes 49160 | tf_op jit(solution)/shard_map/ppermute | solution.py:145
  102.7 4.1 %collective-permute-start.4 = (bf16[32,256]{1,0:T(8,128)(2,1)S(1)}, bf16[32,256]{1,0:T(8,128)(2,1)S(1)}, u32[]{:S(2)}, u32[]{:S(2)}) collective-permute-start(bf16[32,256]{1,0:T(8,128)(2,1)S(1)} %fusion.9), channel_id=1, source_target_pairs={{256,0},{384,128},{0,256},{128,384},{257,1},{385,129},{1,257},{129... | collective-permute-start | bytes 49160 | tf_op jit(solution)/shard_map/ppermute | solution.py:145
  106.9 5.5 %collective-permute-start.5 = (bf16[32,256]{1,0:T(8,128)(2,1)S(1)}, bf16[32,256]{1,0:T(8,128)(2,1)S(1)}, u32[]{:S(2)}, u32[]{:S(2)}) collective-permute-start(bf16[32,256]{1,0:T(8,128)(2,1)S(1)} %fusion.9), channel_id=1, source_target_pairs={{128,0},{256,128},{384,256},{0,384},{129,1},{257,129},{385,257},{1... | collective-permute-start | bytes 49160 | tf_op jit(solution)/shard_map/ppermute | solution.py:145
  112.4 0.8 collective-permute-done.5
  113.2 0.1 multiply_convert_fusion.3
  113.2 0.7 broadcast_in_dim.70
  113.9 6.8 %all-to-all-start.4 = ((bf16[8,32,256]{2,1,0:T(8,128)(2,1)}), bf16[8,32,256]{2,1,0:T(8,128)(2,1)S(1)}, u32[]{:S(2)}, u32[]{:S(2)}) async-start(bf16[8,32,256]{2,1,0:T(8,128)(2,1)} %broadcast_in_dim.70), calls=%async_computation.4 | async-start | bytes 262144 | tf_op jit(solution)/shard_map/all_to_all | solution.py:81
  120.7 0.1 broadcast_select_fusion.1
  120.8 0.1 fusion.7
  120.9 6.0 %collective-permute-start.7 = (bf16[128,256]{1,0:T(8,128)(2,1)S(1)}, bf16[128,256]{1,0:T(8,128)(2,1)S(1)}, u32[]{:S(2)}, u32[]{:S(2)}) collective-permute-start(bf16[128,256]{1,0:T(8,128)(2,1)S(1)} %fusion.7), channel_id=1, source_target_pairs={{128,0},{192,64},{256,128},{320,192},{384,256},{448,320},{0,384},{... | collective-permute-start | bytes 196616 | tf_op jit(solution)/shard_map/ppermute | solution.py:77
  126.9 0.1 fusion.6
  127.0 1.9 %collective-permute-start.6 = (bf16[128,256]{1,0:T(8,128)(2,1)S(1)}, bf16[128,256]{1,0:T(8,128)(2,1)S(1)}, u32[]{:S(2)}, u32[]{:S(2)}) collective-permute-start(bf16[128,256]{1,0:T(8,128)(2,1)S(1)} %fusion.6), channel_id=1, source_target_pairs={{64,0},{128,64},{192,128},{256,192},{320,256},{384,320},{448,384},... | collective-permute-start | bytes 196616 | tf_op jit(solution)/shard_map/ppermute | solution.py:77
  128.9 0.4 all-to-all-done.4
  129.4 0.7 bitcast_convert_fusion
  130.1 1.9 %collective-permute-done.6 = bf16[128,256]{1,0:T(8,128)(2,1)S(1)} collective-permute-done((bf16[128,256]{1,0:T(8,128)(2,1)S(1)}, bf16[128,256]{1,0:T(8,128)(2,1)S(1)}, u32[]{:S(2)}, u32[]{:S(2)}) %collective-permute-start.6) | collective-permute-done | bytes 65568 | tf_op jit(solution)/shard_map/ppermute | solution.py:77
  132.0 0.7 fusion.4
  (21 shorter events, 0.3 us)
Async XLA Ops:
  0.6 61.7 %copy-start = (bf16[256,256]{1,0:T(8,128)(2,1)S(1)}, bf16[256,256]{1,0:T(8,128)(2,1)}, u32[]{:S(2)}) copy-start(bf16[256,256]{1,0:T(8,128)(2,1)} %param.12) | copy-start | bytes 393220
  0.6 19.9 %copy-start.1 = (s32[1,16,8]{1,2,0:T(8,128)S(1)}, s32[1,16,8]{1,2,0:T(8,128)}, u32[]{:S(2)}) copy-start(s32[1,16,8]{1,2,0:T(8,128)} %param.10) | copy-start | bytes 1540
  2.3 8.5 %collective-permute-start.1 = (bf16[128,256]{1,0:T(8,128)(2,1)S(1)}, bf16[128,256]{1,0:T(8,128)(2,1)S(1)}, u32[]{:S(2)}, u32[]{:S(2)}) collective-permute-start(bf16[128,256]{1,0:T(8,128)(2,1)S(1)} %multiply_convert_fusion.2), channel_id=1, source_target_pairs={{384,0},{448,64},{0,128},{64,192},{128,256},{192,320},{256,384},{3... | collective-permute-start | bytes 196616 | tf_op jit(solution)/shard_map/ppermute | solution.py:77
  7.3 6.2 %collective-permute-start = (bf16[128,256]{1,0:T(8,128)(2,1)S(1)}, bf16[128,256]{1,0:T(8,128)(2,1)S(1)}, u32[]{:S(2)}, u32[]{:S(2)}) collective-permute-start(bf16[128,256]{1,0:T(8,128)(2,1)S(1)} %multiply_convert_fusion.2), channel_id=1, source_target_pairs={{448,0},{0,64},{64,128},{128,192},{192,256},{256,320},{320,384},{3... | collective-permute-start | bytes 196616 | tf_op jit(solution)/shard_map/ppermute | solution.py:77
  14.7 19.2 %all-to-all-start = ((bf16[8,2,128,256]{3,2,1,0:T(8,128)(2,1)}), bf16[8,2,128,256]{3,2,1,0:T(8,128)(2,1)S(1)}, u32[]{:S(2)}, u32[]{:S(2)}) async-start(bf16[8,2,128,256]{3,2,1,0:T(8,128)(2,1)} %pad_maximum_fusion), calls=%async_computation | async-start | bytes 2097152 | tf_op jit(solution)/shard_map/all_to_all | solution.py:105
  33.9 28.4 %copy-start.2 = (bf16[128,256]{1,0:T(8,128)(2,1)S(1)}, bf16[128,256]{1,0:T(8,128)(2,1)}, u32[]{:S(2)}) copy-start(bf16[128,256]{1,0:T(8,128)(2,1)} %param.13) | copy-start | bytes 196612
  37.4 6.4 %collective-permute-start.2 = (bf16[512,256]{1,0:T(8,128)(2,1)S(1)}, bf16[512,256]{1,0:T(8,128)(2,1)S(1)}, u32[]{:S(2)}, u32[]{:S(2)}) collective-permute-start(bf16[512,256]{1,0:T(8,128)(2,1)S(1)} %split.15), channel_id=1, source_target_pairs={{0,1},{1,0},{2,3},{3,2},{4,5},{5,4},{6,7},{7,6},{8,9},{9,8},{10,11... | collective-permute-start | bytes 786440 | tf_op jit(solution)/shard_map/ppermute | solution.py:109
  64.4 14.7 %all-to-all-start.2 = ((bf16[4,192,256]{2,1,0:T(8,128)(2,1)}), bf16[4,192,256]{2,1,0:T(8,128)(2,1)S(1)}, u32[]{:S(2)}, u32[]{:S(2)}) async-start(bf16[4,192,256]{2,1,0:T(8,128)(2,1)} %pad_maximum_fusion.1), calls=%async_computation.2 | async-start | bytes 786432 | tf_op jit(solution)/shard_map/all_to_all | solution.py:128
  84.6 10.4 %all-to-all-start.3 = ((bf16[16,32,256]{2,1,0:T(8,128)(2,1)}), bf16[16,32,256]{2,1,0:T(8,128)(2,1)S(1)}, u32[]{:S(2)}, u32[]{:S(2)}) async-start(bf16[16,32,256]{2,1,0:T(8,128)(2,1)} %broadcast_in_dim.69), calls=%async_computation.3 | async-start | bytes 524288 | tf_op jit(solution)/shard_map/all_to_all | solution.py:81
  95.0 18.3 %all-to-all-start.5 = ((bf16[8,2,128,256]{3,2,1,0:T(8,128)(2,1)}), bf16[8,2,128,256]{3,2,1,0:T(8,128)(2,1)S(1)}, u32[]{:S(2)}, u32[]{:S(2)}) async-start(bf16[8,2,128,256]{3,2,1,0:T(8,128)(2,1)} %bitcast.15), calls=%async_computation.5 | async-start | bytes 2097152 | tf_op jit(solution)/shard_map/all_to_all | solution.py:140
  98.6 13.8 %collective-permute-start.3 = (bf16[32,256]{1,0:T(8,128)(2,1)S(1)}, bf16[32,256]{1,0:T(8,128)(2,1)S(1)}, u32[]{:S(2)}, u32[]{:S(2)}) collective-permute-start(bf16[32,256]{1,0:T(8,128)(2,1)S(1)} %fusion.9), channel_id=1, source_target_pairs={{384,0},{0,128},{128,256},{256,384},{385,1},{1,129},{129,257},{257... | collective-permute-start | bytes 49160 | tf_op jit(solution)/shard_map/ppermute | solution.py:145
  102.7 9.6 %collective-permute-start.4 = (bf16[32,256]{1,0:T(8,128)(2,1)S(1)}, bf16[32,256]{1,0:T(8,128)(2,1)S(1)}, u32[]{:S(2)}, u32[]{:S(2)}) collective-permute-start(bf16[32,256]{1,0:T(8,128)(2,1)S(1)} %fusion.9), channel_id=1, source_target_pairs={{256,0},{384,128},{0,256},{128,384},{257,1},{385,129},{1,257},{129... | collective-permute-start | bytes 49160 | tf_op jit(solution)/shard_map/ppermute | solution.py:145
  106.9 6.3 %collective-permute-start.5 = (bf16[32,256]{1,0:T(8,128)(2,1)S(1)}, bf16[32,256]{1,0:T(8,128)(2,1)S(1)}, u32[]{:S(2)}, u32[]{:S(2)}) collective-permute-start(bf16[32,256]{1,0:T(8,128)(2,1)S(1)} %fusion.9), channel_id=1, source_target_pairs={{128,0},{256,128},{384,256},{0,384},{129,1},{257,129},{385,257},{1... | collective-permute-start | bytes 49160 | tf_op jit(solution)/shard_map/ppermute | solution.py:145
  113.9 15.5 %all-to-all-start.4 = ((bf16[8,32,256]{2,1,0:T(8,128)(2,1)}), bf16[8,32,256]{2,1,0:T(8,128)(2,1)S(1)}, u32[]{:S(2)}, u32[]{:S(2)}) async-start(bf16[8,32,256]{2,1,0:T(8,128)(2,1)} %broadcast_in_dim.70), calls=%async_computation.4 | async-start | bytes 262144 | tf_op jit(solution)/shard_map/all_to_all | solution.py:81
  120.9 9.2 %collective-permute-start.7 = (bf16[128,256]{1,0:T(8,128)(2,1)S(1)}, bf16[128,256]{1,0:T(8,128)(2,1)S(1)}, u32[]{:S(2)}, u32[]{:S(2)}) collective-permute-start(bf16[128,256]{1,0:T(8,128)(2,1)S(1)} %fusion.7), channel_id=1, source_target_pairs={{128,0},{192,64},{256,128},{320,192},{384,256},{448,320},{0,384},{... | collective-permute-start | bytes 196616 | tf_op jit(solution)/shard_map/ppermute | solution.py:77
  127.0 5.0 %collective-permute-start.6 = (bf16[128,256]{1,0:T(8,128)(2,1)S(1)}, bf16[128,256]{1,0:T(8,128)(2,1)S(1)}, u32[]{:S(2)}, u32[]{:S(2)}) collective-permute-start(bf16[128,256]{1,0:T(8,128)(2,1)S(1)} %fusion.6), channel_id=1, source_target_pairs={{64,0},{128,64},{192,128},{256,192},{320,256},{384,320},{448,384},... | collective-permute-start | bytes 196616 | tf_op jit(solution)/shard_map/ppermute | solution.py:77

commit v9 on v5

--- a/solution.py
+++ b/solution.py
@@ -121,23 +121,24 @@
     offer = jnp.concatenate([copies, local_weight.reshape(N_ZH, -1, width)], axis=1)
     given = lax.all_to_all(offer, "zh", 0, 0)
     along_zh = given[:, :own_rows].reshape(-1, width)
-    weight_rows = summed_in_f32(given[:, own_rows:])
-    share = weight_rows.shape[0]
-    slab_grads = lax.all_gather(along_zh, "core", axis=0, tiled=True)
+    weight_part = summed_in_f32(given[:, own_rows:]).astype(BF)
+    zh_rows = N_ZH * own_rows
+    pair = lax.all_gather(jnp.concatenate([along_zh, weight_part], axis=0), "core")
+    slab_grads = pair[:, :zh_rows].reshape(-1, width)
+    weight_pair = pair[:, zh_rows:].reshape(N_CORE, N_CORE, -1, width)
+    weight_rows = summed_in_f32(lax.dynamic_index_in_dim(weight_pair, core, 1, keepdims=False))
 
-    along_y = copies_to(weight_rows.astype(BF), PAIR, N_PAIR)
-    weight_rows = summed_in_f32(along_y).astype(BF)
+    along_group = copies_to(weight_rows.astype(BF), GROUP, N_GROUP)
+    weight_rows = summed_in_f32(along_group)
     returned = jnp.dot(flipped, slab_grads, preferred_element_type=F32).astype(BF)
-    returned = returned.reshape(N_GROUP, own_rows, width)
-    copies = jnp.broadcast_to(weight_rows[None], (N_GROUP,) + weight_rows.shape)
-    home = lax.all_to_all(jnp.concatenate([returned, copies], axis=1), GROUP, 0, 0)
+    arrived = lax.all_to_all(returned.reshape(N_GROUP, own_rows, width), GROUP, 0, 0)
+    own_part = weight_rows.astype(BF)
+    parts = [own_part] + [shifted(own_part, away) for away in range(1, N_PAIR)]
     node_total = own_rows * N_PAIR * N_GROUP * N_REP
-    weight_rows = (summed_in_f32(home[:, own_rows:]) / math.sqrt(node_total)).astype(BF)
+    weight_rows = (summed_in_f32(parts) / math.sqrt(node_total)).astype(BF)
     along_rep = copies_to(weight_rows, REP, N_REP)
-    along_rep = along_rep.reshape(N_ZH, N_CORE, share, width).astype(F32)
-    grad_weight = (along_rep[:, 0] + along_rep[:, 1]).reshape(-1, width)
+    grad_weight = along_rep.reshape(-1, width).astype(F32)
 
-    arrived = home[:, :own_rows]
     nothing = jnp.zeros((), BF)
     for_back = summed_in_f32(jnp.where(places < place, arrived, nothing)).astype(BF)
     for_own = summed_in_f32(jnp.where(places >= place, arrived, nothing))

time: 137 us -> 132 us (0.964)
  the two profiles are of different devices: /device:TPU:46 before, /device:TPU:1 now
where the time goes in v9:
time: 132 us; the launch traced here: 131 us
  starting transfers between devices  53.1 us (40%)
  waiting for transfers between devices  25.2 us (19%)
  blocking collectives  25 us (19%)
  matrix products  9.16 us (7%)
  Pallas kernels  8.51 us (6%)
  other arithmetic  6.39 us (5%)
  local copies, waits for them, and re-layouts  2.88 us (2%)
    ppermute x5, starting transfers between devices, shifted(): lax.ppermute(block, PAIR, [((i - distance) % N_PAIR, i) for i in range(N_...  23 us
    all_to_all x1, blocking collectives, per_device(): shares = lax.all_to_all(half.reshape(N_ZH, own_rows, width), 'zh', 0, 0)  18.2 us
    all_to_all x1, waiting for transfers between devices, per_device(): given = lax.all_to_all(offer, 'zh', 0, 0)  9.61 us
    all_to_all x2, starting transfers between devices, copies_to(): lax.all_to_all(jnp.broadcast_to(block[None], (count,) + block.shape), axi...  9.42 us
    pallas_call x1, Pallas kernels, arrange(): pl.pallas_call(arrange_kernel, out_shape=(jax.ShapeDtypeStruct((cap * row...  8.51 us
    all_to_all x1, starting transfers between devices, per_device(): window = lax.all_to_all(offer, GROUP, 0, 0).reshape(-1, width)  8.23 us
    all_gather x1, blocking collectives, per_device(): lax.all_gather(jnp.concatenate([along_zh, weight_part], axis=0), 'core')  6.84 us
    ppermute x5, waiting for transfers between devices, shifted(): lax.ppermute(block, PAIR, [((i - distance) % N_PAIR, i) for i in range(N_...  5.68 us
  transfers between devices with their start and end apart: 11, of which 7 were waited for; matrix products, arithmetic and copies ran while one was open for 6% of the time, Pallas kernels for 6%

profile of v9, /device:TPU:1, one launch (start us, length us, event | category | flops | bytes accessed | tf_op | source)
XLA Modules:
  0.0 131.2 jit_solution(700287893595388755)
XLA Ops:
  0.6 0.0 copy-start
  0.6 0.7 convert_rsqrt_fusion
  1.3 0.9 multiply_convert_fusion.2
  2.3 5.0 %collective-permute-start = (bf16[128,256]{1,0:T(8,128)(2,1)S(1)}, bf16[128,256]{1,0:T(8,128)(2,1)S(1)}, u32[]{:S(2)}, u32[]{:S(2)}) collective-permute-start(bf16[128,256]{1,0:T(8,128)(2,1)S(1)} %multiply_convert_fusion.2), channel_id=1, source_target_pairs={{384,0},{0,128},{128,256},{256,384},{385,1},{1,129},{129,257},{257... | collective-permute-start | bytes 196616 | tf_op jit(solution)/shard_map/ppermute | solution.py:73
  7.3 3.4 %collective-permute-done = bf16[128,256]{1,0:T(8,128)(2,1)S(1)} collective-permute-done((bf16[128,256]{1,0:T(8,128)(2,1)S(1)}, bf16[128,256]{1,0:T(8,128)(2,1)S(1)}, u32[]{:S(2)}, u32[]{:S(2)}) %collective-permute-start) | collective-permute-done | bytes 65568 | tf_op jit(solution)/shard_map/ppermute | solution.py:73
  10.7 1.2 broadcast_select_fusion.2
  11.9 8.2 %all-to-all-start = ((bf16[16,128,256]{2,1,0:T(8,128)(2,1)}), bf16[16,128,256]{2,1,0:T(8,128)(2,1)S(1)}, u32[]{:S(2)}, u32[]{:S(2)}) async-start(bf16[16,128,256]{2,1,0:T(8,128)(2,1)} %broadcast_select_fusion.2), calls=%async_computation | async-start | bytes 2097152 | tf_op jit(solution)/shard_map/all_to_all | solution.py:99
  20.2 1.4 %copy.10.rows_ref = s32[1,16,8]{2,1,0:T(8,128)} copy(s32[1,16,8]{1,2,0:T(8,128)} %param.10) | data formatting | bytes 1024 | tf_op args[3]
  21.5 0.6 pad_add_fusion.here_ref
  22.1 8.5 %arrange_tiles.1 = (bf16[1024,2048]{1,0:T(8,128)(2,1)}, bf16[2048,1024]{1,0:T(8,128)(2,1)}) custom-call(s32[1,16,8]{2,1,0:T(8,128)} %copy.10.rows_ref, s32[1,16]{1,0:T(1,128)} %counts_ref.1, s32[2]{0:T(128)} %pad_add_fusion.here_ref, bf16[1,16,8,128,128]{4,3,2,1,0:T(8,128)(2,1)} %tile_hbm.1), custom_call_target="tpu_custom_call" | custom-call | flops 2097152 | bytes 8388608 | tf_op jit(solution)/shard_map/arrange_tiles/pallas_call | solution.py:55
  30.6 3.3 %all-to-all-done = bf16[16,128,256]{2,1,0:T(8,128)(2,1)S(1)} async-done(((bf16[16,128,256]{2,1,0:T(8,128)(2,1)}), bf16[16,128,256]{2,1,0:T(8,128)(2,1)S(1)}, u32[]{:S(2)}, u32[]{:S(2)}) %all-to-all-start) | async-done | bytes 1048608 | tf_op jit(solution)/shard_map/all_to_all | solution.py:99
  33.9 3.5 %fusion.10 = f32[1024,256]{1,0:T(8,128)S(1)} fusion(bf16[1024,2048]{1,0:T(8,128)(2,1)} %get-tuple-element.5, bf16[2048,256]{1,0:T(8,128)(2,1)S(1)} %bitcast.58), kind=kOutput, calls=%fused_computation.39 | convolution fusion | flops 1073741824 | bytes 6291456 | tf_op jit(solution)/shard_map/dot_general | solution.py:101
  37.5 4.8 %collective-permute-start.1 = (bf16[512,256]{1,0:T(8,128)(2,1)S(1)}, bf16[512,256]{1,0:T(8,128)(2,1)S(1)}, u32[]{:S(2)}, u32[]{:S(2)}) collective-permute-start(bf16[512,256]{1,0:T(8,128)(2,1)S(1)} %split.15), channel_id=1, source_target_pairs={{0,1},{1,0},{2,3},{3,2},{4,5},{5,4},{6,7},{7,6},{8,9},{9,8},{10,11... | collective-permute-start | bytes 786440 | tf_op jit(solution)/shard_map/ppermute | solution.py:103
  42.2 1.1 collective-permute-done.1
  43.4 0.1 fusion.1
  43.5 18.2 %all_to_all.30 = bf16[4,128,256]{2,1,0:T(8,128)(2,1)S(1)} all-to-all(bf16[4,128,256]{2,1,0:T(8,128)(2,1)S(1)} %bitcast.60), channel_id=1, replica_groups=mesh['yp'=4,'ye'=2,'x'=4,'zl'=2,'zh'=4,'core'=2] {'zh'}, dimensions={0} | all-to-all | bytes 524288 | tf_op jit(solution)/shard_map/all_to_all | solution.py:105
  61.7 0.1 fusion.6
  61.7 0.0 copy-done
  61.8 0.0 copy-done.1
  61.8 0.9 multiply_convert_fusion
  62.6 0.2 convolution_convert_fusion.1
  62.8 0.2 fusion
  63.1 0.8 pad_maximum_fusion
  63.8 4.0 %all-to-all-start.2 = ((bf16[4,192,256]{2,1,0:T(8,128)(2,1)}), bf16[4,192,256]{2,1,0:T(8,128)(2,1)S(1)}, u32[]{:S(2)}, u32[]{:S(2)}) async-start(bf16[4,192,256]{2,1,0:T(8,128)(2,1)} %pad_maximum_fusion), calls=%async_computation.2 | async-start | bytes 786432 | tf_op jit(solution)/shard_map/all_to_all | solution.py:122
  67.8 9.6 %all-to-all-done.2 = bf16[4,192,256]{2,1,0:T(8,128)(2,1)S(1)} async-done(((bf16[4,192,256]{2,1,0:T(8,128)(2,1)}), bf16[4,192,256]{2,1,0:T(8,128)(2,1)S(1)}, u32[]{:S(2)}, u32[]{:S(2)}) %all-to-all-start.2) | async-done | bytes 393248 | tf_op jit(solution)/shard_map/all_to_all | solution.py:122
  77.5 6.8 %all-gather = bf16[1152,256]{1,0:T(8,128)(2,1)S(1)} all-gather(bf16[576,256]{1,0:T(8,128)(2,1)S(1)} %pad_maximum_fusion.1), channel_id=2, replica_groups=mesh['yp'=4,'ye'=2,'x'=4,'zl'=2,'zh'=4,'core'=2] {'core'}, dimensions={0}, use_global_device_ids=true | all-gather | bytes 884736 | tf_op jit(solution)/shard_map/all_gather | solution.py:126
  84.3 0.7 broadcast_in_dim.66
  85.1 3.6 %all-to-all-start.3 = ((bf16[16,32,256]{2,1,0:T(8,128)(2,1)}), bf16[16,32,256]{2,1,0:T(8,128)(2,1)S(1)}, u32[]{:S(2)}, u32[]{:S(2)}) async-start(bf16[16,32,256]{2,1,0:T(8,128)(2,1)} %broadcast_in_dim.66), calls=%async_computation.3 | async-start | bytes 524288 | tf_op jit(solution)/shard_map/all_to_all | solution.py:77
  88.7 4.4 %convolution_convert_fusion = bf16[2048,256]{1,0:T(8,128)(2,1)} fusion(bf16[2048,1024]{1,0:T(8,128)(2,1)} %get-tuple-element.6, bf16[1024,256]{1,0:T(8,128)(2,1)S(1)} %bitcast.61), kind=kOutput, calls=%fused_computation | convolution fusion | flops 1074266112 | bytes 5767168 | tf_op jit(solution)/shard_map/dot_general | solution.py:133
  93.1 2.4 %all-to-all-done.3 = bf16[16,32,256]{2,1,0:T(8,128)(2,1)S(1)} async-done(((bf16[16,32,256]{2,1,0:T(8,128)(2,1)}), bf16[16,32,256]{2,1,0:T(8,128)(2,1)S(1)}, u32[]{:S(2)}, u32[]{:S(2)}) %all-to-all-start.3) | async-done | bytes 262176 | tf_op jit(solution)/shard_map/all_to_all | solution.py:77
  95.5 3.7 %all-to-all-start.5 = ((bf16[16,128,256]{2,1,0:T(8,128)(2,1)}), bf16[16,128,256]{2,1,0:T(8,128)(2,1)S(1)}, u32[]{:S(2)}, u32[]{:S(2)}) async-start(bf16[16,128,256]{2,1,0:T(8,128)(2,1)} %bitcast.15), calls=%async_computation.5 | async-start | bytes 2097152 | tf_op jit(solution)/shard_map/all_to_all | solution.py:134
  99.3 3.0 %collective-permute-start.2 = (bf16[32,256]{1,0:T(8,128)(2,1)S(1)}, bf16[32,256]{1,0:T(8,128)(2,1)S(1)}, u32[]{:S(2)}, u32[]{:S(2)}) collective-permute-start(bf16[32,256]{1,0:T(8,128)(2,1)S(1)} %fusion.8), channel_id=1, source_target_pairs={{384,0},{0,128},{128,256},{256,384},{385,1},{1,129},{129,257},{257... | collective-permute-start | bytes 49160 | tf_op jit(solution)/shard_map/ppermute | solution.py:73
  102.2 4.3 %collective-permute-start.3 = (bf16[32,256]{1,0:T(8,128)(2,1)S(1)}, bf16[32,256]{1,0:T(8,128)(2,1)S(1)}, u32[]{:S(2)}, u32[]{:S(2)}) collective-permute-start(bf16[32,256]{1,0:T(8,128)(2,1)S(1)} %fusion.8), channel_id=1, source_target_pairs={{256,0},{384,128},{0,256},{128,384},{257,1},{385,129},{1,257},{129... | collective-permute-start | bytes 49160 | tf_op jit(solution)/shard_map/ppermute | solution.py:73
  106.6 5.5 %collective-permute-start.4 = (bf16[32,256]{1,0:T(8,128)(2,1)S(1)}, bf16[32,256]{1,0:T(8,128)(2,1)S(1)}, u32[]{:S(2)}, u32[]{:S(2)}) collective-permute-start(bf16[32,256]{1,0:T(8,128)(2,1)S(1)} %fusion.8), channel_id=1, source_target_pairs={{128,0},{256,128},{384,256},{0,384},{129,1},{257,129},{385,257},{1... | collective-permute-start | bytes 49160 | tf_op jit(solution)/shard_map/ppermute | solution.py:73
  112.0 0.0 collective-permute-done.2
  112.1 2.3 %collective-permute-done.3 = bf16[32,256]{1,0:T(8,128)(2,1)S(1)} collective-permute-done((bf16[32,256]{1,0:T(8,128)(2,1)S(1)}, bf16[32,256]{1,0:T(8,128)(2,1)S(1)}, u32[]{:S(2)}, u32[]{:S(2)}) %collective-permute-start.3) | collective-permute-done | bytes 16416 | tf_op jit(solution)/shard_map/ppermute | solution.py:73
  114.3 0.0 collective-permute-done.4
  114.3 0.1 multiply_convert_fusion.3
  114.4 0.0 all-to-all-done.5
  114.4 0.7 broadcast_in_dim.67
  115.1 5.9 %all-to-all-start.4 = ((bf16[8,32,256]{2,1,0:T(8,128)(2,1)}), bf16[8,32,256]{2,1,0:T(8,128)(2,1)S(1)}, u32[]{:S(2)}, u32[]{:S(2)}) async-start(bf16[8,32,256]{2,1,0:T(8,128)(2,1)} %broadcast_in_dim.67), calls=%async_computation.4 | async-start | bytes 262144 | tf_op jit(solution)/shard_map/all_to_all | solution.py:77
  120.9 0.2 broadcast_select_fusion.1
  121.1 0.1 fusion.2
  121.3 5.3 %collective-permute-start.5 = (bf16[128,256]{1,0:T(8,128)(2,1)S(1)}, bf16[128,256]{1,0:T(8,128)(2,1)S(1)}, u32[]{:S(2)}, u32[]{:S(2)}) collective-permute-start(bf16[128,256]{1,0:T(8,128)(2,1)S(1)} %fusion.2), channel_id=1, source_target_pairs={{128,0},{256,128},{384,256},{0,384},{129,1},{257,129},{385,257},{1... | collective-permute-start | bytes 196616 | tf_op jit(solution)/shard_map/ppermute | solution.py:73
  126.6 3.1 %all-to-all-done.4 = bf16[8,32,256]{2,1,0:T(8,128)(2,1)S(1)} async-done(((bf16[8,32,256]{2,1,0:T(8,128)(2,1)}), bf16[8,32,256]{2,1,0:T(8,128)(2,1)S(1)}, u32[]{:S(2)}, u32[]{:S(2)}) %all-to-all-start.4) | async-done | bytes 131104 | tf_op jit(solution)/shard_map/all_to_all | solution.py:77
  129.6 0.7 bitcast_convert_fusion
  130.4 0.0 collective-permute-done.5
  130.4 0.8 fusion.5
  (12 shorter events, 0.2 us)
Async XLA Ops:
  0.6 61.1 %copy-start = (bf16[256,256]{1,0:T(8,128)(2,1)S(1)}, bf16[256,256]{1,0:T(8,128)(2,1)}, u32[]{:S(2)}) copy-start(bf16[256,256]{1,0:T(8,128)(2,1)} %param.12) | copy-start | bytes 393220
  2.3 8.5 %collective-permute-start = (bf16[128,256]{1,0:T(8,128)(2,1)S(1)}, bf16[128,256]{1,0:T(8,128)(2,1)S(1)}, u32[]{:S(2)}, u32[]{:S(2)}) collective-permute-start(bf16[128,256]{1,0:T(8,128)(2,1)S(1)} %multiply_convert_fusion.2), channel_id=1, source_target_pairs={{384,0},{0,128},{128,256},{256,384},{385,1},{1,129},{129,257},{257... | collective-permute-start | bytes 196616 | tf_op jit(solution)/shard_map/ppermute | solution.py:73
  11.9 22.0 %all-to-all-start = ((bf16[16,128,256]{2,1,0:T(8,128)(2,1)}), bf16[16,128,256]{2,1,0:T(8,128)(2,1)S(1)}, u32[]{:S(2)}, u32[]{:S(2)}) async-start(bf16[16,128,256]{2,1,0:T(8,128)(2,1)} %broadcast_select_fusion.2), calls=%async_computation | async-start | bytes 2097152 | tf_op jit(solution)/shard_map/all_to_all | solution.py:99
  33.9 27.8 %copy-start.1 = (bf16[128,256]{1,0:T(8,128)(2,1)S(1)}, bf16[128,256]{1,0:T(8,128)(2,1)}, u32[]{:S(2)}) copy-start(bf16[128,256]{1,0:T(8,128)(2,1)} %param.13) | copy-start | bytes 196612
  37.5 5.9 %collective-permute-start.1 = (bf16[512,256]{1,0:T(8,128)(2,1)S(1)}, bf16[512,256]{1,0:T(8,128)(2,1)S(1)}, u32[]{:S(2)}, u32[]{:S(2)}) collective-permute-start(bf16[512,256]{1,0:T(8,128)(2,1)S(1)} %split.15), channel_id=1, source_target_pairs={{0,1},{1,0},{2,3},{3,2},{4,5},{5,4},{6,7},{7,6},{8,9},{9,8},{10,11... | collective-permute-start | bytes 786440 | tf_op jit(solution)/shard_map/ppermute | solution.py:103
  63.8 13.6 %all-to-all-start.2 = ((bf16[4,192,256]{2,1,0:T(8,128)(2,1)}), bf16[4,192,256]{2,1,0:T(8,128)(2,1)S(1)}, u32[]{:S(2)}, u32[]{:S(2)}) async-start(bf16[4,192,256]{2,1,0:T(8,128)(2,1)} %pad_maximum_fusion), calls=%async_computation.2 | async-start | bytes 786432 | tf_op jit(solution)/shard_map/all_to_all | solution.py:122
  85.1 10.5 %all-to-all-start.3 = ((bf16[16,32,256]{2,1,0:T(8,128)(2,1)}), bf16[16,32,256]{2,1,0:T(8,128)(2,1)S(1)}, u32[]{:S(2)}, u32[]{:S(2)}) async-start(bf16[16,32,256]{2,1,0:T(8,128)(2,1)} %broadcast_in_dim.66), calls=%async_computation.3 | async-start | bytes 524288 | tf_op jit(solution)/shard_map/all_to_all | solution.py:77
  95.5 18.9 %all-to-all-start.5 = ((bf16[16,128,256]{2,1,0:T(8,128)(2,1)}), bf16[16,128,256]{2,1,0:T(8,128)(2,1)S(1)}, u32[]{:S(2)}, u32[]{:S(2)}) async-start(bf16[16,128,256]{2,1,0:T(8,128)(2,1)} %bitcast.15), calls=%async_computation.5 | async-start | bytes 2097152 | tf_op jit(solution)/shard_map/all_to_all | solution.py:134
  99.3 12.8 %collective-permute-start.2 = (bf16[32,256]{1,0:T(8,128)(2,1)S(1)}, bf16[32,256]{1,0:T(8,128)(2,1)S(1)}, u32[]{:S(2)}, u32[]{:S(2)}) collective-permute-start(bf16[32,256]{1,0:T(8,128)(2,1)S(1)} %fusion.8), channel_id=1, source_target_pairs={{384,0},{0,128},{128,256},{256,384},{385,1},{1,129},{129,257},{257... | collective-permute-start | bytes 49160 | tf_op jit(solution)/shard_map/ppermute | solution.py:73
  102.2 12.1 %collective-permute-start.3 = (bf16[32,256]{1,0:T(8,128)(2,1)S(1)}, bf16[32,256]{1,0:T(8,128)(2,1)S(1)}, u32[]{:S(2)}, u32[]{:S(2)}) collective-permute-start(bf16[32,256]{1,0:T(8,128)(2,1)S(1)} %fusion.8), channel_id=1, source_target_pairs={{256,0},{384,128},{0,256},{128,384},{257,1},{385,129},{1,257},{129... | collective-permute-start | bytes 49160 | tf_op jit(solution)/shard_map/ppermute | solution.py:73
  106.6 7.8 %collective-permute-start.4 = (bf16[32,256]{1,0:T(8,128)(2,1)S(1)}, bf16[32,256]{1,0:T(8,128)(2,1)S(1)}, u32[]{:S(2)}, u32[]{:S(2)}) collective-permute-start(bf16[32,256]{1,0:T(8,128)(2,1)S(1)} %fusion.8), channel_id=1, source_target_pairs={{128,0},{256,128},{384,256},{0,384},{129,1},{257,129},{385,257},{1... | collective-permute-start | bytes 49160 | tf_op jit(solution)/shard_map/ppermute | solution.py:73
  115.1 14.6 %all-to-all-start.4 = ((bf16[8,32,256]{2,1,0:T(8,128)(2,1)}), bf16[8,32,256]{2,1,0:T(8,128)(2,1)S(1)}, u32[]{:S(2)}, u32[]{:S(2)}) async-start(bf16[8,32,256]{2,1,0:T(8,128)(2,1)} %broadcast_in_dim.67), calls=%async_computation.4 | async-start | bytes 262144 | tf_op jit(solution)/shard_map/all_to_all | solution.py:77
  121.3 9.1 %collective-permute-start.5 = (bf16[128,256]{1,0:T(8,128)(2,1)S(1)}, bf16[128,256]{1,0:T(8,128)(2,1)S(1)}, u32[]{:S(2)}, u32[]{:S(2)}) collective-permute-start(bf16[128,256]{1,0:T(8,128)(2,1)S(1)} %fusion.2), channel_id=1, source_target_pairs={{128,0},{256,128},{384,256},{0,384},{129,1},{257,129},{385,257},{1... | collective-permute-start | bytes 196616 | tf_op jit(solution)/shard_map/ppermute | solution.py:73

commit v10 on v9

--- a/solution.py
+++ b/solution.py
@@ -69,6 +69,74 @@
     )(tile_rows, tile_counts, here, tile_values)
 
 
+def scale_kernel(degrees_ref, features_ref, scaled_ref, root_ref):
+    rows, width = features_ref.shape
+    root = lax.rsqrt(degrees_ref[...].astype(F32))
+    root_ref[...] = root
+    across = jnp.broadcast_to(root, (rows, rows)).T
+    for start in range(0, width, rows):
+        lanes = pl.ds(start, rows)
+        scaled_ref[:, lanes] = (features_ref[:, lanes].astype(F32) * across).astype(BF)
+
+
+def scaled_rows(features, degrees):
+    rows, width = features.shape
+    return pl.pallas_call(
+        scale_kernel,
+        out_shape=(pltpu.VMEM((rows, width), BF), pltpu.VMEM((1, rows), F32)),
+        in_specs=[pl.BlockSpec(memory_space=pltpu.VMEM)] * 2,
+        out_specs=(pl.BlockSpec(memory_space=pltpu.VMEM),) * 2,
+        cost_estimate=pl.CostEstimate(
+            flops=rows * width, bytes_accessed=4 * rows * width, transcendentals=rows
+        ),
+        name="scale_rows",
+    )(degrees[None, :], features)
+
+
+def dense_kernel(shares_ref, root_ref, weight_ref, cotangent_ref, act_ref, offer_ref):
+    rows, width = act_ref.shape
+    across = jnp.broadcast_to(root_ref[...], (rows, rows)).T
+    across = jnp.concatenate([across] * (width // rows), axis=1)
+    aggregated = (summed_in_f32(shares_ref) * across).astype(BF)
+    pre_act = jnp.dot(aggregated, weight_ref[...], preferred_element_type=F32)
+    sigma = jax.nn.sigmoid(pre_act)
+    act_ref[...] = (pre_act * sigma).astype(BF)
+    cotangent = cotangent_ref[...].astype(F32)
+    act_grad = (cotangent * sigma * (1.0 + pre_act * (1.0 - sigma))).astype(BF)
+    back_grad = lax.dot_general(
+        act_grad, weight_ref[...], (((1,), (1,)), ((), ())), preferred_element_type=F32
+    )
+    back_scaled = (back_grad * across).astype(BF)
+    local_weight = lax.dot_general(
+        aggregated, act_grad, (((0,), (0,)), ((), ())), preferred_element_type=F32
+    ).astype(BF)
+    share = width // N_ZH
+    for zh in range(N_ZH):
+        offer_ref[zh, :rows] = back_scaled
+        offer_ref[zh, rows:] = local_weight[zh * share : (zh + 1) * share]
+
+
+def dense(shares, root, weight, cotangent):
+    rows, width = cotangent.shape
+    whole = pl.BlockSpec(memory_space=pltpu.VMEM)
+    return pl.pallas_call(
+        dense_kernel,
+        out_shape=(
+            jax.ShapeDtypeStruct((rows, width), BF),
+            pltpu.VMEM((N_ZH, rows + width // N_ZH, width), BF),
+        ),
+        in_specs=[whole] * 4,
+        out_specs=(whole, whole),
+        cost_estimate=pl.CostEstimate(
+            flops=6 * rows * width * width,
+            bytes_accessed=16 * rows * width,
+            transcendentals=rows * width,
+        ),
+        compiler_params=pltpu.CompilerParams(vmem_limit_bytes=8 * 2**20),
+        name="dense_part",
+    )(shares, root, weight, cotangent)
+
+
 def shifted(block, distance):
     return lax.ppermute(block, PAIR, [((i - distance) % N_PAIR, i) for i in range(N_PAIR)])
 
@@ -79,8 +147,8 @@
 
 def summed_in_f32(blocks):
     total = blocks[0].astype(F32)
-    for block in blocks[1:]:
-        total = total + block.astype(F32)
+    for index in range(1, len(blocks) if isinstance(blocks, list) else blocks.shape[0]):
+        total = total + blocks[index].astype(F32)
     return total
 
 
@@ -88,8 +156,8 @@
     own_rows, width = features.shape
     place, core = lax.axis_index(GROUP), lax.axis_index("core")
     places = jnp.arange(N_GROUP, dtype=jnp.int32)[:, None, None]
-    inv_root = lax.rsqrt(degrees.astype(F32))[:, None]
-    scaled = (features.astype(F32) * inv_root).astype(BF)
+    scaled, root = scaled_rows(features, degrees)
+    inv_root = root[0][:, None]
 
     pair_back = shifted(scaled, 1)
     adjacency, flipped = arrange(
@@ -103,22 +171,7 @@
     other = lax.ppermute(sent.astype(BF), "core", [(0, 1), (1, 0)])
     half = (kept + other.astype(F32)).astype(BF)
     shares = lax.all_to_all(half.reshape(N_ZH, own_rows, width), "zh", 0, 0)
-    own_sum = summed_in_f32(shares)
-
-    aggregated = (own_sum * inv_root).astype(BF)
-    pre_act = jnp.dot(aggregated, weight, preferred_element_type=F32)
-    sigma = jax.nn.sigmoid(pre_act)
-    activations = (pre_act * sigma).astype(BF)
-    act_grad = (cotangent.astype(F32) * sigma * (1.0 + pre_act * (1.0 - sigma))).astype(BF)
-    back_grad = lax.dot_general(
-        act_grad, weight, (((1,), (1,)), ((), ())), preferred_element_type=F32
-    )
-    back_scaled = (back_grad * inv_root).astype(BF)
-    local_weight = lax.dot_general(
-        aggregated, act_grad, (((0,), (0,)), ((), ())), preferred_element_type=F32
-    ).astype(BF)
-    copies = jnp.broadcast_to(back_scaled[None], (N_ZH,) + back_scaled.shape)
-    offer = jnp.concatenate([copies, local_weight.reshape(N_ZH, -1, width)], axis=1)
+    activations, offer = dense(shares, root, weight, cotangent)
     given = lax.all_to_all(offer, "zh", 0, 0)
     along_zh = given[:, :own_rows].reshape(-1, width)
     weight_part = summed_in_f32(given[:, own_rows:]).astype(BF)

time: 132 us -> 131 us (level)
  other arithmetic: 6.39 us -> 3.9 us
  Pallas kernels: 8.51 us -> 10.6 us
    pallas_call x0 -> x2, Pallas kernels: none -> 2.12 us  [the longest x1 1.16 us: dense(): pl.pallas_call(dense_kernel, out_shape=(jax.ShapeDtypeStruct((rows, width...]
  transfers between devices with their start and end apart: 11 -> 11, of which waited for: 7 -> 7; matrix products, arithmetic and copies ran while one was open for 6% -> 6% of each run, Pallas kernels for 6% -> 7%
where the time goes in v10:
time: 131 us; the launch traced here: 129 us
  starting transfers between devices  53.6 us (41%)
  blocking collectives  25 us (19%)
  waiting for transfers between devices  24.5 us (19%)
  Pallas kernels  10.6 us (8%)
  matrix products  7.91 us (6%)
  other arithmetic  3.9 us (3%)
  local copies, waits for them, and re-layouts  2.85 us (2%)
    ppermute x5, starting transfers between devices, shifted(): lax.ppermute(block, PAIR, [((i - distance) % N_PAIR, i) for i in range(N_...  23.2 us
    all_to_all x1, blocking collectives, per_device(): shares = lax.all_to_all(half.reshape(N_ZH, own_rows, width), 'zh', 0, 0)  18.2 us
    all_to_all x2, starting transfers between devices, copies_to(): lax.all_to_all(jnp.broadcast_to(block[None], (count,) + block.shape), axi...  9.76 us
    all_to_all x1, waiting for transfers between devices, per_device(): given = lax.all_to_all(offer, 'zh', 0, 0)  9.61 us
    pallas_call x1, Pallas kernels, arrange(): pl.pallas_call(arrange_kernel, out_shape=(jax.ShapeDtypeStruct((cap * row...  8.52 us
    all_to_all x1, starting transfers between devices, per_device(): window = lax.all_to_all(offer, GROUP, 0, 0).reshape(-1, width)  8.23 us
    all_gather x1, blocking collectives, per_device(): lax.all_gather(jnp.concatenate([along_zh, weight_part], axis=0), 'core')  6.85 us
    all_to_all x2, waiting for transfers between devices, copies_to(): lax.all_to_all(jnp.broadcast_to(block[None], (count,) + block.shape), axi...  5.33 us
  transfers between devices with their start and end apart: 11, of which 7 were waited for; matrix products, arithmetic and copies ran while one was open for 6% of the time, Pallas kernels for 7%

profile of v10, /device:TPU:1, one launch (start us, length us, event | category | flops | bytes accessed | tf_op | source)
XLA Modules:
  0.0 129.3 jit_solution(7632656587093498802)
XLA Ops:
  0.6 1.0 scale_rows.1
  1.6 5.0 %collective-permute-start = (bf16[128,256]{1,0:T(8,128)(2,1)S(1)}, bf16[128,256]{1,0:T(8,128)(2,1)S(1)}, u32[]{:S(2)}, u32[]{:S(2)}) collective-permute-start(bf16[128,256]{1,0:T(8,128)(2,1)S(1)} %get-tuple-element.10), channel_id=1, source_target_pairs={{384,0},{0,128},{128,256},{256,384},{385,1},{1,129},{129,257},{257... | collective-permute-start | bytes 196616 | tf_op jit(solution)/shard_map/ppermute | solution.py:141
  6.7 3.4 %collective-permute-done = bf16[128,256]{1,0:T(8,128)(2,1)S(1)} collective-permute-done((bf16[128,256]{1,0:T(8,128)(2,1)S(1)}, bf16[128,256]{1,0:T(8,128)(2,1)S(1)}, u32[]{:S(2)}, u32[]{:S(2)}) %collective-permute-start) | collective-permute-done | bytes 65568 | tf_op jit(solution)/shard_map/ppermute | solution.py:141
  10.0 1.2 broadcast_select_fusion.2
  11.3 8.2 %all-to-all-start = ((bf16[16,128,256]{2,1,0:T(8,128)(2,1)}), bf16[16,128,256]{2,1,0:T(8,128)(2,1)S(1)}, u32[]{:S(2)}, u32[]{:S(2)}) async-start(bf16[16,128,256]{2,1,0:T(8,128)(2,1)} %broadcast_select_fusion.2), calls=%async_computation | async-start | bytes 2097152 | tf_op jit(solution)/shard_map/all_to_all | solution.py:167
  19.5 1.4 %copy.10.rows_ref = s32[1,16,8]{2,1,0:T(8,128)} copy(s32[1,16,8]{1,2,0:T(8,128)} %param.10) | data formatting | bytes 1024 | tf_op args[3]
  20.9 0.6 pad_add_fusion.here_ref
  21.4 8.5 %arrange_tiles.1 = (bf16[1024,2048]{1,0:T(8,128)(2,1)}, bf16[2048,1024]{1,0:T(8,128)(2,1)}) custom-call(s32[1,16,8]{2,1,0:T(8,128)} %copy.10.rows_ref, s32[1,16]{1,0:T(1,128)} %counts_ref.1, s32[2]{0:T(128)} %pad_add_fusion.here_ref, bf16[1,16,8,128,128]{4,3,2,1,0:T(8,128)(2,1)} %tile_hbm.1), custom_call_target="tpu_custom_call" | custom-call | flops 2097152 | bytes 8388608 | tf_op jit(solution)/shard_map/arrange_tiles/pallas_call | solution.py:55
  30.0 3.3 %all-to-all-done = bf16[16,128,256]{2,1,0:T(8,128)(2,1)S(1)} async-done(((bf16[16,128,256]{2,1,0:T(8,128)(2,1)}), bf16[16,128,256]{2,1,0:T(8,128)(2,1)S(1)}, u32[]{:S(2)}, u32[]{:S(2)}) %all-to-all-start) | async-done | bytes 1048608 | tf_op jit(solution)/shard_map/all_to_all | solution.py:167
  33.2 0.0 copy-start
  33.3 0.0 copy-start.1
  33.3 3.5 %fusion.8 = f32[1024,256]{1,0:T(8,128)S(1)} fusion(bf16[1024,2048]{1,0:T(8,128)(2,1)} %get-tuple-element.9, bf16[2048,256]{1,0:T(8,128)(2,1)S(1)} %bitcast.50), kind=kOutput, calls=%fused_computation.28 | convolution fusion | flops 1073741824 | bytes 6291456 | tf_op jit(solution)/shard_map/dot_general | solution.py:169
  36.8 4.8 %collective-permute-start.1 = (bf16[512,256]{1,0:T(8,128)(2,1)S(1)}, bf16[512,256]{1,0:T(8,128)(2,1)S(1)}, u32[]{:S(2)}, u32[]{:S(2)}) collective-permute-start(bf16[512,256]{1,0:T(8,128)(2,1)S(1)} %split.15), channel_id=1, source_target_pairs={{0,1},{1,0},{2,3},{3,2},{4,5},{5,4},{6,7},{7,6},{8,9},{9,8},{10,11... | collective-permute-start | bytes 786440 | tf_op jit(solution)/shard_map/ppermute | solution.py:171
  41.6 1.1 collective-permute-done.1
  42.7 0.1 fusion
  42.8 18.2 %all_to_all.30.shares_ref = bf16[4,128,256]{2,1,0:T(8,128)(2,1)S(1)} all-to-all(bf16[4,128,256]{2,1,0:T(8,128)(2,1)S(1)} %bitcast.52), channel_id=1, replica_groups=mesh['yp'=4,'ye'=2,'x'=4,'zl'=2,'zh'=4,'core'=2] {'zh'}, dimensions={0} | all-to-all | bytes 524288 | tf_op jit(solution)/shard_map/all_to_all | solution.py:173
  61.0 0.0 copy-done
  61.0 0.0 copy-done.1
  61.0 1.2 dense_part.1
  62.1 4.0 %all-to-all-start.2 = ((bf16[4,192,256]{2,1,0:T(8,128)(2,1)}), bf16[4,192,256]{2,1,0:T(8,128)(2,1)S(1)}, u32[]{:S(2)}, u32[]{:S(2)}) async-start(bf16[4,192,256]{2,1,0:T(8,128)(2,1)} %get-tuple-element.13), calls=%async_computation.2 | async-start | bytes 786432 | tf_op jit(solution)/shard_map/all_to_all | solution.py:175
  66.1 9.6 %all-to-all-done.2 = bf16[4,192,256]{2,1,0:T(8,128)(2,1)S(1)} async-done(((bf16[4,192,256]{2,1,0:T(8,128)(2,1)}), bf16[4,192,256]{2,1,0:T(8,128)(2,1)S(1)}, u32[]{:S(2)}, u32[]{:S(2)}) %all-to-all-start.2) | async-done | bytes 393248 | tf_op jit(solution)/shard_map/all_to_all | solution.py:175
  75.8 6.8 %all-gather = bf16[1152,256]{1,0:T(8,128)(2,1)S(1)} all-gather(bf16[576,256]{1,0:T(8,128)(2,1)S(1)} %pad_maximum_fusion), channel_id=2, replica_groups=mesh['yp'=4,'ye'=2,'x'=4,'zl'=2,'zh'=4,'core'=2] {'core'}, dimensions={0}, use_global_device_ids=true | all-gather | bytes 884736 | tf_op jit(solution)/shard_map/all_gather | solution.py:179
  82.7 0.7 broadcast_in_dim.62
  83.4 3.6 %all-to-all-start.3 = ((bf16[16,32,256]{2,1,0:T(8,128)(2,1)}), bf16[16,32,256]{2,1,0:T(8,128)(2,1)S(1)}, u32[]{:S(2)}, u32[]{:S(2)}) async-start(bf16[16,32,256]{2,1,0:T(8,128)(2,1)} %broadcast_in_dim.62), calls=%async_computation.3 | async-start | bytes 524288 | tf_op jit(solution)/shard_map/all_to_all | solution.py:145
  87.0 4.4 %convolution_convert_fusion = bf16[2048,256]{1,0:T(8,128)(2,1)} fusion(bf16[2048,1024]{1,0:T(8,128)(2,1)} %get-tuple-element.14, bf16[1024,256]{1,0:T(8,128)(2,1)S(1)} %bitcast.53), kind=kOutput, calls=%fused_computation | convolution fusion | flops 1074266112 | bytes 5767168 | tf_op jit(solution)/shard_map/dot_general | solution.py:186
  91.4 2.4 %all-to-all-done.3 = bf16[16,32,256]{2,1,0:T(8,128)(2,1)S(1)} async-done(((bf16[16,32,256]{2,1,0:T(8,128)(2,1)}), bf16[16,32,256]{2,1,0:T(8,128)(2,1)S(1)}, u32[]{:S(2)}, u32[]{:S(2)}) %all-to-all-start.3) | async-done | bytes 262176 | tf_op jit(solution)/shard_map/all_to_all | solution.py:145
  93.8 3.7 %all-to-all-start.5 = ((bf16[16,128,256]{2,1,0:T(8,128)(2,1)}), bf16[16,128,256]{2,1,0:T(8,128)(2,1)S(1)}, u32[]{:S(2)}, u32[]{:S(2)}) async-start(bf16[16,128,256]{2,1,0:T(8,128)(2,1)} %bitcast.14), calls=%async_computation.5 | async-start | bytes 2097152 | tf_op jit(solution)/shard_map/all_to_all | solution.py:187
  97.6 5.3 %collective-permute-start.3 = (bf16[32,256]{1,0:T(8,128)(2,1)S(1)}, bf16[32,256]{1,0:T(8,128)(2,1)S(1)}, u32[]{:S(2)}, u32[]{:S(2)}) collective-permute-start(bf16[32,256]{1,0:T(8,128)(2,1)S(1)} %fusion.6), channel_id=1, source_target_pairs={{256,0},{384,128},{0,256},{128,384},{257,1},{385,129},{1,257},{129... | collective-permute-start | bytes 49160 | tf_op jit(solution)/shard_map/ppermute | solution.py:141
  102.9 1.9 %collective-permute-start.2 = (bf16[32,256]{1,0:T(8,128)(2,1)S(1)}, bf16[32,256]{1,0:T(8,128)(2,1)S(1)}, u32[]{:S(2)}, u32[]{:S(2)}) collective-permute-start(bf16[32,256]{1,0:T(8,128)(2,1)S(1)} %fusion.6), channel_id=1, source_target_pairs={{384,0},{0,128},{128,256},{256,384},{385,1},{1,129},{129,257},{257... | collective-permute-start | bytes 49160 | tf_op jit(solution)/shard_map/ppermute | solution.py:141
  104.8 5.5 %collective-permute-start.4 = (bf16[32,256]{1,0:T(8,128)(2,1)S(1)}, bf16[32,256]{1,0:T(8,128)(2,1)S(1)}, u32[]{:S(2)}, u32[]{:S(2)}) collective-permute-start(bf16[32,256]{1,0:T(8,128)(2,1)S(1)} %fusion.6), channel_id=1, source_target_pairs={{128,0},{256,128},{384,256},{0,384},{129,1},{257,129},{385,257},{1... | collective-permute-start | bytes 49160 | tf_op jit(solution)/shard_map/ppermute | solution.py:141
  110.3 1.8 %collective-permute-done.3 = bf16[32,256]{1,0:T(8,128)(2,1)S(1)} collective-permute-done((bf16[32,256]{1,0:T(8,128)(2,1)S(1)}, bf16[32,256]{1,0:T(8,128)(2,1)S(1)}, u32[]{:S(2)}, u32[]{:S(2)}) %collective-permute-start.3) | collective-permute-done | bytes 16416 | tf_op jit(solution)/shard_map/ppermute | solution.py:141
  112.1 0.0 collective-permute-done.2
  112.1 0.0 collective-permute-done.4
  112.1 0.1 multiply_convert_fusion
  112.2 0.0 all-to-all-done.5
  112.2 0.7 broadcast_in_dim.63
  112.8 6.2 %all-to-all-start.4 = ((bf16[8,32,256]{2,1,0:T(8,128)(2,1)}), bf16[8,32,256]{2,1,0:T(8,128)(2,1)S(1)}, u32[]{:S(2)}, u32[]{:S(2)}) async-start(bf16[8,32,256]{2,1,0:T(8,128)(2,1)} %broadcast_in_dim.63), calls=%async_computation.4 | async-start | bytes 262144 | tf_op jit(solution)/shard_map/all_to_all | solution.py:145
  119.0 0.2 broadcast_select_fusion.1
  119.3 0.1 fusion.1
  119.4 5.4 %collective-permute-start.5 = (bf16[128,256]{1,0:T(8,128)(2,1)S(1)}, bf16[128,256]{1,0:T(8,128)(2,1)S(1)}, u32[]{:S(2)}, u32[]{:S(2)}) collective-permute-start(bf16[128,256]{1,0:T(8,128)(2,1)S(1)} %fusion.1), channel_id=1, source_target_pairs={{128,0},{256,128},{384,256},{0,384},{129,1},{257,129},{385,257},{1... | collective-permute-start | bytes 196616 | tf_op jit(solution)/shard_map/ppermute | solution.py:141
  124.9 2.9 %all-to-all-done.4 = bf16[8,32,256]{2,1,0:T(8,128)(2,1)S(1)} async-done(((bf16[8,32,256]{2,1,0:T(8,128)(2,1)}), bf16[8,32,256]{2,1,0:T(8,128)(2,1)S(1)}, u32[]{:S(2)}, u32[]{:S(2)}) %all-to-all-start.4) | async-done | bytes 131104 | tf_op jit(solution)/shard_map/all_to_all | solution.py:145
  127.8 0.7 bitcast_convert_fusion
  128.5 0.0 collective-permute-done.5
  128.5 0.8 fusion.4
  (10 shorter events, 0.2 us)
Async XLA Ops:
  1.6 8.5 %collective-permute-start = (bf16[128,256]{1,0:T(8,128)(2,1)S(1)}, bf16[128,256]{1,0:T(8,128)(2,1)S(1)}, u32[]{:S(2)}, u32[]{:S(2)}) collective-permute-start(bf16[128,256]{1,0:T(8,128)(2,1)S(1)} %get-tuple-element.10), channel_id=1, source_target_pairs={{384,0},{0,128},{128,256},{256,384},{385,1},{1,129},{129,257},{257... | collective-permute-start | bytes 196616 | tf_op jit(solution)/shard_map/ppermute | solution.py:141
  11.3 22.0 %all-to-all-start = ((bf16[16,128,256]{2,1,0:T(8,128)(2,1)}), bf16[16,128,256]{2,1,0:T(8,128)(2,1)S(1)}, u32[]{:S(2)}, u32[]{:S(2)}) async-start(bf16[16,128,256]{2,1,0:T(8,128)(2,1)} %broadcast_select_fusion.2), calls=%async_computation | async-start | bytes 2097152 | tf_op jit(solution)/shard_map/all_to_all | solution.py:167
  33.2 27.7 %copy-start = (bf16[256,256]{1,0:T(8,128)(2,1)S(1)}, bf16[256,256]{1,0:T(8,128)(2,1)}, u32[]{:S(2)}) copy-start(bf16[256,256]{1,0:T(8,128)(2,1)} %weight_ref.1) | copy-start | bytes 393220
  33.3 27.7 %copy-start.1 = (bf16[128,256]{1,0:T(8,128)(2,1)S(1)}, bf16[128,256]{1,0:T(8,128)(2,1)}, u32[]{:S(2)}) copy-start(bf16[128,256]{1,0:T(8,128)(2,1)} %cotangent_ref.1) | copy-start | bytes 196612
  36.8 5.9 %collective-permute-start.1 = (bf16[512,256]{1,0:T(8,128)(2,1)S(1)}, bf16[512,256]{1,0:T(8,128)(2,1)S(1)}, u32[]{:S(2)}, u32[]{:S(2)}) collective-permute-start(bf16[512,256]{1,0:T(8,128)(2,1)S(1)} %split.15), channel_id=1, source_target_pairs={{0,1},{1,0},{2,3},{3,2},{4,5},{5,4},{6,7},{7,6},{8,9},{9,8},{10,11... | collective-permute-start | bytes 786440 | tf_op jit(solution)/shard_map/ppermute | solution.py:171
  62.1 13.6 %all-to-all-start.2 = ((bf16[4,192,256]{2,1,0:T(8,128)(2,1)}), bf16[4,192,256]{2,1,0:T(8,128)(2,1)S(1)}, u32[]{:S(2)}, u32[]{:S(2)}) async-start(bf16[4,192,256]{2,1,0:T(8,128)(2,1)} %get-tuple-element.13), calls=%async_computation.2 | async-start | bytes 786432 | tf_op jit(solution)/shard_map/all_to_all | solution.py:175
  83.4 10.5 %all-to-all-start.3 = ((bf16[16,32,256]{2,1,0:T(8,128)(2,1)}), bf16[16,32,256]{2,1,0:T(8,128)(2,1)S(1)}, u32[]{:S(2)}, u32[]{:S(2)}) async-start(bf16[16,32,256]{2,1,0:T(8,128)(2,1)} %broadcast_in_dim.62), calls=%async_computation.3 | async-start | bytes 524288 | tf_op jit(solution)/shard_map/all_to_all | solution.py:145
  93.8 18.3 %all-to-all-start.5 = ((bf16[16,128,256]{2,1,0:T(8,128)(2,1)}), bf16[16,128,256]{2,1,0:T(8,128)(2,1)S(1)}, u32[]{:S(2)}, u32[]{:S(2)}) async-start(bf16[16,128,256]{2,1,0:T(8,128)(2,1)} %bitcast.14), calls=%async_computation.5 | async-start | bytes 2097152 | tf_op jit(solution)/shard_map/all_to_all | solution.py:187
  97.6 14.5 %collective-permute-start.3 = (bf16[32,256]{1,0:T(8,128)(2,1)S(1)}, bf16[32,256]{1,0:T(8,128)(2,1)S(1)}, u32[]{:S(2)}, u32[]{:S(2)}) collective-permute-start(bf16[32,256]{1,0:T(8,128)(2,1)S(1)} %fusion.6), channel_id=1, source_target_pairs={{256,0},{384,128},{0,256},{128,384},{257,1},{385,129},{1,257},{129... | collective-permute-start | bytes 49160 | tf_op jit(solution)/shard_map/ppermute | solution.py:141
  102.9 9.2 %collective-permute-start.2 = (bf16[32,256]{1,0:T(8,128)(2,1)S(1)}, bf16[32,256]{1,0:T(8,128)(2,1)S(1)}, u32[]{:S(2)}, u32[]{:S(2)}) collective-permute-start(bf16[32,256]{1,0:T(8,128)(2,1)S(1)} %fusion.6), channel_id=1, source_target_pairs={{384,0},{0,128},{128,256},{256,384},{385,1},{1,129},{129,257},{257... | collective-permute-start | bytes 49160 | tf_op jit(solution)/shard_map/ppermute | solution.py:141
  104.8 7.3 %collective-permute-start.4 = (bf16[32,256]{1,0:T(8,128)(2,1)S(1)}, bf16[32,256]{1,0:T(8,128)(2,1)S(1)}, u32[]{:S(2)}, u32[]{:S(2)}) collective-permute-start(bf16[32,256]{1,0:T(8,128)(2,1)S(1)} %fusion.6), channel_id=1, source_target_pairs={{128,0},{256,128},{384,256},{0,384},{129,1},{257,129},{385,257},{1... | collective-permute-start | bytes 49160 | tf_op jit(solution)/shard_map/ppermute | solution.py:141
  112.8 14.9 %all-to-all-start.4 = ((bf16[8,32,256]{2,1,0:T(8,128)(2,1)}), bf16[8,32,256]{2,1,0:T(8,128)(2,1)S(1)}, u32[]{:S(2)}, u32[]{:S(2)}) async-start(bf16[8,32,256]{2,1,0:T(8,128)(2,1)} %broadcast_in_dim.63), calls=%async_computation.4 | async-start | bytes 262144 | tf_op jit(solution)/shard_map/all_to_all | solution.py:145
  119.4 9.1 %collective-permute-start.5 = (bf16[128,256]{1,0:T(8,128)(2,1)S(1)}, bf16[128,256]{1,0:T(8,128)(2,1)S(1)}, u32[]{:S(2)}, u32[]{:S(2)}) collective-permute-start(bf16[128,256]{1,0:T(8,128)(2,1)S(1)} %fusion.1), channel_id=1, source_target_pairs={{128,0},{256,128},{384,256},{0,384},{129,1},{257,129},{385,257},{1... | collective-permute-start | bytes 196616 | tf_op jit(solution)/shard_map/ppermute | solution.py:141
